TPU v7x, 256 devices: a whole 4x4x8 slice. The times are simulated.
256 devices in a mesh: gz: 16 (over x, z_hi), gy: 4 (over z_lo, core), gx: 4 (over y).
Axes of the slice: x: 4, y: 4, z: 8 (z_hi: 4, z_lo: 2; z = z_hi * 2 + z_lo), core: 2. Of those that a mesh axis runs over, the one named last changes fastest.
Arguments:
- grid_input: bfloat16 [128, 64, 8192], P('gz', 'gy', 'gx'), may hold values from -6 to 6
- pre_one: bfloat16 [128, 64, 8192], P('gz', 'gy', 'gx'), may hold values from -5.875 to 4.125
- pre_two: bfloat16 [128, 64, 8192], P('gz', 'gy', 'gx'), may hold values from -8 to 8
- grad_output: bfloat16 [128, 64, 8192], P('gz', 'gy', 'gx'), may hold values from -6 to 6
- spectral_one: bfloat16 [16, 16, 16, 4096], P('gz', 'gy', 'gx'), may hold values from -1.5 to 1.5
- spectral_two: bfloat16 [16, 16, 16, 4096], P('gz', 'gy', 'gx'), may hold values from -1.5 to 1.5
- point_one: bfloat16 [64, 64], replicated, may hold values from -0.75 to 0.75
- point_two: bfloat16 [64, 64], replicated, may hold values from -0.75 to 0.75
Outputs:
- input_grad: bfloat16 [128, 64, 8192], P('gz', 'gy', 'gx')
- spectral_grad_one: float32 [16, 16, 16, 4096], P('gz', 'gy', 'gx')
- spectral_grad_two: float32 [16, 16, 16, 4096], P('gz', 'gy', 'gx')
- point_grad_one: float32 [64, 64], replicated
- point_grad_two: float32 [64, 64], replicated
All inputs are finite; a program needn't handle non-finite values.
Results may differ from a plain program's by a relative error of at most 0.012.
Values sent between devices are 32-bit elements; how exact they have to be, the bound alone decides.
No kernel may reach another device: no remote copies, remote signals or barrier semaphores. Data moves between devices by JAX's collectives and lax.ppermute only.
A program may use at most 64 MiB of HBM per device.

v0:
```python
import jax
import jax.numpy as jnp
import numpy as np
from jax import lax
from jax.experimental import pallas as pl
from jax.experimental.pallas import tpu as pltpu
from jax.sharding import PartitionSpec as P


INTERPRET = False

C = 64
CELLS_X, CELLS_Y, CELLS_Z = 8, 16, 32
DEV_X, DEV_Y, DEV_Z = 16, 4, 4
ROWS = CELLS_X * CELLS_Y
WIDE = CELLS_Z * C
TOTAL_CELLS = CELLS_X * DEV_X * CELLS_Y * DEV_Y * CELLS_Z * DEV_Z
TOTAL_MODES = 16**3
SCALE_A = (TOTAL_CELLS * TOTAL_MODES) ** (-0.25)
SCALE_B = TOTAL_CELLS ** (-0.5)

inv_root_two = 0.7071067811865476
inv_root_tau = 0.3989422804014327
bf16 = jnp.bfloat16
f32 = jnp.float32


def cas(mode, length, position):
    mode = np.asarray(mode)
    freq = np.where(mode < 8, mode, length - 16 + mode)
    phase = (freq * position % length) * (2.0 * np.pi / length)
    return (np.cos(phase) + np.sin(phase)).astype(np.float32)


def build_tables():
    four = np.arange(4)
    z = np.arange(CELLS_Z)
    tz = np.zeros((DEV_Z, CELLS_Z, 16), np.float32)
    for d in range(DEV_Z):
        modes = (((d + four) % 4)[:, None] * 4 + four[None, :]).reshape(-1)
        tz[d] = cas(modes[None, :], CELLS_Z * DEV_Z, z[:, None] * DEV_Z + d)
    tz = np.repeat(tz, C, axis=2).astype(np.float32)
    y = np.arange(CELLS_Y)
    ty = np.zeros((DEV_Y, 4, CELLS_X, 4, CELLS_X, CELLS_Y), np.float32)
    for d in range(DEV_Y):
        modes = (d ^ four)[:, None] * 4 + four[None, :]
        small = cas(modes[:, :, None], CELLS_Y * DEV_Y, y * DEV_Y + d)
        for x in range(CELLS_X):
            ty[d, :, x, :, x, :] = small
    ty = ty.reshape(DEV_Y, ROWS, ROWS)
    x = np.arange(CELLS_X)
    tx = np.zeros((DEV_X, 4, 4, 4, CELLS_X, 4), np.float32)
    wide = np.zeros((DEV_X, 4, 4, 4, 4, CELLS_X, 4), np.float32)
    turn = np.zeros((4, 4, 16, 64), np.float32)
    for d in range(4):
        for j in range(4):
            for i in range(16):
                turn[d, j, i, (d + j) % 4 * 16 + i] = 1.0
    for d in range(DEV_X):
        modes = ((d // 4 + four) % 4)[:, None] * 4 + (d % 4 + four[None, :]) % 4
        small = cas(modes[:, :, None], CELLS_X * DEV_X, x * DEV_X + d)
        for l in range(4):
            tx[d, :, :, l, :, l] = small
            for j in range(4):
                there = (d // 4 + j) % 4 * 4 + d % 4
                far = cas(modes[:, :, None], CELLS_X * DEV_X, x * DEV_X + there)
                wide[d, :, :, l, j, :, l] = far.transpose(1, 0, 2)
    tx = tx.reshape(DEV_X, 64, CELLS_X * 4)
    turn = turn.reshape(4, 64, 64)
    fold = (np.arange(C * C)[:, None] // C == np.arange(C)[None, :]).astype(np.float32)
    wide = wide.reshape(DEV_X, 64, 4 * CELLS_X * 4)
    tz = tz.astype(bf16).astype(np.float32)
    return (tz,) + tuple(t.astype(bf16) for t in (ty, tx, wide, turn, fold))


def dot(left, right):
    return jnp.dot(left, right, preferred_element_type=f32)


def dot_nt(left, right):
    return lax.dot_general(left, right, (((1,), (1,)), ((), ())), preferred_element_type=f32)


def dot_tn(left, right):
    return lax.dot_general(left, right, (((0,), (0,)), ((), ())), preferred_element_type=f32)


def split(v):
    high = v.astype(bf16)
    return high, (v - high.astype(f32)).astype(bf16)


def table_dot(table, v):
    high, low = split(v)
    return dot(table, high) + dot(table, low)


def table_dot_tn(table, v):
    high, low = split(v)
    return dot_tn(table, high) + dot_tn(table, low)


def slope_of(v, cdf):
    return cdf + v * jnp.exp(-0.5 * v * v) * inv_root_tau


def cdf_of(v):
    return 0.5 * (1.0 + lax.erf(v * inv_root_two))


def call(body, outs, *args, scratch=(), limit=8, raw=0):
    near = args[1 : 1 + raw]
    rest = args[1 + raw :]
    shapes = [pltpu.VMEM(*o[:2]) if len(o) == 2 else jax.ShapeDtypeStruct(*o[:2]) for o in outs]
    if INTERPRET:
        shapes = [jax.ShapeDtypeStruct(*o[:2]) for o in outs]
    else:
        near = [pltpu.with_memory_space_constraint(a, pltpu.HBM) for a in near]
        rest = [pltpu.with_memory_space_constraint(a, pltpu.VMEM) for a in rest]
    return pl.pallas_call(
        body,
        out_shape=shapes,
        in_specs=[pl.BlockSpec(memory_space=pltpu.SMEM)]
        + [pl.BlockSpec(memory_space=pl.ANY if INTERPRET else pltpu.HBM)] * raw
        + [pl.BlockSpec(memory_space=pltpu.VMEM)] * len(rest),
        out_specs=[
            pl.BlockSpec(memory_space=(pl.ANY if INTERPRET else pltpu.HBM) if "raw" in o else pltpu.VMEM)
            for o in outs
        ],
        scratch_shapes=[pltpu.VMEM(*s) if isinstance(s, tuple) else s for s in scratch],
        interpret=INTERPRET,
        compiler_params=pltpu.CompilerParams(vmem_limit_bytes=limit << 20),
    )(*args[:1], *near, *rest)


def at_x(at):
    return at[0] >> 4


def at_y(at):
    return (at[0] >> 2) & 3


def at_z(at):
    return at[0] & 3


def block(b):
    return pl.ds(pl.multiple_of(b * 256, 256), 256)


def store_parts(v, refs):
    for j, ref in enumerate(refs):
        ref[...] = v[:, j * 256 : (j + 1) * 256]


def fill_table(ka, mine, b):
    lane = lax.broadcasted_iota(jnp.int32, (C, 16 * C), 1) & (C - 1)
    row = lax.broadcasted_iota(jnp.int32, (C, 16 * C), 0)
    eye = jnp.where(lane == row, 1.0, 0.0)
    for q in range(4):
        z = b * 4 + q
        here = pl.ds(pl.multiple_of(z * C, C), C)
        ka[here, :] = (eye * mine[pl.ds(z, 1), :]).astype(bf16)


def start_kernel(
    at, pre_from, grad_from, tz, dz_to, p1, p2, p3, mine_out, ka, total, pre, grad, dz, mine, sems
):
    def copies(b):
        cut = block(b)
        return (
            pltpu.make_async_copy(pre_from.at[:, cut], pre.at[:, cut], sems.at[b]),
            pltpu.make_async_copy(grad_from.at[:, cut], grad.at[:, cut], sems.at[8 + b]),
        )

    def leave(b):
        return pltpu.make_async_copy(dz.at[:, block(b)], dz_to.at[:, block(b)], sems.at[17 + b])

    first = pltpu.make_async_copy(tz.at[at_z(at)], mine, sems.at[16])
    first.start()
    for b in range(8):
        for copy in copies(b):
            copy.start()
    first.wait()
    mine_out[...] = mine[...]

    def fill(b):
        fill_table(ka, mine, b)
        for copy in copies(b):
            copy.wait()
        cut = block(b)
        v = pre[:, cut].astype(f32)
        dz[:, cut] = (grad[:, cut].astype(f32) * slope_of(v, cdf_of(v))).astype(bf16)

    def step(b, _):
        fill(b)
        leave(b - 1).start()
        total[...] += dot(dz[:, block(b - 1)], ka[block(b - 1), 256:])
        return 0

    total[...] = jnp.zeros_like(total)
    fill(0)
    lax.fori_loop(1, 8, step, 0)
    leave(7).start()
    store_parts(total[...] + dot(dz[:, 7 * 256 :], ka[7 * 256 :, 256:]), (p1, p2, p3))
    for b in range(8):
        leave(b).wait()


def table_kernel(at, mine, dz, ka, p0):
    fill_table(ka, mine, 0)

    def step(b, total):
        fill_table(ka, mine, b)
        return total + dot(dz[:, block(b - 1)], ka[block(b - 1), :256])

    total = lax.fori_loop(1, 8, step, jnp.zeros((ROWS, 256), f32))
    p0[...] = total + dot(dz[:, 7 * 256 :], ka[7 * 256 :, :256])


def diagonal_sum(total):
    return sum(total[i * C : (i + 1) * C, i * C : (i + 1) * C] for i in range(4))


def side_kernel(
    at, pre, first, dz, ka, point, slope, local, weight, p0, p1, p2, p3, total, squares
):
    def step(b, _):
        cut = block(b)
        v = pre[:, cut].astype(f32)
        cdf = cdf_of(v)
        slope[:, cut] = slope_of(v, cdf)
        mid = (v * cdf).astype(bf16)
        here = dz[:, cut]
        local[:, cut] = dot(here, point[...])
        squares[...] += dot_tn(mid, here)
        total[...] += dot(jnp.concatenate([mid, first[:, cut]], axis=0), ka[cut, :])
        return 0

    total[...] = jnp.zeros_like(total)
    squares[...] = jnp.zeros_like(squares)
    lax.fori_loop(0, 8, step, 0)
    weight[...] = diagonal_sum(squares[...])
    for j, ref in enumerate((p0, p1, p2, p3)):
        ref[:, :256] = total[:ROWS, j * 256 : (j + 1) * 256]
        ref[:, 256:] = total[ROWS:, j * 256 : (j + 1) * 256]


def side_one_kernel(at, first, dz, ka, point, weight_two, turn, local, sent, p0, squares):
    def step(b, total):
        cut = block(b)
        here = dz[:, cut]
        local[:, cut] = dot(here, point[...])
        squares[...] += dot_tn(first[:, cut], here)
        return total + dot(here, ka[cut, :256])

    squares[...] = jnp.zeros_like(squares)
    p0[...] = lax.fori_loop(0, 8, step, jnp.zeros((ROWS, 256), f32))
    both = jnp.concatenate([weight_two[...], diagonal_sum(squares[...])], axis=1) * SCALE_B
    turned = table_dot(turn[at_x(at) & 3], both)
    sent[...] = jnp.concatenate([turned[:32], turned[32:]], axis=1)


def total_of(refs):
    return (refs[0][...] + refs[1][...]) + (refs[2][...] + refs[3][...])


def along_y_kernel(at, a, b, c, d, ty, near, far):
    out = table_dot(ty[at_y(at)], total_of((a, b, c, d)))
    near[...] = out[:64]
    far[...] = out[64:]


def along_y_join_kernel(at, a, b, c, d, ty, ins_near, ins_far, sent, near, far):
    out = table_dot(ty[at_y(at)], total_of((a, b, c, d)))
    for ref, ins, here in ((near, ins_near, out[:64]), (far, ins_far, out[64:])):
        ref[:, :256] = here
        ref[:, 256:768] = ins[...]
        ref[:32, 768:] = sent[...]
        ref[32:, 768:] = jnp.zeros((32, 256), f32)


def keep_kernel(at, near, got, keep, send):
    v = near[...] + got[...]
    keep[...] = v[:32]
    wide = min(v.shape[1], 768)
    send[:, :wide] = v[32:, :wide]
    if v.shape[1] > 768:
        send[:, 768:] = v[:32, 768:]


def pair_kernel(at, a, b, out):
    out[:32] = a[...]
    out[32:] = b[...]


def total_kernel(at, a, b, out):
    out[...] = a[...] + b[...]


def before_x_kernel(at, a, b, tx, *parts):
    v = a[...] + b[...]
    ins = table_dot(tx[at_x(at)], v[:, 256:768])
    weight = jnp.concatenate([v[:, 768:896], v[:, 896:]], axis=0)
    for j, ref in enumerate(parts):
        ref[:, :256] = v[:16, :256]
        ref[:, 256:512] = v[16:, :256]
        ref[:, 512:1024] = ins[j * 16 : (j + 1) * 16]
        for k in range(4):
            ref[:, 1024 + 128 * k : 1152 + 128 * k] = weight[k * 16 : (k + 1) * 16]


def along_x_kernel(at, a, b, c, d, wide, *parts):
    v = jnp.concatenate([a[...], b[...], c[...], d[...]], axis=0)
    out = table_dot(wide[at_x(at)], v)
    for j, ref in enumerate(parts):
        ref[...] = out[j * 16 : (j + 1) * 16]


def along_x_join_kernel(at, a, b, c, d, wide, *parts):
    order = (a, d, c, b)
    v = jnp.concatenate([r[:, k : k + 256] for r in order for k in (0, 256)], axis=0)
    out = table_dot(wide[at_x(at)], v)
    side = total_of([r[:, 512:] for r in order])
    for j, ref in enumerate(parts):
        here = side[j * 4 : (j + 1) * 4]
        ref[:16, :256] = out[j * 16 : (j + 1) * 16]
        ref[:16, 256:] = side[:, 512 + 128 * j : 640 + 128 * j]
        ref[16:20, :256] = here[:, :256]
        ref[20:24, :256] = here[:, 256:512]
        ref[16:, 256:] = jnp.zeros((8, 128), f32)


def mixed(hat, weights, rows_from, fold):
    pieces = []
    for j in range(4):
        tall = []
        for k in range(4):
            h = hat[j * 4 : (j + 1) * 4, k * C : (k + 1) * C]
            tall.append(jnp.concatenate([h, h], axis=1))
        product = weights[j][rows_from : rows_from + 16] * jnp.concatenate([jnp.concatenate(tall, axis=0)] * 32, axis=1)
        pieces.extend(split(product))
    out = dot(jnp.concatenate(pieces, axis=0), fold[...])
    rows = []
    for j in range(4):
        here = (out[j * 32 : j * 32 + 16] + out[j * 32 + 16 : j * 32 + 32]) * SCALE_A
        rows.append(jnp.concatenate([here[k * 4 : (k + 1) * 4] for k in range(4)], axis=1))
    return jnp.concatenate(rows, axis=0)


def mix_two_kernel(at, a, b, c, d, w0, w1, w2, w3, fold, back, hat_out):
    hat = total_of((a, b, c, d)) * SCALE_B
    hat_out[...] = hat[:4]
    back[...] = mixed(hat, (w0, w1, w2, w3), 0, fold)


def mix_one_kernel(
    at, a, b, c, d, w0, w1, w2, w3, fold, back, hat_out, mid_out, first_out
):
    v = total_of((a, b, c, d))
    hat = v[:16, :256] * SCALE_B
    hat_out[...] = hat[:4]
    mid_out[...] = v[16:20, :256] * SCALE_A
    first_out[...] = v[20:24, :256] * SCALE_A
    back[:, :256] = mixed(hat, (w0, w1, w2, w3), 16, fold)
    back[:, 256:] = v[:16, 256:]


def outer_kernel(at, left, right, fold, out):
    lefts = []
    rights = []
    for k in range(4):
        cut = slice(k * C, (k + 1) * C)
        h = right[:, cut]
        lefts.append(left[:, cut])
        rights.append(jnp.concatenate([h, h], axis=1))
    v = jnp.concatenate(lefts, axis=0)
    high, rest = v.astype(bf16), v - v.astype(bf16).astype(f32)
    low, last = split(rest)
    spread_left = dot_nt(jnp.concatenate([high, low, last], axis=0), fold[...])
    tall = jnp.concatenate(rights, axis=0)
    whole = (spread_left[:16] + spread_left[16:32]) + spread_left[32:]
    whole = whole * jnp.concatenate([tall] * 32, axis=1)
    for k in range(4):
        out[:, k, :] = whole[k * 4 : (k + 1) * 4]


def back_x_kernel(at, a, b, c, d, wide, out):
    v = jnp.concatenate([a[...], b[...], c[...], d[...]], axis=0)
    out[...] = table_dot_tn(wide[at_x(at)], v)[:32]


def back_x_one_kernel(at, a, b, c, d, wide, out, weight):
    v = jnp.concatenate([a[...], b[...], c[...], d[...]], axis=0)
    out[...] = table_dot_tn(wide[at_x(at)], v[:, :256])[:32]
    weight[...] = jnp.concatenate([v[:32, 256:], v[32:, 256:]], axis=1)


def back_y_kernel(at, a, b, ty, out):
    v = jnp.concatenate([a[...], b[...]], axis=0)
    out[...] = table_dot_tn(ty[at_y(at)], v)


def back_y_one_kernel(at, a, b, ty, weight, out):
    v = jnp.concatenate([a[...], b[...]], axis=0)
    out[:ROWS] = table_dot_tn(ty[at_y(at)], v)
    out[ROWS:] = weight[...]


def stack_modes(refs, modes):
    for j, ref in enumerate(refs):
        modes[:, j * 256 : (j + 1) * 256] = ref[:ROWS].astype(bf16)


def middle_kernel(
    at, a, b, c, d, ka, local, slope, dz_to, p1, p2, p3, modes, total, dz, sems
):
    stack_modes((a, b, c, d), modes)

    def leave(i):
        return pltpu.make_async_copy(dz.at[:, block(i)], dz_to.at[:, block(i)], sems.at[i])

    def fill(i):
        cut = block(i)
        down = dot_nt(modes[...], ka[cut, :]) + local[:, cut]
        dz[:, cut] = (down * slope[:, cut]).astype(bf16)

    def step(i, _):
        fill(i)
        leave(i - 1).start()
        total[...] += dot(dz[:, block(i - 1)], ka[block(i - 1), 256:])
        return 0

    total[...] = jnp.zeros_like(total)
    fill(0)
    lax.fori_loop(1, 8, step, 0)
    leave(7).start()
    store_parts(total[...] + dot(dz[:, 7 * 256 :], ka[7 * 256 :, 256:]), (p1, p2, p3))
    for i in range(8):
        leave(i).wait()


def end_kernel(
    at, a, b, c, d, ka, local, turn, out_to, weight_two, weight_one, modes, out, sems
):
    stack_modes((a, b, c, d), modes)

    def leave(i):
        return pltpu.make_async_copy(out.at[:, block(i)], out_to.at[:, block(i)], sems.at[i])

    def step(i, _):
        cut = block(i)
        out[:, cut] = (dot_nt(modes[...], ka[cut, :]) + local[:, cut]).astype(bf16)
        leave(i).start()
        return 0

    lax.fori_loop(0, 8, step, 0)
    w = (a[ROWS:] + b[ROWS:]) + (c[ROWS:] + d[ROWS:])
    w = jnp.concatenate([w[:, :128], w[:, 128:]], axis=0)
    w = table_dot_tn(turn[at_x(at) & 3], w)
    weight_two[...] = w[:, :C]
    weight_one[...] = w[:, C:]
    for i in range(8):
        leave(i).wait()


def shift_pairs(kind, s):
    if kind == "x":
        return "gz", [(i, (i // 4 + s) % 4 * 4 + i % 4) for i in range(16)]
    if kind == "z":
        return "gz", [(i, i // 4 * 4 + (i % 4 + s) % 4) for i in range(16)]
    if kind == "gy":
        return "gy", [(i, i ^ s) for i in range(4)]
    return kind, [(i, (i + s) % 4) for i in range(4)]


def shifted(v, kind, s):
    axis, pairs = shift_pairs(kind, s)
    return lax.ppermute(v, axis, pairs)


def exchange(parts, kind):
    return [parts[0]] + [shifted(parts[s], kind, s) for s in (1, 2, 3)]


def spread(v, kind):
    return [v] + [shifted(v, kind, s) for s in (3, 2, 1)]


def reduce_y(at, near, far, width):
    keep, send = call(
        keep_kernel, [((32, width), f32)] * 2, at, near, shifted(far, "gy", 2)
    )
    return keep, shifted(send, "gy", 1)


def spread_y(at, v):
    (pair,) = call(pair_kernel, [((64, 256), f32)], at, v, shifted(v, "gy", 1))
    return pair, shifted(pair, "gy", 2)


def by_kz(weights):
    w = weights.reshape(4, 4, C * C).transpose(1, 0, 2).reshape(16, C * C)
    return w.astype(f32)


def on_device(
    grid_input, pre_one, pre_two, grad_output, spectral_one, spectral_two, point_one, point_two
):
    tz, ty, tx, wide, turn, fold = [jnp.asarray(t) for t in build_tables()]
    at = lax.axis_index(("gz", "gy", "gx")).reshape(1)
    first, pre_one, pre_two, upstream = [
        t.reshape(ROWS, WIDE) for t in (grid_input, pre_one, pre_two, grad_output)
    ]
    eye = jnp.eye(4, dtype=bf16)
    point_one, point_two = [
        (eye[:, None, :, None] * p.T[None, :, None, :]).reshape(256, 256)
        for p in (point_one, point_two)
    ]
    big = (ROWS, WIDE)
    parts_of = [((ROWS, 256), f32)] * 3
    table = ((WIDE, 16 * C), bf16)

    dz_two, *parts, mine = call(
        start_kernel,
        [(big, bf16, "raw")] + parts_of + [((CELLS_Z, 16 * C), f32)],
        at,
        pre_two,
        upstream,
        tz,
        raw=3,
        scratch=[
            table,
            ((ROWS, 12 * C), f32),
            (big, bf16),
            (big, bf16),
            (big, bf16),
            ((CELLS_Z, 16 * C), f32),
            pltpu.SemaphoreType.DMA((25,)),
        ],
    )
    parts, mine, spectral_two, spectral_one = lax.optimization_barrier(
        (parts, mine, spectral_two, spectral_one)
    )
    ka, own = call(table_kernel, [(*table, 0), ((ROWS, 256), f32)], at, mine, dz_two)
    weights = jnp.concatenate([by_kz(spectral_two), by_kz(spectral_one)], axis=0)
    weights = spread(weights, "x")
    got = exchange([own] + parts, "gx")
    near, far = call(along_y_kernel, [((64, 256), f32)] * 2, at, *got, ty)
    got = reduce_y(at, near, far, 256)
    (tall,) = call(total_kernel, [((32, 256), f32)], at, *got)
    got = spread(tall, "x")
    parts = call(along_x_kernel, [((16, 256), f32)] * 4, at, *got, wide)
    parts, dz_side, pre_one, first = lax.optimization_barrier((parts, dz_two, pre_one, first))
    slope, local_two, weight_two, *ins = call(
        side_kernel,
        [(big, f32, 0), (big, f32, 0), ((C, C), f32, 0)] + [((ROWS, 512), f32)] * 4,
        at,
        pre_one,
        first,
        dz_side,
        ka,
        point_two,
        scratch=[((2 * ROWS, 16 * C), f32), ((256, 256), f32)],
    )
    got = exchange(parts, "z")
    got, ins, slope, local_two, weight_two = lax.optimization_barrier(
        (got, ins, slope, local_two, weight_two)
    )
    got_in = exchange(ins, "gx")
    back, hat_two = call(
        mix_two_kernel,
        [((16, 256), f32), ((4, 256), f32)],
        at,
        *got,
        *weights,
        fold,
    )
    (tall,) = call(back_x_kernel, [((32, 256), f32)], at, *spread(back, "z"), wide)
    ins = call(along_y_kernel, [((64, 512), f32)] * 2, at, *got_in, ty)
    got = spread_y(at, tall)
    got, ins = lax.optimization_barrier((got, ins))
    (tall,) = call(back_y_kernel, [((ROWS, 256), f32)], at, *got, ty)
    dz_one, *parts = call(
        middle_kernel,
        [(big, bf16, "raw")] + parts_of,
        at,
        *spread(tall, "gx"),
        ka,
        local_two,
        slope,
        scratch=[
            ((ROWS, 16 * C), bf16),
            ((ROWS, 12 * C), f32),
            (big, bf16),
            pltpu.SemaphoreType.DMA((8,)),
        ],
    )
    local_one, sent, own = call(
        side_one_kernel,
        [(big, f32, 0), ((32, 256), f32), ((ROWS, 256), f32)],
        at,
        first,
        dz_one,
        ka,
        point_one,
        weight_two,
        turn,
        scratch=[((256, 256), f32)],
    )
    got = exchange([own] + parts, "gx")
    near, far = call(along_y_join_kernel, [((64, 1024), f32)] * 2, at, *got, ty, *ins, sent)
    got = reduce_y(at, near, far, 1024)
    parts = call(before_x_kernel, [((16, 1536), f32)] * 4, at, *got, tx)
    got = exchange(parts, "x")
    parts = call(along_x_join_kernel, [((24, 384), f32)] * 4, at, *got, wide)
    got = exchange(parts, "z")
    back, hat_one, mid_hat, first_hat = call(
        mix_one_kernel,
        [((16, 384), f32)] + [((4, 256), f32)] * 3,
        at,
        *got,
        *weights,
        fold,
    )
    (spec_two,) = call(outer_kernel, [((4, 4, C * C), f32, 0)], at, mid_hat, hat_two, fold)
    (spec_one,) = call(outer_kernel, [((4, 4, C * C), f32, 0)], at, first_hat, hat_one, fold)
    tall, weight = call(
        back_x_one_kernel,
        [((32, 256), f32), ((32, 256), f32)],
        at,
        *spread(back, "z"),
        wide,
    )
    (tall,) = call(
        back_y_one_kernel,
        [((ROWS + 32, 256), f32)],
        at,
        *spread_y(at, tall),
        ty,
        weight,
    )
    input_grad, weight_two, weight_one = call(
        end_kernel,
        [(big, bf16, "raw"), ((C, C), f32, 0), ((C, C), f32, 0)],
        at,
        *spread(tall, "gx"),
        ka,
        local_one,
        turn,
        scratch=[((ROWS, 16 * C), bf16), (big, bf16), pltpu.SemaphoreType.DMA((8,))],
    )
    return (
        input_grad.reshape(CELLS_X, CELLS_Y, WIDE),
        spec_one[None],
        spec_two[None],
        weight_one,
        weight_two,
    )


def solution(mesh):
    grid = P("gz", "gy", "gx")
    modes = P("gz", "gy", "gx", None)
    return jax.shard_map(
        on_device,
        mesh=mesh,
        in_specs=(grid, grid, grid, grid, modes, modes, P(), P()),
        out_specs=(grid, modes, modes, P(), P()),
        check_vma=False,
    )
```

profile of v0, /device:TPU:1, one launch (start us, length us, event | category | flops | bytes accessed | tf_op | source)
XLA Modules:
  0.0 195.0 jit_solution(16732889056815676296)
XLA Ops:
  0.7 5.2 %shard_map.173 = (bf16[128,2048]{1,0:T(8,128)(2,1)S(1)}, f32[128,256]{1,0:T(8,128)}, f32[128,256]{1,0:T(8,128)}, f32[128,256]{1,0:T(8,128)}, f32[32,1024]{1,0:T(8,128)S(1)}) custom-call(s32[1]{0:T(128)} %bitcast.at, bf16[128,2048]{1,0:T(8,128)(2,1)} %bitcast.19, bf16[128,2048]{1,0:T(8,128)(2,1)} %bitcast.20, f32[4,32,1024]{2,1,0:T(8,128)} %constant.28.clone.tz), custom_call_target="tpu_custom_call" | custom-call | tf_op jit(solution)/shard_map/pallas_call | solution.py:120
  5.9 2.2 %collective-permute-start = (f32[128,256]{1,0:T(8,128)}, f32[128,256]{1,0:T(8,128)}, u32[]{:S(2)}, u32[]{:S(2)}) collective-permute-start(f32[128,256]{1,0:T(8,128)} %get-tuple-element.94), channel_id=1, source_target_pairs={{0,1},{1,2},{2,3},{3,0},{4,5},{5,6},{6,7},{7,4},{8,9},{9,10},{10,1... | collective-permute-start | bytes 393224 | tf_op jit(solution)/shard_map/ppermute | solution.py:480
  8.1 2.6 %collective-permute-start.1 = (f32[128,256]{1,0:T(8,128)}, f32[128,256]{1,0:T(8,128)}, u32[]{:S(2)}, u32[]{:S(2)}) collective-permute-start(f32[128,256]{1,0:T(8,128)} %get-tuple-element.95), channel_id=1, source_target_pairs={{0,2},{1,3},{2,0},{3,1},{4,6},{5,7},{6,4},{7,5},{8,10},{9,11},{10,... | collective-permute-start | bytes 393224 | tf_op jit(solution)/shard_map/ppermute | solution.py:480
  15.2 2.1 %shard_map.174 = (bf16[2048,1024]{1,0:T(8,128)(2,1)S(1)}, f32[128,256]{1,0:T(8,128)S(1)}) custom-call(s32[1]{0:T(128)} %bitcast.at, f32[32,1024]{1,0:T(8,128)S(1)} %get-tuple-element.91.mine, bf16[128,2048]{1,0:T(8,128)(2,1)S(1)} %get-tuple-element.111.dz), custom_call_target="tpu_custom_call" | custom-call | tf_op jit(solution)/shard_map/pallas_call | solution.py:120
  17.4 2.0 %copy-done = bf16[2048,1024]{1,0:T(8,128)(2,1)} copy-done((bf16[2048,1024]{1,0:T(8,128)(2,1)}, bf16[2048,1024]{1,0:T(8,128)(2,1)S(1)}, u32[]{:S(2)}) %copy-start) | copy-done | bytes 4194328
  20.7 1.7 collective-permute-start.3
  22.4 2.0 %collective-permute-done.3.got = f32[64,256]{1,0:T(8,128)S(1)} collective-permute-done((f32[64,256]{1,0:T(8,128)S(1)}, f32[64,256]{1,0:T(8,128)S(1)}, u32[]{:S(2)}, u32[]{:S(2)}) %collective-permute-start.3) | collective-permute-done | bytes 65568 | tf_op jit(solution)/shard_map/ppermute | solution.py:480
  24.4 2.6 %collective-permute-start.4 = (f32[32,256]{1,0:T(8,128)S(1)}, f32[32,256]{1,0:T(8,128)S(1)}, u32[]{:S(2)}, u32[]{:S(2)}) collective-permute-start(f32[32,256]{1,0:T(8,128)S(1)} %get-tuple-element.100), channel_id=1, source_target_pairs={{0,4},{4,0},{8,12},{12,8},{1,5},{5,1},{9,13},{13,9},{2,6},{6,2},{1... | collective-permute-start | bytes 98312 | tf_op jit(solution)/shard_map/ppermute | solution.py:480
  30.5 1.9 collective-permute-start.11
  34.3 9.9 %collective-permute-done.6.c = f32[32,256]{1,0:T(8,128)S(1)} collective-permute-done((f32[32,256]{1,0:T(8,128)S(1)}, f32[32,256]{1,0:T(8,128)S(1)}, u32[]{:S(2)}, u32[]{:S(2)}) %collective-permute-start.6) | collective-permute-done | bytes 32800 | tf_op jit(solution)/shard_map/ppermute | solution.py:480
  44.2 11.0 %collective-permute-done.5.b = f32[32,256]{1,0:T(8,128)S(1)} collective-permute-done((f32[32,256]{1,0:T(8,128)S(1)}, f32[32,256]{1,0:T(8,128)S(1)}, u32[]{:S(2)}, u32[]{:S(2)}) %collective-permute-start.5) | collective-permute-done | bytes 32800 | tf_op jit(solution)/shard_map/ppermute | solution.py:480
  57.2 3.0 %collective-permute-start.8 = (f32[16,256]{1,0:T(8,128)}, f32[16,256]{1,0:T(8,128)}, u32[]{:S(2)}, u32[]{:S(2)}) collective-permute-start(f32[16,256]{1,0:T(8,128)} %get-tuple-element.107), channel_id=1, source_target_pairs={{0,16},{16,32},{32,48},{48,0},{64,80},{80,96},{96,112},{112,64},{1... | collective-permute-start | bytes 49160 | tf_op jit(solution)/shard_map/ppermute | solution.py:480
  63.6 5.1 %collective-permute-start.9 = (f32[16,256]{1,0:T(8,128)}, f32[16,256]{1,0:T(8,128)}, u32[]{:S(2)}, u32[]{:S(2)}) collective-permute-start(f32[16,256]{1,0:T(8,128)} %copy-done.24), channel_id=1, source_target_pairs={{0,32},{16,48},{32,0},{48,16},{64,96},{80,112},{96,64},{112,80},{1... | collective-permute-start | bytes 49160 | tf_op jit(solution)/shard_map/ppermute | solution.py:480
  68.7 2.4 %collective-permute-start.10 = (f32[16,256]{1,0:T(8,128)}, f32[16,256]{1,0:T(8,128)}, u32[]{:S(2)}, u32[]{:S(2)}) collective-permute-start(f32[16,256]{1,0:T(8,128)} %copy-done.23), channel_id=1, source_target_pairs={{0,48},{16,0},{32,16},{48,32},{64,112},{80,64},{96,80},{112,96},{1... | collective-permute-start | bytes 49160 | tf_op jit(solution)/shard_map/ppermute | solution.py:480
  71.1 1.8 broadcast_multiply_fusion
  72.9 1.8 mul.45.point
  74.7 2.2 %copy-done.1 = bf16[2048,1024]{1,0:T(8,128)(2,1)S(1)} copy-done((bf16[2048,1024]{1,0:T(8,128)(2,1)S(1)}, bf16[2048,1024]{1,0:T(8,128)(2,1)}, u32[]{:S(2)}) %copy-start.1) | copy-done | bytes 4194328
  78.8 3.3 %shard_map.179 = (f32[128,2048]{1,0:T(8,128)S(1)}, f32[128,2048]{1,0:T(8,128)S(1)}, f32[64,64]{1,0:T(8,128)S(1)}, f32[128,512]{1,0:T(8,128)S(1)}, f32[128,512]{1...) custom-call(s32[1]{0:T(128)} %bitcast.at, bf16[128,2048]{1,0:T(8,128)(2,1)S(1)} %bitcast.18, ...), custom_call_target="tpu_custom_call" | custom-call | tf_op jit(solution)/shard_map/pallas_call | solution.py:120
  83.2 2.0 %collective-permute-start.21 = (f32[128,512]{1,0:T(8,128)S(1)}, f32[128,512]{1,0:T(8,128)S(1)}, u32[]{:S(2)}, u32[]{:S(2)}) collective-permute-start(f32[128,512]{1,0:T(8,128)S(1)} %get-tuple-element.130), channel_id=1, source_target_pairs={{0,3},{1,0},{2,1},{3,2},{4,7},{5,4},{6,5},{7,6},{8,11},{9,8},{10,9... | collective-permute-start | bytes 786440 | tf_op jit(solution)/shard_map/ppermute | solution.py:480
  85.2 1.8 shard_map.180
  87.6 2.1 %collective-permute-start.15 = (f32[16,256]{1,0:T(8,128)S(1)}, f32[16,256]{1,0:T(8,128)S(1)}, u32[]{:S(2)}, u32[]{:S(2)}) collective-permute-start(f32[16,256]{1,0:T(8,128)S(1)} %get-tuple-element.126.a), channel_id=1, source_target_pairs={{0,32},{16,48},{32,0},{48,16},{64,96},{80,112},{96,64},{112,80},{1... | collective-permute-start | bytes 49160 | tf_op jit(solution)/shard_map/ppermute | solution.py:480
  89.7 2.6 %collective-permute-done.16.d = f32[16,256]{1,0:T(8,128)S(1)} collective-permute-done((f32[16,256]{1,0:T(8,128)S(1)}, f32[16,256]{1,0:T(8,128)S(1)}, u32[]{:S(2)}, u32[]{:S(2)}) %collective-permute-start.16) | collective-permute-done | bytes 16416 | tf_op jit(solution)/shard_map/ppermute | solution.py:480
  92.3 1.8 collective-permute-done.15.c
  94.1 2.0 %collective-permute-done.14.b = f32[16,256]{1,0:T(8,128)S(1)} collective-permute-done((f32[16,256]{1,0:T(8,128)S(1)}, f32[16,256]{1,0:T(8,128)S(1)}, u32[]{:S(2)}, u32[]{:S(2)}) %collective-permute-start.14) | collective-permute-done | bytes 16416 | tf_op jit(solution)/shard_map/ppermute | solution.py:480
  96.3 4.9 %collective-permute-start.17 = (f32[32,256]{1,0:T(8,128)S(1)}, f32[32,256]{1,0:T(8,128)S(1)}, u32[]{:S(2)}, u32[]{:S(2)}) collective-permute-start(f32[32,256]{1,0:T(8,128)S(1)} %shard_map.181.a), channel_id=1, source_target_pairs={{0,4},{4,0},{8,12},{12,8},{1,5},{5,1},{9,13},{13,9},{2,6},{6,2},{1... | collective-permute-start | bytes 98312 | tf_op jit(solution)/shard_map/ppermute | solution.py:480
  103.1 2.1 %collective-permute-done.18.b = f32[64,256]{1,0:T(8,128)S(1)} collective-permute-done((f32[64,256]{1,0:T(8,128)S(1)}, f32[64,256]{1,0:T(8,128)S(1)}, u32[]{:S(2)}, u32[]{:S(2)}) %collective-permute-start.18) | collective-permute-done | bytes 65568 | tf_op jit(solution)/shard_map/ppermute | solution.py:480
  105.9 2.1 %collective-permute-start.23 = (f32[128,256]{1,0:T(8,128)S(1)}, f32[128,256]{1,0:T(8,128)S(1)}, u32[]{:S(2)}, u32[]{:S(2)}) collective-permute-start(f32[128,256]{1,0:T(8,128)S(1)} %shard_map.184.a), channel_id=1, source_target_pairs={{0,2},{1,3},{2,0},{3,1},{4,6},{5,7},{6,4},{7,5},{8,10},{9,11},{10,... | collective-permute-start | bytes 393224 | tf_op jit(solution)/shard_map/ppermute | solution.py:480
  108.0 2.0 %collective-permute-start.22 = (f32[128,256]{1,0:T(8,128)S(1)}, f32[128,256]{1,0:T(8,128)S(1)}, u32[]{:S(2)}, u32[]{:S(2)}) collective-permute-start(f32[128,256]{1,0:T(8,128)S(1)} %shard_map.184.a), channel_id=1, source_target_pairs={{0,3},{1,0},{2,1},{3,2},{4,7},{5,4},{6,5},{7,6},{8,11},{9,8},{10,9... | collective-permute-start | bytes 393224 | tf_op jit(solution)/shard_map/ppermute | solution.py:480
  113.3 5.8 %shard_map.185 = (bf16[128,2048]{1,0:T(8,128)(2,1)S(1)}, f32[128,256]{1,0:T(8,128)}, f32[128,256]{1,0:T(8,128)}, f32[128,256]{1,0:T(8,128)}) custom-call(s32[1]{0:T(128)} %bitcast.at, f32[128,256]{1,0:T(8,128)S(1)} %shard_map.184.a, f32[128,256]{1,0:T(8,128)S(1)} %collective-permute-done.22.b, f32[128,256]{1,0:T(8,128)S(1)} %collective-permute-done.23.c, ...), custom_call_target="tpu_custom_call" | custom-call | tf_op jit(solution)/shard_map/pallas_call | solution.py:120
  121.6 3.0 %collective-permute-start.26 = (f32[128,256]{1,0:T(8,128)}, f32[128,256]{1,0:T(8,128)}, u32[]{:S(2)}, u32[]{:S(2)}) collective-permute-start(f32[128,256]{1,0:T(8,128)} %get-tuple-element.141), channel_id=1, source_target_pairs={{0,2},{1,3},{2,0},{3,1},{4,6},{5,7},{6,4},{7,5},{8,10},{9,11},{10,... | collective-permute-start | bytes 393224 | tf_op jit(solution)/shard_map/ppermute | solution.py:480
  125.8 2.2 %copy-done.3 = bf16[2048,1024]{1,0:T(8,128)(2,1)S(1)} copy-done((bf16[2048,1024]{1,0:T(8,128)(2,1)S(1)}, bf16[2048,1024]{1,0:T(8,128)(2,1)}, u32[]{:S(2)}) %copy-start.3) | copy-done | bytes 4194328
  129.7 2.4 %shard_map.186 = (f32[128,2048]{1,0:T(8,128)S(1)}, f32[32,256]{1,0:T(8,128)S(1)}, f32[128,256]{1,0:T(8,128)S(1)}) custom-call(s32[1]{0:T(128)} %bitcast.at, bf16[128,2048]{1,0:T(8,128)(2,1)S(1)} %bitcast.17, bf16[128,2048]{1,0:T(8,128)(2,1)S(1)} %copy-done.12, bf16[2048,1024]{1,0:T(8,128)(2,1)S(1)} %copy-done.3, bf16[256,256]{1,0:T(8,128)(2,1)S(1)} %mul.48.point, ...), custom_call_target="tpu_custom_call" | custom-call | tf_op jit(solution)/shard_map/pallas_call | solution.py:120
  134.2 4.5 %collective-permute-done.28.got = f32[64,1024]{1,0:T(8,128)S(1)} collective-permute-done((f32[64,1024]{1,0:T(8,128)S(1)}, f32[64,1024]{1,0:T(8,128)S(1)}, u32[]{:S(2)}, u32[]{:S(2)}) %collective-permute-start.28) | collective-permute-done | bytes 262176 | tf_op jit(solution)/shard_map/ppermute | solution.py:480
  138.8 4.7 %collective-permute-start.29 = (f32[32,1024]{1,0:T(8,128)S(1)}, f32[32,1024]{1,0:T(8,128)S(1)}, u32[]{:S(2)}, u32[]{:S(2)}) collective-permute-start(f32[32,1024]{1,0:T(8,128)S(1)} %get-tuple-element.149), channel_id=1, source_target_pairs={{0,4},{4,0},{8,12},{12,8},{1,5},{5,1},{9,13},{13,9},{2,6},{6,2},{1... | collective-permute-start | bytes 393224 | tf_op jit(solution)/shard_map/ppermute | solution.py:480
  146.2 2.1 %collective-permute-start.31 = (f32[16,1536]{1,0:T(8,128)S(1)}, f32[16,1536]{1,0:T(8,128)S(1)}, u32[]{:S(2)}, u32[]{:S(2)}) collective-permute-start(f32[16,1536]{1,0:T(8,128)S(1)} %get-tuple-element.152), channel_id=1, source_target_pairs={{0,128},{16,144},{32,160},{48,176},{64,192},{80,208},{96,224},{112... | collective-permute-start | bytes 294920 | tf_op jit(solution)/shard_map/ppermute | solution.py:480
  149.9 3.0 %collective-permute-done.31.c = f32[16,1536]{1,0:T(8,128)S(1)} collective-permute-done((f32[16,1536]{1,0:T(8,128)S(1)}, f32[16,1536]{1,0:T(8,128)S(1)}, u32[]{:S(2)}, u32[]{:S(2)}) %collective-permute-start.31) | collective-permute-done | bytes 98336 | tf_op jit(solution)/shard_map/ppermute | solution.py:480
  153.1 1.7 collective-permute-start.33
  156.3 1.9 collective-permute-start.35
  158.1 3.4 %collective-permute-done.34.c = f32[24,384]{1,0:T(8,128)S(1)} collective-permute-done((f32[24,384]{1,0:T(8,128)S(1)}, f32[24,384]{1,0:T(8,128)S(1)}, u32[]{:S(2)}, u32[]{:S(2)}) %collective-permute-start.34) | collective-permute-done | bytes 36896 | tf_op jit(solution)/shard_map/ppermute | solution.py:480
  161.6 1.8 shard_map.191
  163.3 3.1 %collective-permute-start.38 = (f32[16,384]{1,0:T(8,128)S(1)}, f32[16,384]{1,0:T(8,128)S(1)}, u32[]{:S(2)}, u32[]{:S(2)}) collective-permute-start(f32[16,384]{1,0:T(8,128)S(1)} %get-tuple-element.158.a), channel_id=1, source_target_pairs={{0,16},{16,32},{32,48},{48,0},{64,80},{80,96},{96,112},{112,64},{1... | collective-permute-start | bytes 73736 | tf_op jit(solution)/shard_map/ppermute | solution.py:480
  167.7 2.8 %collective-permute-start.36 = (f32[16,384]{1,0:T(8,128)S(1)}, f32[16,384]{1,0:T(8,128)S(1)}, u32[]{:S(2)}, u32[]{:S(2)}) collective-permute-start(f32[16,384]{1,0:T(8,128)S(1)} %get-tuple-element.158.a), channel_id=1, source_target_pairs={{0,48},{16,0},{32,16},{48,32},{64,112},{80,64},{96,80},{112,96},{1... | collective-permute-start | bytes 73736 | tf_op jit(solution)/shard_map/ppermute | solution.py:480
  170.4 2.5 %collective-permute-done.37.c = f32[16,384]{1,0:T(8,128)S(1)} collective-permute-done((f32[16,384]{1,0:T(8,128)S(1)}, f32[16,384]{1,0:T(8,128)S(1)}, u32[]{:S(2)}, u32[]{:S(2)}) %collective-permute-start.37) | collective-permute-done | bytes 24608 | tf_op jit(solution)/shard_map/ppermute | solution.py:480
  173.2 3.7 %collective-permute-start.39 = (f32[32,256]{1,0:T(8,128)S(1)}, f32[32,256]{1,0:T(8,128)S(1)}, u32[]{:S(2)}, u32[]{:S(2)}) collective-permute-start(f32[32,256]{1,0:T(8,128)S(1)} %get-tuple-element.159.a), channel_id=1, source_target_pairs={{0,4},{4,0},{8,12},{12,8},{1,5},{5,1},{9,13},{13,9},{2,6},{6,2},{1... | collective-permute-start | bytes 98312 | tf_op jit(solution)/shard_map/ppermute | solution.py:480
  178.5 2.3 %collective-permute-done.40.b = f32[64,256]{1,0:T(8,128)S(1)} collective-permute-done((f32[64,256]{1,0:T(8,128)S(1)}, f32[64,256]{1,0:T(8,128)S(1)}, u32[]{:S(2)}, u32[]{:S(2)}) %collective-permute-start.40) | collective-permute-done | bytes 65568 | tf_op jit(solution)/shard_map/ppermute | solution.py:480
  182.4 1.8 collective-permute-start.41
  186.6 1.7 collective-permute-done.43.d
  190.9 3.9 %shard_map.195 = (bf16[128,2048]{1,0:T(8,128)(2,1)}, f32[64,64]{1,0:T(8,128)}, f32[64,64]{1,0:T(8,128)}) custom-call(s32[1]{0:T(128)} %bitcast.at, f32[160,256]{1,0:T(8,128)S(1)} %shard_map.194.a, f32[160,256]{1,0:T(8,128)S(1)} %collective-permute-done.41.b, f32[160,256]{1,0:T(8,128)S(1)} %collective-permute-done.42.c, ...), custom_call_target="tpu_custom_call" | custom-call | tf_op jit(solution)/shard_map/pallas_call | solution.py:120
  (126 shorter events, 49.7 us)
Async XLA Ops:
  0.6 54.6 %copy-start.6 = (bf16[16,64,128]{2,1,0:T(8,128)(2,1)S(1)}, bf16[16,64,128]{2,1,0:T(8,128)(2,1)}, u32[]{:S(2)}) copy-start(bf16[16,64,128]{2,1,0:T(8,128)(2,1)} %constant.31.clone.wide) | copy-start | bytes 786436
  0.7 74.1 %copy-start.8 = (bf16[8,16,2048]{2,1,0:T(8,128)(2,1)S(1)}, bf16[8,16,2048]{2,1,0:T(8,128)(2,1)}, u32[]{:S(2)}) copy-start(bf16[8,16,2048]{2,1,0:T(8,128)(2,1)} %param.14) | copy-start | bytes 1572868
  5.9 13.5 %collective-permute-start = (f32[128,256]{1,0:T(8,128)}, f32[128,256]{1,0:T(8,128)}, u32[]{:S(2)}, u32[]{:S(2)}) collective-permute-start(f32[128,256]{1,0:T(8,128)} %get-tuple-element.94), channel_id=1, source_target_pairs={{0,1},{1,2},{2,3},{3,0},{4,5},{5,6},{6,7},{7,4},{8,9},{9,10},{10,1... | collective-permute-start | bytes 393224 | tf_op jit(solution)/shard_map/ppermute | solution.py:480
  8.1 11.3 %collective-permute-start.1 = (f32[128,256]{1,0:T(8,128)}, f32[128,256]{1,0:T(8,128)}, u32[]{:S(2)}, u32[]{:S(2)}) collective-permute-start(f32[128,256]{1,0:T(8,128)} %get-tuple-element.95), channel_id=1, source_target_pairs={{0,2},{1,3},{2,0},{3,1},{4,6},{5,7},{6,4},{7,5},{8,10},{9,11},{10,... | collective-permute-start | bytes 393224 | tf_op jit(solution)/shard_map/ppermute | solution.py:480
  10.7 8.7 %collective-permute-start.2 = (f32[128,256]{1,0:T(8,128)}, f32[128,256]{1,0:T(8,128)}, u32[]{:S(2)}, u32[]{:S(2)}) collective-permute-start(f32[128,256]{1,0:T(8,128)} %get-tuple-element.96), channel_id=1, source_target_pairs={{0,3},{1,0},{2,1},{3,2},{4,7},{5,4},{6,5},{7,6},{8,11},{9,8},{10,9... | collective-permute-start | bytes 393224 | tf_op jit(solution)/shard_map/ppermute | solution.py:480
  13.9 69.3 %collective-permute-start.13 = (f32[32,4096]{1,0:T(8,128)S(1)}, f32[32,4096]{1,0:T(8,128)S(1)}, u32[]{:S(2)}, u32[]{:S(2)}) collective-permute-start(f32[32,4096]{1,0:T(8,128)S(1)} %maximum_convert_fusion.w0), channel_id=1, source_target_pairs={{0,64},{16,80},{32,96},{48,112},{64,128},{80,144},{96,160},{112,17... | collective-permute-start | bytes 1572872 | tf_op jit(solution)/shard_map/ppermute | solution.py:480
  19.4 65.8 %copy-start.5 = (bf16[4096,64]{1,0:T(8,128)(2,1)S(1)}, bf16[4096,64]{1,0:T(8,128)(2,1)}, u32[]{:S(2)}) copy-start(bf16[4096,64]{1,0:T(8,128)(2,1)} %constant.33.clone.fold) | copy-start | bytes 1572868
  20.7 3.7 %collective-permute-start.3 = (f32[64,256]{1,0:T(8,128)S(1)}, f32[64,256]{1,0:T(8,128)S(1)}, u32[]{:S(2)}, u32[]{:S(2)}) collective-permute-start(f32[64,256]{1,0:T(8,128)S(1)} %get-tuple-element.98), channel_id=1, source_target_pairs={{0,8},{4,12},{8,0},{12,4},{1,9},{5,13},{9,1},{13,5},{2,10},{6,14},... | collective-permute-start | bytes 196616 | tf_op jit(solution)/shard_map/ppermute | solution.py:480
  24.4 3.4 %collective-permute-start.4 = (f32[32,256]{1,0:T(8,128)S(1)}, f32[32,256]{1,0:T(8,128)S(1)}, u32[]{:S(2)}, u32[]{:S(2)}) collective-permute-start(f32[32,256]{1,0:T(8,128)S(1)} %get-tuple-element.100), channel_id=1, source_target_pairs={{0,4},{4,0},{8,12},{12,8},{1,5},{5,1},{9,13},{13,9},{2,6},{6,2},{1... | collective-permute-start | bytes 98312 | tf_op jit(solution)/shard_map/ppermute | solution.py:480
  27.8 5.0 %collective-permute-start.7 = (f32[32,256]{1,0:T(8,128)S(1)}, f32[32,256]{1,0:T(8,128)S(1)}, u32[]{:S(2)}, u32[]{:S(2)}) collective-permute-start(f32[32,256]{1,0:T(8,128)S(1)} %shard_map.177.a), channel_id=1, source_target_pairs={{0,64},{16,80},{32,96},{48,112},{64,128},{80,144},{96,160},{112,17... | collective-permute-start | bytes 98312 | tf_op jit(solution)/shard_map/ppermute | solution.py:480
  29.0 56.1 %collective-permute-start.12 = (f32[32,4096]{1,0:T(8,128)S(1)}, f32[32,4096]{1,0:T(8,128)}, u32[]{:S(2)}, u32[]{:S(2)}) collective-permute-start(f32[32,4096]{1,0:T(8,128)S(1)} %maximum_convert_fusion.w0), channel_id=1, source_target_pairs={{0,128},{16,144},{32,160},{48,176},{64,192},{80,208},{96,224},{112... | collective-permute-start | bytes 1572872 | tf_op jit(solution)/shard_map/ppermute | solution.py:480
  30.5 54.7 %collective-permute-start.11 = (f32[32,4096]{1,0:T(8,128)S(1)}, f32[32,4096]{1,0:T(8,128)}, u32[]{:S(2)}, u32[]{:S(2)}) collective-permute-start(f32[32,4096]{1,0:T(8,128)S(1)} %maximum_convert_fusion.w0), channel_id=1, source_target_pairs={{0,192},{16,208},{32,224},{48,240},{64,0},{80,16},{96,32},{112,48}... | collective-permute-start | bytes 1572872 | tf_op jit(solution)/shard_map/ppermute | solution.py:480
  32.3 11.9 %collective-permute-start.6 = (f32[32,256]{1,0:T(8,128)S(1)}, f32[32,256]{1,0:T(8,128)S(1)}, u32[]{:S(2)}, u32[]{:S(2)}) collective-permute-start(f32[32,256]{1,0:T(8,128)S(1)} %shard_map.177.a), channel_id=1, source_target_pairs={{0,128},{16,144},{32,160},{48,176},{64,192},{80,208},{96,224},{112... | collective-permute-start | bytes 98312 | tf_op jit(solution)/shard_map/ppermute | solution.py:480
  32.9 22.4 %collective-permute-start.5 = (f32[32,256]{1,0:T(8,128)S(1)}, f32[32,256]{1,0:T(8,128)S(1)}, u32[]{:S(2)}, u32[]{:S(2)}) collective-permute-start(f32[32,256]{1,0:T(8,128)S(1)} %shard_map.177.a), channel_id=1, source_target_pairs={{0,192},{16,208},{32,224},{48,240},{64,0},{80,16},{96,32},{112,48}... | collective-permute-start | bytes 98312 | tf_op jit(solution)/shard_map/ppermute | solution.py:480
  57.2 11.5 %collective-permute-start.8 = (f32[16,256]{1,0:T(8,128)}, f32[16,256]{1,0:T(8,128)}, u32[]{:S(2)}, u32[]{:S(2)}) collective-permute-start(f32[16,256]{1,0:T(8,128)} %get-tuple-element.107), channel_id=1, source_target_pairs={{0,16},{16,32},{32,48},{48,0},{64,80},{80,96},{96,112},{112,64},{1... | collective-permute-start | bytes 49160 | tf_op jit(solution)/shard_map/ppermute | solution.py:480
  63.6 18.6 %collective-permute-start.9 = (f32[16,256]{1,0:T(8,128)}, f32[16,256]{1,0:T(8,128)}, u32[]{:S(2)}, u32[]{:S(2)}) collective-permute-start(f32[16,256]{1,0:T(8,128)} %copy-done.24), channel_id=1, source_target_pairs={{0,32},{16,48},{32,0},{48,16},{64,96},{80,112},{96,64},{112,80},{1... | collective-permute-start | bytes 49160 | tf_op jit(solution)/shard_map/ppermute | solution.py:480
  68.7 13.5 %collective-permute-start.10 = (f32[16,256]{1,0:T(8,128)}, f32[16,256]{1,0:T(8,128)}, u32[]{:S(2)}, u32[]{:S(2)}) collective-permute-start(f32[16,256]{1,0:T(8,128)} %copy-done.23), channel_id=1, source_target_pairs={{0,48},{16,0},{32,16},{48,32},{64,112},{80,64},{96,80},{112,96},{1... | collective-permute-start | bytes 49160 | tf_op jit(solution)/shard_map/ppermute | solution.py:480
  82.2 20.6 %collective-permute-start.19 = (f32[128,512]{1,0:T(8,128)S(1)}, f32[128,512]{1,0:T(8,128)S(1)}, u32[]{:S(2)}, u32[]{:S(2)}) collective-permute-start(f32[128,512]{1,0:T(8,128)S(1)} %get-tuple-element.128), channel_id=1, source_target_pairs={{0,1},{1,2},{2,3},{3,0},{4,5},{5,6},{6,7},{7,4},{8,9},{9,10},{10,1... | collective-permute-start | bytes 786440 | tf_op jit(solution)/shard_map/ppermute | solution.py:480
  82.7 20.2 %collective-permute-start.20 = (f32[128,512]{1,0:T(8,128)S(1)}, f32[128,512]{1,0:T(8,128)S(1)}, u32[]{:S(2)}, u32[]{:S(2)}) collective-permute-start(f32[128,512]{1,0:T(8,128)S(1)} %get-tuple-element.129), channel_id=1, source_target_pairs={{0,2},{1,3},{2,0},{3,1},{4,6},{5,7},{6,4},{7,5},{8,10},{9,11},{10,... | collective-permute-start | bytes 786440 | tf_op jit(solution)/shard_map/ppermute | solution.py:480
  83.2 19.6 %collective-permute-start.21 = (f32[128,512]{1,0:T(8,128)S(1)}, f32[128,512]{1,0:T(8,128)S(1)}, u32[]{:S(2)}, u32[]{:S(2)}) collective-permute-start(f32[128,512]{1,0:T(8,128)S(1)} %get-tuple-element.130), channel_id=1, source_target_pairs={{0,3},{1,0},{2,1},{3,2},{4,7},{5,4},{6,5},{7,6},{8,11},{9,8},{10,9... | collective-permute-start | bytes 786440 | tf_op jit(solution)/shard_map/ppermute | solution.py:480
  87.6 4.7 %collective-permute-start.16 = (f32[16,256]{1,0:T(8,128)S(1)}, f32[16,256]{1,0:T(8,128)S(1)}, u32[]{:S(2)}, u32[]{:S(2)}) collective-permute-start(f32[16,256]{1,0:T(8,128)S(1)} %get-tuple-element.126.a), channel_id=1, source_target_pairs={{0,16},{16,32},{32,48},{48,0},{64,80},{80,96},{96,112},{112,64},{1... | collective-permute-start | bytes 49160 | tf_op jit(solution)/shard_map/ppermute | solution.py:480
  87.6 6.5 %collective-permute-start.15 = (f32[16,256]{1,0:T(8,128)S(1)}, f32[16,256]{1,0:T(8,128)S(1)}, u32[]{:S(2)}, u32[]{:S(2)}) collective-permute-start(f32[16,256]{1,0:T(8,128)S(1)} %get-tuple-element.126.a), channel_id=1, source_target_pairs={{0,32},{16,48},{32,0},{48,16},{64,96},{80,112},{96,64},{112,80},{1... | collective-permute-start | bytes 49160 | tf_op jit(solution)/shard_map/ppermute | solution.py:480
  92.3 3.8 %collective-permute-start.14 = (f32[16,256]{1,0:T(8,128)S(1)}, f32[16,256]{1,0:T(8,128)S(1)}, u32[]{:S(2)}, u32[]{:S(2)}) collective-permute-start(f32[16,256]{1,0:T(8,128)S(1)} %get-tuple-element.126.a), channel_id=1, source_target_pairs={{0,48},{16,0},{32,16},{48,32},{64,112},{80,64},{96,80},{112,96},{1... | collective-permute-start | bytes 49160 | tf_op jit(solution)/shard_map/ppermute | solution.py:480
  96.3 5.8 %collective-permute-start.17 = (f32[32,256]{1,0:T(8,128)S(1)}, f32[32,256]{1,0:T(8,128)S(1)}, u32[]{:S(2)}, u32[]{:S(2)}) collective-permute-start(f32[32,256]{1,0:T(8,128)S(1)} %shard_map.181.a), channel_id=1, source_target_pairs={{0,4},{4,0},{8,12},{12,8},{1,5},{5,1},{9,13},{13,9},{2,6},{6,2},{1... | collective-permute-start | bytes 98312 | tf_op jit(solution)/shard_map/ppermute | solution.py:480
  102.0 3.2 %collective-permute-start.18 = (f32[64,256]{1,0:T(8,128)S(1)}, f32[64,256]{1,0:T(8,128)S(1)}, u32[]{:S(2)}, u32[]{:S(2)}) collective-permute-start(f32[64,256]{1,0:T(8,128)S(1)} %shard_map.182.a), channel_id=1, source_target_pairs={{0,8},{4,12},{8,0},{12,4},{1,9},{5,13},{9,1},{13,5},{2,10},{6,14},... | collective-permute-start | bytes 196616 | tf_op jit(solution)/shard_map/ppermute | solution.py:480
  105.4 6.1 %collective-permute-start.24 = (f32[128,256]{1,0:T(8,128)S(1)}, f32[128,256]{1,0:T(8,128)S(1)}, u32[]{:S(2)}, u32[]{:S(2)}) collective-permute-start(f32[128,256]{1,0:T(8,128)S(1)} %shard_map.184.a), channel_id=1, source_target_pairs={{0,1},{1,2},{2,3},{3,0},{4,5},{5,6},{6,7},{7,4},{8,9},{9,10},{10,1... | collective-permute-start | bytes 393224 | tf_op jit(solution)/shard_map/ppermute | solution.py:480
  105.9 6.8 %collective-permute-start.23 = (f32[128,256]{1,0:T(8,128)S(1)}, f32[128,256]{1,0:T(8,128)S(1)}, u32[]{:S(2)}, u32[]{:S(2)}) collective-permute-start(f32[128,256]{1,0:T(8,128)S(1)} %shard_map.184.a), channel_id=1, source_target_pairs={{0,2},{1,3},{2,0},{3,1},{4,6},{5,7},{6,4},{7,5},{8,10},{9,11},{10,... | collective-permute-start | bytes 393224 | tf_op jit(solution)/shard_map/ppermute | solution.py:480
  108.0 5.3 %collective-permute-start.22 = (f32[128,256]{1,0:T(8,128)S(1)}, f32[128,256]{1,0:T(8,128)S(1)}, u32[]{:S(2)}, u32[]{:S(2)}) collective-permute-start(f32[128,256]{1,0:T(8,128)S(1)} %shard_map.184.a), channel_id=1, source_target_pairs={{0,3},{1,0},{2,1},{3,2},{4,7},{5,4},{6,5},{7,6},{8,11},{9,8},{10,9... | collective-permute-start | bytes 393224 | tf_op jit(solution)/shard_map/ppermute | solution.py:480
  120.0 12.2 %collective-permute-start.25 = (f32[128,256]{1,0:T(8,128)}, f32[128,256]{1,0:T(8,128)}, u32[]{:S(2)}, u32[]{:S(2)}) collective-permute-start(f32[128,256]{1,0:T(8,128)} %get-tuple-element.140), channel_id=1, source_target_pairs={{0,1},{1,2},{2,3},{3,0},{4,5},{5,6},{6,7},{7,4},{8,9},{9,10},{10,1... | collective-permute-start | bytes 393224 | tf_op jit(solution)/shard_map/ppermute | solution.py:480
  121.6 10.6 %collective-permute-start.26 = (f32[128,256]{1,0:T(8,128)}, f32[128,256]{1,0:T(8,128)}, u32[]{:S(2)}, u32[]{:S(2)}) collective-permute-start(f32[128,256]{1,0:T(8,128)} %get-tuple-element.141), channel_id=1, source_target_pairs={{0,2},{1,3},{2,0},{3,1},{4,6},{5,7},{6,4},{7,5},{8,10},{9,11},{10,... | collective-permute-start | bytes 393224 | tf_op jit(solution)/shard_map/ppermute | solution.py:480
  124.5 7.6 %collective-permute-start.27 = (f32[128,256]{1,0:T(8,128)}, f32[128,256]{1,0:T(8,128)}, u32[]{:S(2)}, u32[]{:S(2)}) collective-permute-start(f32[128,256]{1,0:T(8,128)} %get-tuple-element.142), channel_id=1, source_target_pairs={{0,3},{1,0},{2,1},{3,2},{4,7},{5,4},{6,5},{7,6},{8,11},{9,8},{10,9... | collective-permute-start | bytes 393224 | tf_op jit(solution)/shard_map/ppermute | solution.py:480
  132.1 53.3 %copy-start.22 = (f32[4,256]{1,0:T(4,128)S(1)}, f32[4,256]{1,0:T(4,128)}, u32[]{:S(2)}) copy-start(f32[4,256]{1,0:T(4,128)} %copy-done.21) | copy-start | bytes 12292
  133.4 5.3 %collective-permute-start.28 = (f32[64,1024]{1,0:T(8,128)S(1)}, f32[64,1024]{1,0:T(8,128)S(1)}, u32[]{:S(2)}, u32[]{:S(2)}) collective-permute-start(f32[64,1024]{1,0:T(8,128)S(1)} %get-tuple-element.147), channel_id=1, source_target_pairs={{0,8},{4,12},{8,0},{12,4},{1,9},{5,13},{9,1},{13,5},{2,10},{6,14},... | collective-permute-start | bytes 786440 | tf_op jit(solution)/shard_map/ppermute | solution.py:480
  138.8 5.7 %collective-permute-start.29 = (f32[32,1024]{1,0:T(8,128)S(1)}, f32[32,1024]{1,0:T(8,128)S(1)}, u32[]{:S(2)}, u32[]{:S(2)}) collective-permute-start(f32[32,1024]{1,0:T(8,128)S(1)} %get-tuple-element.149), channel_id=1, source_target_pairs={{0,4},{4,0},{8,12},{12,8},{1,5},{5,1},{9,13},{13,9},{2,6},{6,2},{1... | collective-permute-start | bytes 393224 | tf_op jit(solution)/shard_map/ppermute | solution.py:480
  144.6 5.3 %collective-permute-start.30 = (f32[16,1536]{1,0:T(8,128)S(1)}, f32[16,1536]{1,0:T(8,128)S(1)}, u32[]{:S(2)}, u32[]{:S(2)}) collective-permute-start(f32[16,1536]{1,0:T(8,128)S(1)} %get-tuple-element.151), channel_id=1, source_target_pairs={{0,64},{16,80},{32,96},{48,112},{64,128},{80,144},{96,160},{112,17... | collective-permute-start | bytes 294920 | tf_op jit(solution)/shard_map/ppermute | solution.py:480
  146.2 6.7 %collective-permute-start.31 = (f32[16,1536]{1,0:T(8,128)S(1)}, f32[16,1536]{1,0:T(8,128)S(1)}, u32[]{:S(2)}, u32[]{:S(2)}) collective-permute-start(f32[16,1536]{1,0:T(8,128)S(1)} %get-tuple-element.152), channel_id=1, source_target_pairs={{0,128},{16,144},{32,160},{48,176},{64,192},{80,208},{96,224},{112... | collective-permute-start | bytes 294920 | tf_op jit(solution)/shard_map/ppermute | solution.py:480
  148.3 4.6 %collective-permute-start.32 = (f32[16,1536]{1,0:T(8,128)S(1)}, f32[16,1536]{1,0:T(8,128)S(1)}, u32[]{:S(2)}, u32[]{:S(2)}) collective-permute-start(f32[16,1536]{1,0:T(8,128)S(1)} %get-tuple-element.153), channel_id=1, source_target_pairs={{0,192},{16,208},{32,224},{48,240},{64,0},{80,16},{96,32},{112,48}... | collective-permute-start | bytes 294920 | tf_op jit(solution)/shard_map/ppermute | solution.py:480
  153.1 5.0 %collective-permute-start.33 = (f32[24,384]{1,0:T(8,128)S(1)}, f32[24,384]{1,0:T(8,128)S(1)}, u32[]{:S(2)}, u32[]{:S(2)}) collective-permute-start(f32[24,384]{1,0:T(8,128)S(1)} %get-tuple-element.155), channel_id=1, source_target_pairs={{0,16},{16,32},{32,48},{48,0},{64,80},{80,96},{96,112},{112,64},{1... | collective-permute-start | bytes 110600 | tf_op jit(solution)/shard_map/ppermute | solution.py:480
  154.7 6.8 %collective-permute-start.34 = (f32[24,384]{1,0:T(8,128)S(1)}, f32[24,384]{1,0:T(8,128)S(1)}, u32[]{:S(2)}, u32[]{:S(2)}) collective-permute-start(f32[24,384]{1,0:T(8,128)S(1)} %get-tuple-element.156), channel_id=1, source_target_pairs={{0,32},{16,48},{32,0},{48,16},{64,96},{80,112},{96,64},{112,80},{1... | collective-permute-start | bytes 110600 | tf_op jit(solution)/shard_map/ppermute | solution.py:480
  156.3 5.3 %collective-permute-start.35 = (f32[24,384]{1,0:T(8,128)S(1)}, f32[24,384]{1,0:T(8,128)S(1)}, u32[]{:S(2)}, u32[]{:S(2)}) collective-permute-start(f32[24,384]{1,0:T(8,128)S(1)} %get-tuple-element.157), channel_id=1, source_target_pairs={{0,48},{16,0},{32,16},{48,32},{64,112},{80,64},{96,80},{112,96},{1... | collective-permute-start | bytes 110600 | tf_op jit(solution)/shard_map/ppermute | solution.py:480
  163.3 7.1 %collective-permute-start.38 = (f32[16,384]{1,0:T(8,128)S(1)}, f32[16,384]{1,0:T(8,128)S(1)}, u32[]{:S(2)}, u32[]{:S(2)}) collective-permute-start(f32[16,384]{1,0:T(8,128)S(1)} %get-tuple-element.158.a), channel_id=1, source_target_pairs={{0,16},{16,32},{32,48},{48,0},{64,80},{80,96},{96,112},{112,64},{1... | collective-permute-start | bytes 73736 | tf_op jit(solution)/shard_map/ppermute | solution.py:480
  166.4 6.6 %collective-permute-start.37 = (f32[16,384]{1,0:T(8,128)S(1)}, f32[16,384]{1,0:T(8,128)S(1)}, u32[]{:S(2)}, u32[]{:S(2)}) collective-permute-start(f32[16,384]{1,0:T(8,128)S(1)} %get-tuple-element.158.a), channel_id=1, source_target_pairs={{0,32},{16,48},{32,0},{48,16},{64,96},{80,112},{96,64},{112,80},{1... | collective-permute-start | bytes 73736 | tf_op jit(solution)/shard_map/ppermute | solution.py:480
  167.7 5.3 %collective-permute-start.36 = (f32[16,384]{1,0:T(8,128)S(1)}, f32[16,384]{1,0:T(8,128)S(1)}, u32[]{:S(2)}, u32[]{:S(2)}) collective-permute-start(f32[16,384]{1,0:T(8,128)S(1)} %get-tuple-element.158.a), channel_id=1, source_target_pairs={{0,48},{16,0},{32,16},{48,32},{64,112},{80,64},{96,80},{112,96},{1... | collective-permute-start | bytes 73736 | tf_op jit(solution)/shard_map/ppermute | solution.py:480
  173.2 4.5 %collective-permute-start.39 = (f32[32,256]{1,0:T(8,128)S(1)}, f32[32,256]{1,0:T(8,128)S(1)}, u32[]{:S(2)}, u32[]{:S(2)}) collective-permute-start(f32[32,256]{1,0:T(8,128)S(1)} %get-tuple-element.159.a), channel_id=1, source_target_pairs={{0,4},{4,0},{8,12},{12,8},{1,5},{5,1},{9,13},{13,9},{2,6},{6,2},{1... | collective-permute-start | bytes 98312 | tf_op jit(solution)/shard_map/ppermute | solution.py:480
  177.7 3.1 %collective-permute-start.40 = (f32[64,256]{1,0:T(8,128)S(1)}, f32[64,256]{1,0:T(8,128)S(1)}, u32[]{:S(2)}, u32[]{:S(2)}) collective-permute-start(f32[64,256]{1,0:T(8,128)S(1)} %shard_map.193.a), channel_id=1, source_target_pairs={{0,8},{4,12},{8,0},{12,4},{1,9},{5,13},{9,1},{13,5},{2,10},{6,14},... | collective-permute-start | bytes 196616 | tf_op jit(solution)/shard_map/ppermute | solution.py:480
  181.0 7.2 %collective-permute-start.43 = (f32[160,256]{1,0:T(8,128)S(1)}, f32[160,256]{1,0:T(8,128)S(1)}, u32[]{:S(2)}, u32[]{:S(2)}) collective-permute-start(f32[160,256]{1,0:T(8,128)S(1)} %shard_map.194.a), channel_id=1, source_target_pairs={{0,1},{1,2},{2,3},{3,0},{4,5},{5,6},{6,7},{7,4},{8,9},{9,10},{10,1... | collective-permute-start | bytes 491528 | tf_op jit(solution)/shard_map/ppermute | solution.py:480
  181.7 7.7 %collective-permute-start.42 = (f32[160,256]{1,0:T(8,128)S(1)}, f32[160,256]{1,0:T(8,128)S(1)}, u32[]{:S(2)}, u32[]{:S(2)}) collective-permute-start(f32[160,256]{1,0:T(8,128)S(1)} %shard_map.194.a), channel_id=1, source_target_pairs={{0,2},{1,3},{2,0},{3,1},{4,6},{5,7},{6,4},{7,5},{8,10},{9,11},{10,... | collective-permute-start | bytes 491528 | tf_op jit(solution)/shard_map/ppermute | solution.py:480
  182.4 8.5 %collective-permute-start.41 = (f32[160,256]{1,0:T(8,128)S(1)}, f32[160,256]{1,0:T(8,128)S(1)}, u32[]{:S(2)}, u32[]{:S(2)}) collective-permute-start(f32[160,256]{1,0:T(8,128)S(1)} %shard_map.194.a), channel_id=1, source_target_pairs={{0,3},{1,0},{2,1},{3,2},{4,7},{5,4},{6,5},{7,6},{8,11},{9,8},{10,9... | collective-permute-start | bytes 491528 | tf_op jit(solution)/shard_map/ppermute | solution.py:480
  (21 other events, 251.1 us)
where the time goes:
time: 196 us; the launch traced here: 195 us
  starting transfers between devices  78.3 us (40%)
  waiting for transfers between devices  59 us (30%)
  Pallas kernels  33.4 us (17%)
  local copies, waits for them, and re-layouts  20.7 us (11%)
  other arithmetic  2.4 us (1%)
    ppermute x44, starting transfers between devices, shifted(): return lax.ppermute(v, axis, pairs)  78.3 us
    ppermute x44, waiting for transfers between devices, shifted(): return lax.ppermute(v, axis, pairs)  59 us
    pallas_call x25, Pallas kernels, call(): pl.pallas_call(body, out_shape=shapes, in_specs=[pl.BlockSpec(memory_spac...  33.4 us
    unnamed x50, local copies, waits for them, and re-layouts  12.8 us
  transfers between devices with their start and end apart: 44, of which 23 were waited for; matrix products, arithmetic and copies ran while one was open for 5% of the time, Pallas kernels for 7%

commit v1 on v0

v1 whole, which is shorter than its diff:
```python
import jax
import jax.numpy as jnp
import numpy as np
from jax import lax
from jax.experimental import pallas as pl
from jax.experimental.pallas import tpu as pltpu
from jax.sharding import PartitionSpec as P


INTERPRET = False

C = 64
CELLS_X, CELLS_Y, CELLS_Z = 8, 16, 32
DEV_X, DEV_Y, DEV_Z = 16, 4, 4
ROWS = CELLS_X * CELLS_Y
WIDE = CELLS_Z * C
TOTAL_CELLS = CELLS_X * DEV_X * CELLS_Y * DEV_Y * CELLS_Z * DEV_Z
TOTAL_MODES = 16**3
SCALE_A = (TOTAL_CELLS * TOTAL_MODES) ** (-0.25)
SCALE_B = TOTAL_CELLS ** (-0.5)

inv_root_two = 0.7071067811865476
inv_root_tau = 0.3989422804014327
bf16 = jnp.bfloat16
f32 = jnp.float32


def cas(mode, length, position):
    mode = np.asarray(mode)
    freq = np.where(mode < 8, mode, length - 16 + mode)
    phase = (freq * position % length) * (2.0 * np.pi / length)
    return (np.cos(phase) + np.sin(phase)).astype(np.float32)


def build_tables():
    four = np.arange(4)
    z = np.arange(CELLS_Z)
    tz = np.zeros((DEV_Z, CELLS_Z, 16), np.float32)
    for d in range(DEV_Z):
        modes = (((d + four) % 4)[:, None] * 4 + four[None, :]).reshape(-1)
        tz[d] = cas(modes[None, :], CELLS_Z * DEV_Z, z[:, None] * DEV_Z + d)
    tz = np.repeat(tz, C, axis=2).astype(np.float32)
    y = np.arange(CELLS_Y)
    ty = np.zeros((DEV_Y, 4, CELLS_X, 4, CELLS_X, CELLS_Y), np.float32)
    for d in range(DEV_Y):
        modes = (d ^ np.array([0, 2, 1, 3]))[:, None] * 4 + four[None, :]
        small = cas(modes[:, :, None], CELLS_Y * DEV_Y, y * DEV_Y + d)
        for x in range(CELLS_X):
            ty[d, :, x, :, x, :] = small
    ty = ty.reshape(DEV_Y, ROWS, ROWS)
    x = np.arange(CELLS_X)
    tx = np.zeros((DEV_X, 16, 4, CELLS_X, 4), np.float32)
    for d in range(DEV_X):
        small = cas(np.arange(16)[:, None], CELLS_X * DEV_X, x * DEV_X + d)
        for l in range(4):
            tx[d, :, l, :, l] = small
    tx = tx.reshape(DEV_X, 64, CELLS_X * 4)
    return tuple(t.astype(bf16) for t in (tz, ty, tx))


def dot(left, right):
    return jnp.dot(left, right, preferred_element_type=f32)


def dot_nt(left, right):
    return lax.dot_general(left, right, (((1,), (1,)), ((), ())), preferred_element_type=f32)


def dot_tn(left, right):
    return lax.dot_general(left, right, (((0,), (0,)), ((), ())), preferred_element_type=f32)


def split(v):
    high = v.astype(bf16)
    return high, (v - high.astype(f32)).astype(bf16)


def table_dot(table, v):
    high, low = split(v)
    return dot(table, high) + dot(table, low)


def table_dot_tn(table, v):
    high, low = split(v)
    return dot_tn(table, high) + dot_tn(table, low)


def slope_of(v, cdf):
    return cdf + v * jnp.exp(-0.5 * v * v) * inv_root_tau


def cdf_of(v):
    return 0.5 * (1.0 + lax.erf(v * inv_root_two))


def call(body, outs, *args, scratch=(), limit=8, raw=0):
    near = args[1 : 1 + raw]
    rest = args[1 + raw :]
    shapes = [pltpu.VMEM(*o[:2]) if len(o) == 2 else jax.ShapeDtypeStruct(*o[:2]) for o in outs]
    if INTERPRET:
        shapes = [jax.ShapeDtypeStruct(*o[:2]) for o in outs]
    else:
        near = [pltpu.with_memory_space_constraint(a, pltpu.HBM) for a in near]
        rest = [pltpu.with_memory_space_constraint(a, pltpu.VMEM) for a in rest]
    return pl.pallas_call(
        body,
        out_shape=shapes,
        in_specs=[pl.BlockSpec(memory_space=pltpu.SMEM)]
        + [pl.BlockSpec(memory_space=pl.ANY if INTERPRET else pltpu.HBM)] * raw
        + [pl.BlockSpec(memory_space=pltpu.VMEM)] * len(rest),
        out_specs=[
            pl.BlockSpec(memory_space=(pl.ANY if INTERPRET else pltpu.HBM) if "raw" in o else pltpu.VMEM)
            for o in outs
        ],
        scratch_shapes=[pltpu.VMEM(*s) if isinstance(s, tuple) else s for s in scratch],
        interpret=INTERPRET,
        compiler_params=pltpu.CompilerParams(vmem_limit_bytes=limit << 20),
    )(*args[:1], *near, *rest)


def at_x(at):
    return at[0] >> 4


def at_y(at):
    return (at[0] >> 2) & 3


def at_z(at):
    return at[0] & 3


def block(b):
    return pl.ds(pl.multiple_of(b * 256, 256), 256)


def store_parts(v, refs):
    for j, ref in enumerate(refs):
        ref[...] = v[:, j * 256 : (j + 1) * 256]


def fill_table(ka, mine, b, wide=16 * C):
    lane = lax.broadcasted_iota(jnp.int32, (C, wide), 1) & (C - 1)
    row = lax.broadcasted_iota(jnp.int32, (C, wide), 0)
    eye = jnp.where(lane == row, 1.0, 0.0)
    for q in range(4):
        z = b * 4 + q
        here = pl.ds(pl.multiple_of(z * C, C), C) if wide > 256 else slice(q * C, (q + 1) * C)
        ka[here, :] = (eye * mine[pl.ds(z, 1), :wide]).astype(bf16)


def start_kernel(
    at, pre_from, grad_from, tz, dz_to, p1, p2, p3, mine_out, ka, total, pre, grad, dz, short, mine, sems
):
    def copies(b):
        cut = block(b)
        return (
            pltpu.make_async_copy(pre_from.at[:, cut], pre.at[:, cut], sems.at[b]),
            pltpu.make_async_copy(grad_from.at[:, cut], grad.at[:, cut], sems.at[8 + b]),
        )

    def leave(b):
        return pltpu.make_async_copy(dz.at[:, block(b)], dz_to.at[:, block(b)], sems.at[17 + b])

    first = pltpu.make_async_copy(tz.at[at_z(at)], short, sems.at[16])
    first.start()
    for b in range(8):
        for copy in copies(b):
            copy.start()
    first.wait()
    mine[...] = short[...].astype(f32)
    mine_out[...] = mine[...]

    def fill(b):
        fill_table(ka, mine, b)
        for copy in copies(b):
            copy.wait()
        cut = block(b)
        v = pre[:, cut].astype(f32)
        dz[:, cut] = (grad[:, cut].astype(f32) * slope_of(v, cdf_of(v))).astype(bf16)

    def step(b, _):
        fill(b)
        leave(b - 1).start()
        total[...] += dot(dz[:, block(b - 1)], ka[block(b - 1), 256:])
        return 0

    total[...] = jnp.zeros_like(total)
    fill(0)
    lax.fori_loop(1, 8, step, 0)
    leave(7).start()
    store_parts(total[...] + dot(dz[:, 7 * 256 :], ka[7 * 256 :, 256:]), (p1, p2, p3))
    for b in range(8):
        leave(b).wait()


def fill_point(square, point):
    square[...] = jnp.zeros_like(square)
    for i in range(4):
        square[i * C : (i + 1) * C, i * C : (i + 1) * C] = point[...]


def diagonal_sum(total):
    return sum(total[i * C : (i + 1) * C, i * C : (i + 1) * C] for i in range(4))


def side_kernel(
    at, pre, first, dz, mine, point, slope_to, local_to, weight, p0, q0, q1, q2, q3,
    ka, total, own, squares, square, slope, local, sems,
):
    fill_point(square, point)

    def leave(b):
        cut = block(b)
        return (
            pltpu.make_async_copy(slope.at[:, cut], slope_to.at[:, cut], sems.at[b]),
            pltpu.make_async_copy(local.at[:, cut], local_to.at[:, cut], sems.at[8 + b]),
        )

    def fill(b):
        fill_table(ka, mine, b)
        cut = block(b)
        v = pre[:, cut].astype(f32)
        cdf = cdf_of(v)
        slope[:, cut] = slope_of(v, cdf)
        total[b, :ROWS] = (v * cdf).astype(bf16)
        total[b, ROWS:] = first[:, cut]

    def step(b, _):
        cut = block(b)
        fill(b)
        here = dz[:, cut]
        local[:, cut] = dot_nt(here, square[...])
        for copy in leave(b):
            copy.start()
        squares[...] += dot_tn(total[b, :ROWS], here)
        own[: 2 * ROWS] += dot(total[b], ka[cut, :])
        own[2 * ROWS :, :256] += dot(here, ka[cut, :256])
        return 0

    own[...] = jnp.zeros_like(own)
    squares[...] = jnp.zeros_like(squares)
    lax.fori_loop(0, 8, step, 0)
    weight[...] = diagonal_sum(squares[...])
    p0[...] = own[2 * ROWS :, :256]
    for j, ref in enumerate((q0, q1, q2, q3)):
        ref[:, :256] = own[:ROWS, j * 256 : (j + 1) * 256]
        ref[:, 256:] = own[ROWS : 2 * ROWS, j * 256 : (j + 1) * 256]
    for b in range(8):
        for copy in leave(b):
            copy.wait()


def side_one_kernel(
    at, first, dz, mine, point, weight_two, local_to, sent, p0, ka, squares, square, local, sems
):
    fill_point(square, point)

    def leave(b):
        cut = block(b)
        return pltpu.make_async_copy(local.at[:, cut], local_to.at[:, cut], sems.at[b])

    def step(b, total):
        cut = block(b)
        here = dz[:, cut]
        local[:, cut] = dot_nt(here, square[...])
        leave(b).start()
        squares[...] += dot_tn(first[:, cut], here)
        fill_table(ka, mine, b, 256)
        return total + dot(here, ka[...])

    squares[...] = jnp.zeros_like(squares)
    p0[...] = lax.fori_loop(0, 8, step, jnp.zeros((ROWS, 256), f32))
    both = jnp.concatenate([weight_two[...], diagonal_sum(squares[...])], axis=1) * SCALE_B
    sent[...] = jnp.concatenate([both[:32], both[32:]], axis=1)
    for b in range(8):
        leave(b).wait()


def total_of(refs):
    return (refs[0][...] + refs[1][...]) + (refs[2][...] + refs[3][...])


def along_y_kernel(at, a, b, c, d, ty, near, far):
    out = table_dot(ty[at_y(at)], total_of((a, b, c, d)))
    near[...] = out[:64]
    far[...] = out[64:]


def along_y_join_kernel(at, a, b, c, d, ty, ins_near, ins_far, sent, near, far):
    out = table_dot(ty[at_y(at)], total_of((a, b, c, d)))
    for ref, ins, here in ((near, ins_near, out[:64]), (far, ins_far, out[64:])):
        ref[:, :256] = here
        ref[:, 256:768] = ins[...]
        ref[:32, 768:] = sent[...]
        ref[32:, 768:] = jnp.zeros((32, 256), f32)


def keep_kernel(at, near, got, keep, send):
    v = near[...] + got[...]
    keep[...] = v[:32]
    wide = min(v.shape[1], 768)
    send[:, :wide] = v[32:, :wide]
    if v.shape[1] > 768:
        send[:, 768:] = v[:32, 768:]


def pair_kernel(at, a, b, out):
    out[:32] = a[...]
    out[32:] = b[...]


def along_x_kernel(at, a, b, tx, out):
    v = a[...] + b[...]
    modes = table_dot(tx[at_x(at)], v[:, : min(v.shape[1], 768)])
    for i in range(16):
        out[i, :, : modes.shape[1]] = modes[i * 4 : (i + 1) * 4]
    if v.shape[1] > 768:
        weight = jnp.concatenate([v[:, 768:896], v[:, 896:]], axis=0)
        for i in range(16):
            out[i, :, 768:] = weight[i * 4 : (i + 1) * 4]


def mixed(hat, spectral, wide, fold):
    wide[...] = spectral[0].astype(f32)
    products = []
    for k in range(4):
        h = hat[:, k * C : (k + 1) * C]
        h = jnp.concatenate([h, h], axis=1)
        products.append(wide[:, k, :] * jnp.concatenate([h] * 32, axis=1))
    high, low = split(jnp.concatenate(products, axis=0))
    out = dot(jnp.concatenate([high, low], axis=0), fold[...])
    out = (out[:16] + out[16:]) * SCALE_A
    return jnp.concatenate([out[k * 4 : (k + 1) * 4] for k in range(4)], axis=1)


def sixteen(got):
    v = [got[i] for i in range(16)]
    while len(v) > 1:
        v = [v[i] + v[i + 1] for i in range(0, len(v), 2)]
    return v[0]


def mix_two_kernel(at, got, spectral, fold, back, hat_out, wide):
    hat = sixteen(got) * SCALE_B
    hat_out[...] = hat
    out = mixed(hat, spectral, wide, fold)
    for i in range(16):
        back[i] = out


def mix_one_kernel(at, got, spectral, fold, back, hat_out, mid_out, first_out, wide):
    v = sixteen(got)
    hat = v[:, :256] * SCALE_B
    hat_out[...] = hat
    mid_out[...] = v[:, 256:512] * SCALE_A
    first_out[...] = v[:, 512:768] * SCALE_A
    out = mixed(hat, spectral, wide, fold)
    for i in range(16):
        back[i, :, :256] = out
        back[i, :, 256:] = v[:, 768:]


def outer_kernel(at, left, right, fold, out):
    lefts = []
    rights = []
    for k in range(4):
        cut = slice(k * C, (k + 1) * C)
        h = right[:, cut]
        lefts.append(left[:, cut])
        rights.append(jnp.concatenate([h, h], axis=1))
    v = jnp.concatenate(lefts, axis=0)
    high, rest = v.astype(bf16), v - v.astype(bf16).astype(f32)
    low, last = split(rest)
    spread_left = dot_nt(jnp.concatenate([high, low, last], axis=0), fold[...])
    tall = jnp.concatenate(rights, axis=0)
    whole = (spread_left[:16] + spread_left[16:32]) + spread_left[32:]
    whole = whole * jnp.concatenate([tall] * 32, axis=1)
    for k in range(4):
        out[:, k, :] = whole[k * 4 : (k + 1) * 4]


def back_x_kernel(at, got, tx, out):
    v = jnp.concatenate([got[i] for i in range(16)], axis=0)
    out[...] = table_dot_tn(tx[at_x(at)], v)


def back_x_one_kernel(at, got, tx, out, weight):
    v = jnp.concatenate([got[i] for i in range(16)], axis=0)
    out[...] = table_dot_tn(tx[at_x(at)], v[:, :256])
    weight[...] = jnp.concatenate([v[:32, 256:], v[32:, 256:]], axis=1)


def back_y_kernel(at, a, b, ty, out):
    v = jnp.concatenate([a[...], b[...]], axis=0)
    out[...] = table_dot_tn(ty[at_y(at)], v)


def back_y_one_kernel(at, a, b, ty, weight, out):
    v = jnp.concatenate([a[...], b[...]], axis=0)
    out[:ROWS] = table_dot_tn(ty[at_y(at)], v)
    out[ROWS:] = weight[...]


def stack_modes(refs, modes):
    for j, ref in enumerate(refs):
        modes[:, j * 256 : (j + 1) * 256] = ref[:ROWS].astype(bf16)


def middle_kernel(
    at, a, b, c, d, mine, local, slope, dz_to, p1, p2, p3, modes, total, dz, ka, sems
):
    stack_modes((a, b, c, d), modes)

    def leave(i):
        return pltpu.make_async_copy(dz.at[:, block(i)], dz_to.at[:, block(i)], sems.at[i])

    def fill(i):
        cut = block(i)
        fill_table(ka, mine, i)
        down = dot_nt(modes[...], ka[cut, :]) + local[:, cut]
        dz[:, cut] = (down * slope[:, cut]).astype(bf16)

    def step(i, _):
        fill(i)
        leave(i - 1).start()
        total[...] += dot(dz[:, block(i - 1)], ka[block(i - 1), 256:])
        return 0

    total[...] = jnp.zeros_like(total)
    fill(0)
    lax.fori_loop(1, 8, step, 0)
    leave(7).start()
    store_parts(total[...] + dot(dz[:, 7 * 256 :], ka[7 * 256 :, 256:]), (p1, p2, p3))
    for i in range(8):
        leave(i).wait()


def end_kernel(
    at, a, b, c, d, mine, local, out_to, weight_two, weight_one, modes, out, ka, sems
):
    stack_modes((a, b, c, d), modes)

    def leave(i):
        return pltpu.make_async_copy(out.at[:, block(i)], out_to.at[:, block(i)], sems.at[i])

    def step(i, _):
        cut = block(i)
        fill_table(ka, mine, i)
        out[:, cut] = (dot_nt(modes[...], ka[cut, :]) + local[:, cut]).astype(bf16)
        leave(i).start()
        return 0

    lax.fori_loop(0, 8, step, 0)
    w = (a[ROWS:] + b[ROWS:]) + (c[ROWS:] + d[ROWS:])
    w = jnp.concatenate([w[:, :128], w[:, 128:]], axis=0)
    weight_two[...] = w[:, :C]
    weight_one[...] = w[:, C:]
    for i in range(8):
        leave(i).wait()


def shift_pairs(kind, s):
    return kind, [(i, i ^ s if kind == "gy" else (i + s) % 4) for i in range(4)]


def shifted(v, kind, s):
    axis, pairs = shift_pairs(kind, s)
    return lax.ppermute(v, axis, pairs)


def exchange(parts, kind):
    return [parts[0]] + [shifted(parts[s], kind, s) for s in (1, 2, 3)]


def spread(v, kind):
    return [v] + [shifted(v, kind, s) for s in (3, 2, 1)]


def reduce_y(at, near, far, width):
    keep, send = call(
        keep_kernel, [((32, width), f32)] * 2, at, near, shifted(far, "gy", 1)
    )
    return keep, shifted(send, "gy", 2)


def spread_y(at, v):
    (pair,) = call(pair_kernel, [((64, 256), f32)], at, v, shifted(v, "gy", 2))
    return pair, shifted(pair, "gy", 1)


def over_x(v):
    return lax.all_to_all(v, "gz", 0, 0, tiled=True)


def on_device(
    grid_input, pre_one, pre_two, grad_output, spectral_one, spectral_two, point_one, point_two
):
    tz, ty, tx = [jnp.asarray(t) for t in build_tables()]
    row = lax.broadcasted_iota(jnp.int32, (C * C, C), 0)
    fold = (row // C == lax.broadcasted_iota(jnp.int32, (C * C, C), 1)).astype(bf16)
    at = lax.axis_index(("gz", "gy", "gx")).reshape(1)
    first, pre_one, pre_two, upstream = [
        t.reshape(ROWS, WIDE) for t in (grid_input, pre_one, pre_two, grad_output)
    ]
    big = (ROWS, WIDE)
    half = ((ROWS, 256), f32)
    table = ((WIDE, 16 * C), bf16)
    native = ((4, 4, C * C), f32)
    dma = pltpu.SemaphoreType.DMA

    dz_two, *parts, mine = call(
        start_kernel,
        [(big, bf16, "raw")] + [half] * 3 + [((CELLS_Z, 16 * C), f32)],
        at,
        pre_two,
        upstream,
        tz,
        raw=3,
        scratch=[
            table,
            ((ROWS, 12 * C), f32),
            (big, bf16),
            (big, bf16),
            (big, bf16),
            ((CELLS_Z, 16 * C), bf16),
            ((CELLS_Z, 16 * C), f32),
            dma((25,)),
        ],
    )
    slope, local_two, weight_two, own, *ins = call(
        side_kernel,
        [(big, f32, "raw")] * 2 + [((C, C), f32, 0), half] + [((ROWS, 512), f32)] * 4,
        at,
        pre_one,
        first,
        dz_two,
        mine,
        point_two,
        limit=14,
        scratch=[
            table,
            ((8, 2 * ROWS, 256), bf16),
            ((3 * ROWS, 16 * C), f32),
            ((256, 256), f32),
            ((256, 256), bf16),
            (big, f32),
            (big, f32),
            dma((16,)),
        ],
    )
    got = exchange([own] + parts, "gx")
    near, far = call(along_y_kernel, [((64, 256), f32)] * 2, at, *got, ty)
    got = reduce_y(at, near, far, 256)
    (modes,) = call(along_x_kernel, [((16, 4, 256), f32)], at, *got, tx)
    got_in = exchange(ins, "gx")
    modes, got_in[0] = lax.optimization_barrier((modes, got_in[0]))
    got = over_x(modes)
    back, hat_two = call(
        mix_two_kernel,
        [((16, 4, 256), f32), ((4, 256), f32)],
        at,
        got,
        spectral_two,
        fold,
        scratch=[native],
    )
    got = over_x(back)
    got, got_in = lax.optimization_barrier((got, got_in))
    (tall,) = call(back_x_kernel, [((32, 256), f32)], at, got, tx)
    got = spread_y(at, tall)
    (tall,) = call(back_y_kernel, [half], at, *got, ty)
    got = spread(tall, "gx")
    ins = call(along_y_kernel, [((64, 512), f32)] * 2, at, *got_in, ty)
    dz_one, *parts = call(
        middle_kernel,
        [(big, bf16, "raw")] + [half] * 3,
        at,
        *got,
        mine,
        local_two,
        slope,
        scratch=[((ROWS, 16 * C), bf16), ((ROWS, 12 * C), f32), (big, bf16), table, dma((8,))],
    )
    local_one, sent, own = call(
        side_one_kernel,
        [(big, f32, "raw"), ((32, 256), f32), half],
        at,
        first,
        dz_one,
        mine,
        point_one,
        weight_two,
        scratch=[
            ((256, 256), bf16),
            ((256, 256), f32),
            ((256, 256), bf16),
            (big, f32),
            dma((8,)),
        ],
    )
    got = exchange([own] + parts, "gx")
    near, far = call(along_y_join_kernel, [((64, 1024), f32)] * 2, at, *got, ty, *ins, sent)
    got = reduce_y(at, near, far, 1024)
    (modes,) = call(along_x_kernel, [((16, 4, 896), f32)], at, *got, tx)
    back, hat_one, mid_hat, first_hat = call(
        mix_one_kernel,
        [((16, 4, 384), f32)] + [((4, 256), f32)] * 3,
        at,
        over_x(modes),
        spectral_one,
        fold,
        scratch=[native],
    )
    (spec_two,) = call(outer_kernel, [(*native, 0)], at, mid_hat, hat_two, fold)
    (spec_one,) = call(outer_kernel, [(*native, 0)], at, first_hat, hat_one, fold)
    tall, weight = call(back_x_one_kernel, [((32, 256), f32)] * 2, at, over_x(back), tx)
    got = spread_y(at, tall)
    (tall,) = call(back_y_one_kernel, [((ROWS + 32, 256), f32)], at, *got, ty, weight)
    got = spread(tall, "gx")
    input_grad, weight_two, weight_one = call(
        end_kernel,
        [(big, bf16, "raw"), ((C, C), f32, 0), ((C, C), f32, 0)],
        at,
        *got,
        mine,
        local_one,
        scratch=[((ROWS, 16 * C), bf16), (big, bf16), table, dma((8,))],
    )
    return (
        input_grad.reshape(CELLS_X, CELLS_Y, WIDE),
        spec_one[None],
        spec_two[None],
        weight_one,
        weight_two,
    )


def solution(mesh):
    grid = P("gz", "gy", "gx")
    modes = P("gz", "gy", "gx", None)
    return jax.shard_map(
        on_device,
        mesh=mesh,
        in_specs=(grid, grid, grid, grid, modes, modes, P(), P()),
        out_specs=(grid, modes, modes, P(), P()),
        check_vma=False,
    )
```

time: 196 us -> 162 us (0.83)
  starting transfers between devices: 78.3 us -> 47.9 us
  blocking collectives: 0 us -> 26.4 us
  local copies, waits for them, and re-layouts: 20.7 us -> 3.15 us
  waiting for transfers between devices: 59 us -> 45 us
    ppermute x44 -> x23, starting transfers between devices: 78.3 us -> 35 us  [shifted(): return lax.ppermute(v, axis, pairs)]
    ppermute x44 -> x23, waiting for transfers between devices: 59 us -> 30.4 us  [shifted(): return lax.ppermute(v, axis, pairs)]
    all_to_all x0 -> x2, blocking collectives: none -> 26.4 us  [over_x(): return lax.all_to_all(v, 'gz', 0, 0, tiled=True)]
    all_to_all x0 -> x2, waiting for transfers between devices: none -> 14.6 us  [over_x(): return lax.all_to_all(v, 'gz', 0, 0, tiled=True)]
    all_to_all x0 -> x2, starting transfers between devices: none -> 12.9 us  [over_x(): return lax.all_to_all(v, 'gz', 0, 0, tiled=True)]
    unnamed x50 -> x20, local copies, waits for them, and re-layouts: 12.8 us -> 3.15 us
    mul x2 -> x0, local copies, waits for them, and re-layouts: 3.03 us -> none  [on_device(): eye[:, None, :, None] * p.T[None, :, None, :]]
    transpose x2 -> x0, local copies, waits for them, and re-layouts: 2.8 us -> none  [on_device(): p.T[None, :, None, :]]
  transfers between devices with their start and end apart: 44 -> 25, of which waited for: 23 -> 16; matrix products, arithmetic and copies ran while one was open for 5% -> 2% of each run, Pallas kernels for 7% -> 11%
where the time goes in v1:
time: 162 us; the launch traced here: 161 us
  starting transfers between devices  47.9 us (30%)
  waiting for transfers between devices  45 us (28%)
  Pallas kernels  34.4 us (21%)
  blocking collectives  26.4 us (16%)
  other arithmetic  3.38 us (2%)
  local copies, waits for them, and re-layouts  3.15 us (2%)
    ppermute x23, starting transfers between devices, shifted(): return lax.ppermute(v, axis, pairs)  35 us
    pallas_call x22, Pallas kernels, call(): pl.pallas_call(body, out_shape=shapes, in_specs=[pl.BlockSpec(memory_spac...  34.4 us
    ppermute x23, waiting for transfers between devices, shifted(): return lax.ppermute(v, axis, pairs)  30.4 us
    all_to_all x2, blocking collectives, over_x(): return lax.all_to_all(v, 'gz', 0, 0, tiled=True)  26.4 us
    all_to_all x2, waiting for transfers between devices, over_x(): return lax.all_to_all(v, 'gz', 0, 0, tiled=True)  14.6 us
    all_to_all x2, starting transfers between devices, over_x(): return lax.all_to_all(v, 'gz', 0, 0, tiled=True)  12.9 us
    convert_element_type x1, other arithmetic, on_device(): (row // C == lax.broadcasted_iota(jnp.int32, (C * C, C), 1)).astype(bf16)  3.37 us
  transfers between devices with their start and end apart: 25, of which 16 were waited for; matrix products, arithmetic and copies ran while one was open for 2% of the time, Pallas kernels for 11%

profile of v1, /device:TPU:1, one launch (start us, length us, event | category | flops | bytes accessed | tf_op | source)
XLA Modules:
  0.0 161.3 jit_solution(9046517509642213655)
XLA Ops:
  0.7 4.5 %shard_map.146 = (bf16[128,2048]{1,0:T(8,128)(2,1)S(1)}, f32[128,256]{1,0:T(8,128)S(1)}, f32[128,256]{1,0:T(8,128)S(1)}, f32[128,256]{1,0:T(8,128)S(1)}, f32[32,1024]{1,0:T(8,128)S(1)}) custom-call(s32[1]{0:T(128)} %bitcast.at, bf16[128,2048]{1,0:T(8,128)(2,1)} %bitcast.11, bf16[128,2048]{1,0:T(8,128)(2,1)} %bitcast.12, bf16[4,32,1024]{2,1,0:T(8,128)(2,1)} %constant.42.clone.tz), custom_call_target="tpu_custom_call" | custom-call | tf_op jit(solution)/shard_map/pallas_call | solution.py:105
  5.2 2.2 %collective-permute-start = (f32[128,256]{1,0:T(8,128)S(1)}, f32[128,256]{1,0:T(8,128)S(1)}, u32[]{:S(2)}, u32[]{:S(2)}) collective-permute-start(f32[128,256]{1,0:T(8,128)S(1)} %get-tuple-element.56), channel_id=1, source_target_pairs={{0,1},{1,2},{2,3},{3,0},{4,5},{5,6},{6,7},{7,4},{8,9},{9,10},{10,1... | collective-permute-start | bytes 393224 | tf_op jit(solution)/shard_map/ppermute | solution.py:469
  7.3 2.6 %collective-permute-start.1 = (f32[128,256]{1,0:T(8,128)S(1)}, f32[128,256]{1,0:T(8,128)S(1)}, u32[]{:S(2)}, u32[]{:S(2)}) collective-permute-start(f32[128,256]{1,0:T(8,128)S(1)} %get-tuple-element.57), channel_id=1, source_target_pairs={{0,2},{1,3},{2,0},{3,1},{4,6},{5,7},{6,4},{7,5},{8,10},{9,11},{10,... | collective-permute-start | bytes 393224 | tf_op jit(solution)/shard_map/ppermute | solution.py:469
  10.0 1.1 collective-permute-start.2
  11.1 7.6 %shard_map.147 = (f32[128,2048]{1,0:T(8,128)S(1)}, f32[128,2048]{1,0:T(8,128)S(1)}, f32[64,64]{1,0:T(8,128)S(1)}, f32[128,256]{1,0:T(8,128)S(1)}, f32[128,512]{1...) custom-call(s32[1]{0:T(128)} %bitcast.at, bf16[128,2048]{1,0:T(8,128)(2,1)S(1)} %bitcast.10, ...), custom_call_target="tpu_custom_call" | custom-call | tf_op jit(solution)/shard_map/pallas_call | solution.py:105
  18.6 1.0 copy-done.3
  20.0 0.8 collective-permute-start.6
  20.8 1.6 collective-permute-start.7
  22.6 3.5 %collective-permute-start.3 = (f32[64,256]{1,0:T(8,128)S(1)}, f32[64,256]{1,0:T(8,128)S(1)}, u32[]{:S(2)}, u32[]{:S(2)}) collective-permute-start(f32[64,256]{1,0:T(8,128)S(1)} %get-tuple-element.60), channel_id=1, source_target_pairs={{0,4},{4,0},{8,12},{12,8},{1,5},{5,1},{9,13},{13,9},{2,6},{6,2},{1... | collective-permute-start | bytes 196616 | tf_op jit(solution)/shard_map/ppermute | solution.py:469
  26.1 0.9 collective-permute-done.3.got
  27.4 2.8 %collective-permute-done.4.b = f32[32,256]{1,0:T(8,128)S(1)} collective-permute-done((f32[32,256]{1,0:T(8,128)S(1)}, f32[32,256]{1,0:T(8,128)S(1)}, u32[]{:S(2)}, u32[]{:S(2)}) %collective-permute-start.4) | collective-permute-done | bytes 32800 | tf_op jit(solution)/shard_map/ppermute | solution.py:469
  30.3 0.8 shard_map.150
  31.0 9.4 %all-to-all-start = ((f32[16,4,256]{2,1,0:T(4,128)}), f32[16,4,256]{2,1,0:T(4,128)S(1)}, u32[]{:S(2)}, u32[]{:S(2)}) async-start(f32[16,4,256]{2,1,0:T(4,128)} %shard_map.150), calls=%async_computation | async-start | bytes 131072 | tf_op jit(solution)/shard_map/all_to_all | solution.py:493
  40.5 3.4 %fusion.fold = bf16[4096,64]{1,0:T(8,128)(2,1)S(1)} fusion(s32[4096]{0:T(1024)S(1)} %get-tuple-element.101, s32[4096]{0:T(1024)S(1)} %get-tuple-element.102, pred[4096]{0:T(1024)(128)(4,1)S(1)} %fusion.3), kind=kLoop, calls=%fused_computation.1 | loop fusion | flops 786432 | bytes 561152 | tf_op jit(solution)/shard_map/convert_element_type | solution.py:501
  43.9 5.6 %all-to-all-done.got = f32[16,4,256]{2,1,0:T(4,128)S(1)} async-done(((f32[16,4,256]{2,1,0:T(4,128)}), f32[16,4,256]{2,1,0:T(4,128)S(1)}, u32[]{:S(2)}, u32[]{:S(2)}) %all-to-all-start) | async-done | bytes 65568 | tf_op jit(solution)/shard_map/all_to_all | solution.py:493
  49.5 0.9 copy-done.6
  50.4 1.1 shard_map.151
  51.5 3.5 %all-to-all-start.1 = ((f32[16,4,256]{2,1,0:T(4,128)}), f32[16,4,256]{2,1,0:T(4,128)S(1)}, u32[]{:S(2)}, u32[]{:S(2)}) async-start(f32[16,4,256]{2,1,0:T(4,128)} %get-tuple-element.65), calls=%async_computation.1 | async-start | bytes 131072 | tf_op jit(solution)/shard_map/all_to_all | solution.py:493
  55.0 9.0 %all-to-all-done.1.got = f32[16,4,256]{2,1,0:T(4,128)S(1)} async-done(((f32[16,4,256]{2,1,0:T(4,128)}), f32[16,4,256]{2,1,0:T(4,128)S(1)}, u32[]{:S(2)}, u32[]{:S(2)}) %all-to-all-start.1) | async-done | bytes 65568 | tf_op jit(solution)/shard_map/all_to_all | solution.py:493
  64.9 2.3 %collective-permute-done.8.b = f32[32,256]{1,0:T(8,128)S(1)} collective-permute-done((f32[32,256]{1,0:T(8,128)S(1)}, f32[32,256]{1,0:T(8,128)S(1)}, u32[]{:S(2)}, u32[]{:S(2)}) %collective-permute-start.8) | collective-permute-done | bytes 32800 | tf_op jit(solution)/shard_map/ppermute | solution.py:469
  67.2 4.6 %collective-permute-start.9 = (f32[64,256]{1,0:T(8,128)S(1)}, f32[64,256]{1,0:T(8,128)S(1)}, u32[]{:S(2)}, u32[]{:S(2)}) collective-permute-start(f32[64,256]{1,0:T(8,128)S(1)} %shard_map.153.a), channel_id=1, source_target_pairs={{0,4},{4,0},{8,12},{12,8},{1,5},{5,1},{9,13},{13,9},{2,6},{6,2},{1... | collective-permute-start | bytes 196616 | tf_op jit(solution)/shard_map/ppermute | solution.py:469
  71.9 0.9 collective-permute-done.9.b
  73.0 1.2 collective-permute-start.10
  74.2 1.7 %collective-permute-start.11 = (f32[128,256]{1,0:T(8,128)S(1)}, f32[128,256]{1,0:T(8,128)S(1)}, u32[]{:S(2)}, u32[]{:S(2)}) collective-permute-start(f32[128,256]{1,0:T(8,128)S(1)} %shard_map.154.a), channel_id=1, source_target_pairs={{0,2},{1,3},{2,0},{3,1},{4,6},{5,7},{6,4},{7,5},{8,10},{9,11},{10,... | collective-permute-start | bytes 393224 | tf_op jit(solution)/shard_map/ppermute | solution.py:469
  76.7 1.1 collective-permute-done.10.b
  77.8 2.4 %collective-permute-done.11.c = f32[128,256]{1,0:T(8,128)S(1)} collective-permute-done((f32[128,256]{1,0:T(8,128)S(1)}, f32[128,256]{1,0:T(8,128)S(1)}, u32[]{:S(2)}, u32[]{:S(2)}) %collective-permute-start.11) | collective-permute-done | bytes 131104 | tf_op jit(solution)/shard_map/ppermute | solution.py:469
  80.1 3.5 %collective-permute-done.12.d = f32[128,256]{1,0:T(8,128)S(1)} collective-permute-done((f32[128,256]{1,0:T(8,128)S(1)}, f32[128,256]{1,0:T(8,128)S(1)}, u32[]{:S(2)}, u32[]{:S(2)}) %collective-permute-start.12) | collective-permute-done | bytes 131104 | tf_op jit(solution)/shard_map/ppermute | solution.py:469
  83.6 1.2 copy-done.4
  84.8 5.8 %shard_map.155 = (bf16[128,2048]{1,0:T(8,128)(2,1)S(1)}, f32[128,256]{1,0:T(8,128)S(1)}, f32[128,256]{1,0:T(8,128)S(1)}, f32[128,256]{1,0:T(8,128)S(1)}) custom-call(s32[1]{0:T(128)} %bitcast.at, f32[128,256]{1,0:T(8,128)S(1)} %shard_map.154.a, f32[128,256]{1,0:T(8,128)S(1)} %collective-permute-done.10.b, f32[128,256]{1,0:T(8,128)S(1)} %collective-permute-done.11.c, ...), custom_call_target="tpu_custom_call" | custom-call | tf_op jit(solution)/shard_map/pallas_call | solution.py:105
  90.7 1.6 collective-permute-start.14
  92.3 2.0 %collective-permute-start.15 = (f32[128,256]{1,0:T(8,128)S(1)}, f32[128,256]{1,0:T(8,128)S(1)}, u32[]{:S(2)}, u32[]{:S(2)}) collective-permute-start(f32[128,256]{1,0:T(8,128)S(1)} %get-tuple-element.78), channel_id=1, source_target_pairs={{0,3},{1,0},{2,1},{3,2},{4,7},{5,4},{6,5},{7,6},{8,11},{9,8},{10,9... | collective-permute-start | bytes 393224 | tf_op jit(solution)/shard_map/ppermute | solution.py:469
  94.3 1.4 shard_map.157
  95.7 4.4 %shard_map.156 = (f32[128,2048]{1,0:T(8,128)S(1)}, f32[32,256]{1,0:T(8,128)S(1)}, f32[128,256]{1,0:T(8,128)S(1)}) custom-call(s32[1]{0:T(128)} %bitcast.at, bf16[128,2048]{1,0:T(8,128)(2,1)S(1)} %bitcast.9, bf16[128,2048]{1,0:T(8,128)(2,1)S(1)} %get-tuple-element.73.dz, f32[32,1024]{1,0:T(8,128)S(1)} %get-tuple-element.54.mine, ...), custom_call_target="tpu_custom_call" | custom-call | tf_op jit(solution)/shard_map/pallas_call | solution.py:105
  100.3 1.7 %collective-permute-start.16 = (f32[64,1024]{1,0:T(8,128)S(1)}, f32[64,1024]{1,0:T(8,128)S(1)}, u32[]{:S(2)}, u32[]{:S(2)}) collective-permute-start(f32[64,1024]{1,0:T(8,128)S(1)} %get-tuple-element.87), channel_id=1, source_target_pairs={{0,4},{4,0},{8,12},{12,8},{1,5},{5,1},{9,13},{13,9},{2,6},{6,2},{1... | collective-permute-start | bytes 786440 | tf_op jit(solution)/shard_map/ppermute | solution.py:469
  102.0 1.2 collective-permute-done.16.got
  103.2 0.8 collective-permute-start.17
  104.0 4.0 %collective-permute-done.17.b = f32[32,1024]{1,0:T(8,128)S(1)} collective-permute-done((f32[32,1024]{1,0:T(8,128)S(1)}, f32[32,1024]{1,0:T(8,128)S(1)}, u32[]{:S(2)}, u32[]{:S(2)}) %collective-permute-start.17) | collective-permute-done | bytes 131104 | tf_op jit(solution)/shard_map/ppermute | solution.py:469
  108.2 13.9 %all_to_all.20.got = f32[16,4,896]{2,1,0:T(4,128)S(1)} all-to-all(f32[16,4,896]{2,1,0:T(4,128)S(1)} %shard_map.160), channel_id=1, replica_groups=mesh['gz'=16,'gy'=4,'gx'=4] {'gz'}, dimensions={0} | all-to-all | bytes 458752 | tf_op jit(solution)/shard_map/all_to_all | solution.py:493
  122.5 12.5 %all_to_all.21.got = f32[16,4,384]{2,1,0:T(4,128)S(1)} all-to-all(f32[16,4,384]{2,1,0:T(4,128)S(1)} %get-tuple-element.90), channel_id=1, replica_groups=mesh['gz'=16,'gy'=4,'gx'=4] {'gz'}, dimensions={0} | all-to-all | bytes 196608 | tf_op jit(solution)/shard_map/all_to_all | solution.py:493
  135.6 2.3 %collective-permute-done.18.b = f32[32,256]{1,0:T(8,128)S(1)} collective-permute-done((f32[32,256]{1,0:T(8,128)S(1)}, f32[32,256]{1,0:T(8,128)S(1)}, u32[]{:S(2)}, u32[]{:S(2)}) %collective-permute-start.18) | collective-permute-done | bytes 32800 | tf_op jit(solution)/shard_map/ppermute | solution.py:469
  138.0 4.1 %collective-permute-start.19 = (f32[64,256]{1,0:T(8,128)S(1)}, f32[64,256]{1,0:T(8,128)S(1)}, u32[]{:S(2)}, u32[]{:S(2)}) collective-permute-start(f32[64,256]{1,0:T(8,128)S(1)} %shard_map.163.a), channel_id=1, source_target_pairs={{0,4},{4,0},{8,12},{12,8},{1,5},{5,1},{9,13},{13,9},{2,6},{6,2},{1... | collective-permute-start | bytes 196616 | tf_op jit(solution)/shard_map/ppermute | solution.py:469
  142.1 0.9 collective-permute-done.19.b
  143.2 2.0 %collective-permute-start.20 = (f32[160,256]{1,0:T(8,128)S(1)}, f32[160,256]{1,0:T(8,128)S(1)}, u32[]{:S(2)}, u32[]{:S(2)}) collective-permute-start(f32[160,256]{1,0:T(8,128)S(1)} %shard_map.164.a), channel_id=1, source_target_pairs={{0,3},{1,0},{2,1},{3,2},{4,7},{5,4},{6,5},{7,6},{8,11},{9,8},{10,9... | collective-permute-start | bytes 491528 | tf_op jit(solution)/shard_map/ppermute | solution.py:469
  145.9 1.2 shard_map.167
  147.1 1.2 shard_map.166
  148.7 3.2 %collective-permute-done.21.c = f32[160,256]{1,0:T(8,128)S(1)} collective-permute-done((f32[160,256]{1,0:T(8,128)S(1)}, f32[160,256]{1,0:T(8,128)S(1)}, u32[]{:S(2)}, u32[]{:S(2)}) %collective-permute-start.21) | collective-permute-done | bytes 163872 | tf_op jit(solution)/shard_map/ppermute | solution.py:469
  151.9 4.5 %collective-permute-done.22.d = f32[160,256]{1,0:T(8,128)S(1)} collective-permute-done((f32[160,256]{1,0:T(8,128)S(1)}, f32[160,256]{1,0:T(8,128)S(1)}, u32[]{:S(2)}, u32[]{:S(2)}) %collective-permute-start.22) | collective-permute-done | bytes 163872 | tf_op jit(solution)/shard_map/ppermute | solution.py:469
  156.3 4.8 %shard_map.165 = (bf16[128,2048]{1,0:T(8,128)(2,1)}, f32[64,64]{1,0:T(8,128)}, f32[64,64]{1,0:T(8,128)}) custom-call(s32[1]{0:T(128)} %bitcast.at, f32[160,256]{1,0:T(8,128)S(1)} %shard_map.164.a, f32[160,256]{1,0:T(8,128)S(1)} %collective-permute-done.20.b, f32[160,256]{1,0:T(8,128)S(1)} %collective-permute-done.21.c, ...), custom_call_target="tpu_custom_call" | custom-call | tf_op jit(solution)/shard_map/pallas_call | solution.py:105
  (49 shorter events, 5.8 us)
Async XLA Ops:
  0.6 10.4 %copy-start.2 = (bf16[8,16,2048]{2,1,0:T(8,128)(2,1)S(1)}, bf16[8,16,2048]{2,1,0:T(8,128)(2,1)}, u32[]{:S(2)}) copy-start(bf16[8,16,2048]{2,1,0:T(8,128)(2,1)} %param.11) | copy-start | bytes 1572868
  0.6 10.4 %copy-start.5 = (bf16[8,16,2048]{2,1,0:T(8,128)(2,1)S(1)}, bf16[8,16,2048]{2,1,0:T(8,128)(2,1)}, u32[]{:S(2)}) copy-start(bf16[8,16,2048]{2,1,0:T(8,128)(2,1)} %param.12) | copy-start | bytes 1572868
  0.7 10.4 %copy-start.8 = (bf16[64,64]{1,0:T(8,128)(2,1)S(1)}, bf16[64,64]{1,0:T(8,128)(2,1)}, u32[]{:S(2)}) copy-start(bf16[64,64]{1,0:T(8,128)(2,1)} %point.2) | copy-start | bytes 24580
  5.1 17.3 %copy-start.1 = (bf16[4,128,128]{2,1,0:T(8,128)(2,1)S(1)}, bf16[4,128,128]{2,1,0:T(8,128)(2,1)}, u32[]{:S(2)}) copy-start(bf16[4,128,128]{2,1,0:T(8,128)(2,1)} %constant.43.clone.ty) | copy-start | bytes 393220
  5.2 15.7 %collective-permute-start = (f32[128,256]{1,0:T(8,128)S(1)}, f32[128,256]{1,0:T(8,128)S(1)}, u32[]{:S(2)}, u32[]{:S(2)}) collective-permute-start(f32[128,256]{1,0:T(8,128)S(1)} %get-tuple-element.56), channel_id=1, source_target_pairs={{0,1},{1,2},{2,3},{3,0},{4,5},{5,6},{6,7},{7,4},{8,9},{9,10},{10,1... | collective-permute-start | bytes 393224 | tf_op jit(solution)/shard_map/ppermute | solution.py:469
  7.3 15.1 %collective-permute-start.1 = (f32[128,256]{1,0:T(8,128)S(1)}, f32[128,256]{1,0:T(8,128)S(1)}, u32[]{:S(2)}, u32[]{:S(2)}) collective-permute-start(f32[128,256]{1,0:T(8,128)S(1)} %get-tuple-element.57), channel_id=1, source_target_pairs={{0,2},{1,3},{2,0},{3,1},{4,6},{5,7},{6,4},{7,5},{8,10},{9,11},{10,... | collective-permute-start | bytes 393224 | tf_op jit(solution)/shard_map/ppermute | solution.py:469
  10.0 12.4 %collective-permute-start.2 = (f32[128,256]{1,0:T(8,128)S(1)}, f32[128,256]{1,0:T(8,128)S(1)}, u32[]{:S(2)}, u32[]{:S(2)}) collective-permute-start(f32[128,256]{1,0:T(8,128)S(1)} %get-tuple-element.58), channel_id=1, source_target_pairs={{0,3},{1,0},{2,1},{3,2},{4,7},{5,4},{6,5},{7,6},{8,11},{9,8},{10,9... | collective-permute-start | bytes 393224 | tf_op jit(solution)/shard_map/ppermute | solution.py:469
  11.0 19.2 %copy-start = (bf16[16,64,32]{2,1,0:T(8,128)(2,1)S(1)}, bf16[16,64,32]{2,1,0:T(8,128)(2,1)}, u32[]{:S(2)}) copy-start(bf16[16,64,32]{2,1,0:T(8,128)(2,1)} %constant.44.clone.tx) | copy-start | bytes 196612
  18.6 1.0 copy-start.3
  19.6 35.4 %collective-permute-start.5 = (f32[128,512]{1,0:T(8,128)}, f32[128,512]{1,0:T(8,128)}, u32[]{:S(2)}, u32[]{:S(2)}) collective-permute-start(f32[128,512]{1,0:T(8,128)} %get-tuple-element.67), channel_id=1, source_target_pairs={{0,1},{1,2},{2,3},{3,0},{4,5},{5,6},{6,7},{7,4},{8,9},{9,10},{10,1... | collective-permute-start | bytes 786440 | tf_op jit(solution)/shard_map/ppermute | solution.py:469
  20.0 35.0 %collective-permute-start.6 = (f32[128,512]{1,0:T(8,128)}, f32[128,512]{1,0:T(8,128)}, u32[]{:S(2)}, u32[]{:S(2)}) collective-permute-start(f32[128,512]{1,0:T(8,128)} %get-tuple-element.68), channel_id=1, source_target_pairs={{0,2},{1,3},{2,0},{3,1},{4,6},{5,7},{6,4},{7,5},{8,10},{9,11},{10,... | collective-permute-start | bytes 786440 | tf_op jit(solution)/shard_map/ppermute | solution.py:469
  20.8 34.2 %collective-permute-start.7 = (f32[128,512]{1,0:T(8,128)}, f32[128,512]{1,0:T(8,128)}, u32[]{:S(2)}, u32[]{:S(2)}) collective-permute-start(f32[128,512]{1,0:T(8,128)} %get-tuple-element.69), channel_id=1, source_target_pairs={{0,3},{1,0},{2,1},{3,2},{4,7},{5,4},{6,5},{7,6},{8,11},{9,8},{10,9... | collective-permute-start | bytes 786440 | tf_op jit(solution)/shard_map/ppermute | solution.py:469
  22.6 4.4 %collective-permute-start.3 = (f32[64,256]{1,0:T(8,128)S(1)}, f32[64,256]{1,0:T(8,128)S(1)}, u32[]{:S(2)}, u32[]{:S(2)}) collective-permute-start(f32[64,256]{1,0:T(8,128)S(1)} %get-tuple-element.60), channel_id=1, source_target_pairs={{0,4},{4,0},{8,12},{12,8},{1,5},{5,1},{9,13},{13,9},{2,6},{6,2},{1... | collective-permute-start | bytes 196616 | tf_op jit(solution)/shard_map/ppermute | solution.py:469
  27.0 3.3 %collective-permute-start.4 = (f32[32,256]{1,0:T(8,128)S(1)}, f32[32,256]{1,0:T(8,128)S(1)}, u32[]{:S(2)}, u32[]{:S(2)}) collective-permute-start(f32[32,256]{1,0:T(8,128)S(1)} %get-tuple-element.62), channel_id=1, source_target_pairs={{0,8},{4,12},{8,0},{12,4},{1,9},{5,13},{9,1},{13,5},{2,10},{6,14},... | collective-permute-start | bytes 98312 | tf_op jit(solution)/shard_map/ppermute | solution.py:469
  31.0 18.5 %all-to-all-start = ((f32[16,4,256]{2,1,0:T(4,128)}), f32[16,4,256]{2,1,0:T(4,128)S(1)}, u32[]{:S(2)}, u32[]{:S(2)}) async-start(f32[16,4,256]{2,1,0:T(4,128)} %shard_map.150), calls=%async_computation | async-start | bytes 131072 | tf_op jit(solution)/shard_map/all_to_all | solution.py:493
  49.5 0.9 copy-start.6
  51.5 12.5 %all-to-all-start.1 = ((f32[16,4,256]{2,1,0:T(4,128)}), f32[16,4,256]{2,1,0:T(4,128)S(1)}, u32[]{:S(2)}, u32[]{:S(2)}) async-start(f32[16,4,256]{2,1,0:T(4,128)} %get-tuple-element.65), calls=%async_computation.1 | async-start | bytes 131072 | tf_op jit(solution)/shard_map/all_to_all | solution.py:493
  64.2 3.1 %collective-permute-start.8 = (f32[32,256]{1,0:T(8,128)S(1)}, f32[32,256]{1,0:T(8,128)S(1)}, u32[]{:S(2)}, u32[]{:S(2)}) collective-permute-start(f32[32,256]{1,0:T(8,128)S(1)} %shard_map.152.a), channel_id=1, source_target_pairs={{0,8},{4,12},{8,0},{12,4},{1,9},{5,13},{9,1},{13,5},{2,10},{6,14},... | collective-permute-start | bytes 98312 | tf_op jit(solution)/shard_map/ppermute | solution.py:469
  67.2 5.5 %collective-permute-start.9 = (f32[64,256]{1,0:T(8,128)S(1)}, f32[64,256]{1,0:T(8,128)S(1)}, u32[]{:S(2)}, u32[]{:S(2)}) collective-permute-start(f32[64,256]{1,0:T(8,128)S(1)} %shard_map.153.a), channel_id=1, source_target_pairs={{0,4},{4,0},{8,12},{12,8},{1,5},{5,1},{9,13},{13,9},{2,6},{6,2},{1... | collective-permute-start | bytes 196616 | tf_op jit(solution)/shard_map/ppermute | solution.py:469
  73.0 4.8 %collective-permute-start.10 = (f32[128,256]{1,0:T(8,128)S(1)}, f32[128,256]{1,0:T(8,128)S(1)}, u32[]{:S(2)}, u32[]{:S(2)}) collective-permute-start(f32[128,256]{1,0:T(8,128)S(1)} %shard_map.154.a), channel_id=1, source_target_pairs={{0,3},{1,0},{2,1},{3,2},{4,7},{5,4},{6,5},{7,6},{8,11},{9,8},{10,9... | collective-permute-start | bytes 393224 | tf_op jit(solution)/shard_map/ppermute | solution.py:469
  74.2 5.9 %collective-permute-start.11 = (f32[128,256]{1,0:T(8,128)S(1)}, f32[128,256]{1,0:T(8,128)S(1)}, u32[]{:S(2)}, u32[]{:S(2)}) collective-permute-start(f32[128,256]{1,0:T(8,128)S(1)} %shard_map.154.a), channel_id=1, source_target_pairs={{0,2},{1,3},{2,0},{3,1},{4,6},{5,7},{6,4},{7,5},{8,10},{9,11},{10,... | collective-permute-start | bytes 393224 | tf_op jit(solution)/shard_map/ppermute | solution.py:469
  75.9 7.7 %collective-permute-start.12 = (f32[128,256]{1,0:T(8,128)S(1)}, f32[128,256]{1,0:T(8,128)S(1)}, u32[]{:S(2)}, u32[]{:S(2)}) collective-permute-start(f32[128,256]{1,0:T(8,128)S(1)} %shard_map.154.a), channel_id=1, source_target_pairs={{0,1},{1,2},{2,3},{3,0},{4,5},{5,6},{6,7},{7,4},{8,9},{9,10},{10,1... | collective-permute-start | bytes 393224 | tf_op jit(solution)/shard_map/ppermute | solution.py:469
  83.6 1.2 copy-start.4
  90.6 5.0 %copy-start.9 = (bf16[64,64]{1,0:T(8,128)(2,1)S(1)}, bf16[64,64]{1,0:T(8,128)(2,1)}, u32[]{:S(2)}) copy-start(bf16[64,64]{1,0:T(8,128)(2,1)} %point.3) | copy-start | bytes 24580
  90.6 9.4 %collective-permute-start.13 = (f32[128,256]{1,0:T(8,128)S(1)}, f32[128,256]{1,0:T(8,128)S(1)}, u32[]{:S(2)}, u32[]{:S(2)}) collective-permute-start(f32[128,256]{1,0:T(8,128)S(1)} %get-tuple-element.76), channel_id=1, source_target_pairs={{0,1},{1,2},{2,3},{3,0},{4,5},{5,6},{6,7},{7,4},{8,9},{9,10},{10,1... | collective-permute-start | bytes 393224 | tf_op jit(solution)/shard_map/ppermute | solution.py:469
  90.7 9.4 %collective-permute-start.14 = (f32[128,256]{1,0:T(8,128)S(1)}, f32[128,256]{1,0:T(8,128)S(1)}, u32[]{:S(2)}, u32[]{:S(2)}) collective-permute-start(f32[128,256]{1,0:T(8,128)S(1)} %get-tuple-element.77), channel_id=1, source_target_pairs={{0,2},{1,3},{2,0},{3,1},{4,6},{5,7},{6,4},{7,5},{8,10},{9,11},{10,... | collective-permute-start | bytes 393224 | tf_op jit(solution)/shard_map/ppermute | solution.py:469
  92.3 7.8 %collective-permute-start.15 = (f32[128,256]{1,0:T(8,128)S(1)}, f32[128,256]{1,0:T(8,128)S(1)}, u32[]{:S(2)}, u32[]{:S(2)}) collective-permute-start(f32[128,256]{1,0:T(8,128)S(1)} %get-tuple-element.78), channel_id=1, source_target_pairs={{0,3},{1,0},{2,1},{3,2},{4,7},{5,4},{6,5},{7,6},{8,11},{9,8},{10,9... | collective-permute-start | bytes 393224 | tf_op jit(solution)/shard_map/ppermute | solution.py:469
  100.3 21.8 %copy-start.7 = (bf16[1,4,4,4096]{3,2,1,0:T(4,128)(2,1)S(1)}, bf16[1,4,4,4096]{3,2,1,0:T(4,128)(2,1)}, u32[]{:S(2)}) copy-start(bf16[1,4,4,4096]{3,2,1,0:T(4,128)(2,1)} %spectral.3) | copy-start | bytes 393220
  100.3 2.9 %collective-permute-start.16 = (f32[64,1024]{1,0:T(8,128)S(1)}, f32[64,1024]{1,0:T(8,128)S(1)}, u32[]{:S(2)}, u32[]{:S(2)}) collective-permute-start(f32[64,1024]{1,0:T(8,128)S(1)} %get-tuple-element.87), channel_id=1, source_target_pairs={{0,4},{4,0},{8,12},{12,8},{1,5},{5,1},{9,13},{13,9},{2,6},{6,2},{1... | collective-permute-start | bytes 786440 | tf_op jit(solution)/shard_map/ppermute | solution.py:469
  103.2 4.8 %collective-permute-start.17 = (f32[32,1024]{1,0:T(8,128)S(1)}, f32[32,1024]{1,0:T(8,128)S(1)}, u32[]{:S(2)}, u32[]{:S(2)}) collective-permute-start(f32[32,1024]{1,0:T(8,128)S(1)} %get-tuple-element.89), channel_id=1, source_target_pairs={{0,8},{4,12},{8,0},{12,4},{1,9},{5,13},{9,1},{13,5},{2,10},{6,14},... | collective-permute-start | bytes 393224 | tf_op jit(solution)/shard_map/ppermute | solution.py:469
  135.2 2.8 %collective-permute-start.18 = (f32[32,256]{1,0:T(8,128)S(1)}, f32[32,256]{1,0:T(8,128)S(1)}, u32[]{:S(2)}, u32[]{:S(2)}) collective-permute-start(f32[32,256]{1,0:T(8,128)S(1)} %get-tuple-element.91.a), channel_id=1, source_target_pairs={{0,8},{4,12},{8,0},{12,4},{1,9},{5,13},{9,1},{13,5},{2,10},{6,14},... | collective-permute-start | bytes 98312 | tf_op jit(solution)/shard_map/ppermute | solution.py:469
  138.0 5.0 %collective-permute-start.19 = (f32[64,256]{1,0:T(8,128)S(1)}, f32[64,256]{1,0:T(8,128)S(1)}, u32[]{:S(2)}, u32[]{:S(2)}) collective-permute-start(f32[64,256]{1,0:T(8,128)S(1)} %shard_map.163.a), channel_id=1, source_target_pairs={{0,4},{4,0},{8,12},{12,8},{1,5},{5,1},{9,13},{13,9},{2,6},{6,2},{1... | collective-permute-start | bytes 196616 | tf_op jit(solution)/shard_map/ppermute | solution.py:469
  143.2 5.5 %collective-permute-start.20 = (f32[160,256]{1,0:T(8,128)S(1)}, f32[160,256]{1,0:T(8,128)S(1)}, u32[]{:S(2)}, u32[]{:S(2)}) collective-permute-start(f32[160,256]{1,0:T(8,128)S(1)} %shard_map.164.a), channel_id=1, source_target_pairs={{0,3},{1,0},{2,1},{3,2},{4,7},{5,4},{6,5},{7,6},{8,11},{9,8},{10,9... | collective-permute-start | bytes 491528 | tf_op jit(solution)/shard_map/ppermute | solution.py:469
  145.2 6.7 %collective-permute-start.21 = (f32[160,256]{1,0:T(8,128)S(1)}, f32[160,256]{1,0:T(8,128)S(1)}, u32[]{:S(2)}, u32[]{:S(2)}) collective-permute-start(f32[160,256]{1,0:T(8,128)S(1)} %shard_map.164.a), channel_id=1, source_target_pairs={{0,2},{1,3},{2,0},{3,1},{4,6},{5,7},{6,4},{7,5},{8,10},{9,11},{10,... | collective-permute-start | bytes 491528 | tf_op jit(solution)/shard_map/ppermute | solution.py:469
  145.5 10.8 %collective-permute-start.22 = (f32[160,256]{1,0:T(8,128)S(1)}, f32[160,256]{1,0:T(8,128)S(1)}, u32[]{:S(2)}, u32[]{:S(2)}) collective-permute-start(f32[160,256]{1,0:T(8,128)S(1)} %shard_map.164.a), channel_id=1, source_target_pairs={{0,1},{1,2},{2,3},{3,0},{4,5},{5,6},{6,7},{7,4},{8,9},{9,10},{10,1... | collective-permute-start | bytes 491528 | tf_op jit(solution)/shard_map/ppermute | solution.py:469

commit v2 on v1

--- a/solution.py
+++ b/solution.py
@@ -54,7 +54,7 @@
         small = cas(np.arange(16)[:, None], CELLS_X * DEV_X, x * DEV_X + d)
         for l in range(4):
             tx[d, :, l, :, l] = small
-    tx = tx.reshape(DEV_X, 64, CELLS_X * 4)
+    tx = tx.reshape(DEV_X, 64, CELLS_X * 4).transpose(0, 2, 1)
     return tuple(t.astype(bf16) for t in (tz, ty, tx))
 
 
@@ -96,7 +96,8 @@
 def call(body, outs, *args, scratch=(), limit=8, raw=0):
     near = args[1 : 1 + raw]
     rest = args[1 + raw :]
-    shapes = [pltpu.VMEM(*o[:2]) if len(o) == 2 else jax.ShapeDtypeStruct(*o[:2]) for o in outs]
+    shapes = [pltpu.VMEM(*o) if len(o) == 2 else jax.ShapeDtypeStruct(*o[:2]) for o in outs]
+    shapes = [pltpu.HBM(*o[:2]) if "raw" in o else v for o, v in zip(outs, shapes)]
     if INTERPRET:
         shapes = [jax.ShapeDtypeStruct(*o[:2]) for o in outs]
     else:
@@ -131,7 +132,7 @@
 
 
 def block(b):
-    return pl.ds(pl.multiple_of(b * 256, 256), 256)
+    return slice(b * 256, (b + 1) * 256)
 
 
 def store_parts(v, refs):
@@ -143,14 +144,13 @@
     lane = lax.broadcasted_iota(jnp.int32, (C, wide), 1) & (C - 1)
     row = lax.broadcasted_iota(jnp.int32, (C, wide), 0)
     eye = jnp.where(lane == row, 1.0, 0.0)
-    for q in range(4):
-        z = b * 4 + q
-        here = pl.ds(pl.multiple_of(z * C, C), C) if wide > 256 else slice(q * C, (q + 1) * C)
-        ka[here, :] = (eye * mine[pl.ds(z, 1), :wide]).astype(bf16)
+    for z in range(4 * b, 4 * b + 4):
+        ka[z * C : (z + 1) * C, :] = (eye * mine[z : z + 1, :wide]).astype(bf16)
 
 
 def start_kernel(
-    at, pre_from, grad_from, tz, dz_to, p1, p2, p3, mine_out, ka, total, pre, grad, dz, short, mine, sems
+    at, pre_from, grad_from, tz, dz_to, p1, p2, p3, mine,
+    ka, total, pre, grad, dz, short, sems,
 ):
     def copies(b):
         cut = block(b)
@@ -169,29 +169,31 @@
             copy.start()
     first.wait()
     mine[...] = short[...].astype(f32)
-    mine_out[...] = mine[...]
-
-    def fill(b):
-        fill_table(ka, mine, b)
-        for copy in copies(b):
-            copy.wait()
-        cut = block(b)
-        v = pre[:, cut].astype(f32)
-        dz[:, cut] = (grad[:, cut].astype(f32) * slope_of(v, cdf_of(v))).astype(bf16)
-
-    def step(b, _):
-        fill(b)
-        leave(b - 1).start()
-        total[...] += dot(dz[:, block(b - 1)], ka[block(b - 1), 256:])
-        return 0
-
     total[...] = jnp.zeros_like(total)
-    fill(0)
-    lax.fori_loop(1, 8, step, 0)
-    leave(7).start()
-    store_parts(total[...] + dot(dz[:, 7 * 256 :], ka[7 * 256 :, 256:]), (p1, p2, p3))
+    for b in range(9):
+        if b < 8:
+            fill_table(ka, mine, b)
+            for copy in copies(b):
+                copy.wait()
+            v = pre[:, block(b)].astype(f32)
+            slope = slope_of(v, cdf_of(v))
+            dz[:, block(b)] = (grad[:, block(b)].astype(f32) * slope).astype(bf16)
+            leave(b).start()
+        if b > 0:
+            total[...] += dot(dz[:, block(b - 1)], ka[block(b - 1), 256:])
+    store_parts(total[...], (p1, p2, p3))
     for b in range(8):
         leave(b).wait()
+
+
+def own_kernel(at, mine, dz, p0, fold, ka):
+    for b in range(8):
+        fill_table(ka, mine, b, 256)
+    p0[...] = dot(dz[...], ka[...])
+    row = lax.broadcasted_iota(jnp.int32, (256, C), 0) >> 6
+    lane = lax.broadcasted_iota(jnp.int32, (256, C), 1)
+    for r in range(16):
+        fold[r * 256 : (r + 1) * 256, :] = jnp.where(lane == row + 4 * r, 1.0, 0.0).astype(bf16)
 
 
 def fill_point(square, point):
@@ -205,8 +207,8 @@
 
 
 def side_kernel(
-    at, pre, first, dz, mine, point, slope_to, local_to, weight, p0, q0, q1, q2, q3,
-    ka, total, own, squares, square, slope, local, sems,
+    at, pre, first, dz, mine, point, slope_to, local_to, weight, q0, q1, q2, q3,
+    ka, mid, own, squares, square, slope, local, sems,
 ):
     fill_point(square, point)
 
@@ -217,62 +219,53 @@
             pltpu.make_async_copy(local.at[:, cut], local_to.at[:, cut], sems.at[8 + b]),
         )
 
-    def fill(b):
-        fill_table(ka, mine, b)
-        cut = block(b)
-        v = pre[:, cut].astype(f32)
-        cdf = cdf_of(v)
-        slope[:, cut] = slope_of(v, cdf)
-        total[b, :ROWS] = (v * cdf).astype(bf16)
-        total[b, ROWS:] = first[:, cut]
-
-    def step(b, _):
-        cut = block(b)
-        fill(b)
-        here = dz[:, cut]
-        local[:, cut] = dot_nt(here, square[...])
-        for copy in leave(b):
-            copy.start()
-        squares[...] += dot_tn(total[b, :ROWS], here)
-        own[: 2 * ROWS] += dot(total[b], ka[cut, :])
-        own[2 * ROWS :, :256] += dot(here, ka[cut, :256])
-        return 0
-
     own[...] = jnp.zeros_like(own)
     squares[...] = jnp.zeros_like(squares)
-    lax.fori_loop(0, 8, step, 0)
+    for b in range(9):
+        if b < 8:
+            cut = block(b)
+            fill_table(ka, mine, b)
+            v = pre[:, cut].astype(f32)
+            cdf = cdf_of(v)
+            slope[:, cut] = slope_of(v, cdf)
+            mid[:ROWS, cut] = (v * cdf).astype(bf16)
+            mid[ROWS:, cut] = first[:, cut]
+            local[:, cut] = dot_nt(dz[:, cut], square[...])
+            for copy in leave(b):
+                copy.start()
+        if b > 0:
+            cut = block(b - 1)
+            squares[...] += dot_tn(mid[:ROWS, cut], dz[:, cut])
+            own[...] += dot(mid[:, cut], ka[cut, :])
     weight[...] = diagonal_sum(squares[...])
-    p0[...] = own[2 * ROWS :, :256]
     for j, ref in enumerate((q0, q1, q2, q3)):
         ref[:, :256] = own[:ROWS, j * 256 : (j + 1) * 256]
-        ref[:, 256:] = own[ROWS : 2 * ROWS, j * 256 : (j + 1) * 256]
+        ref[:, 256:] = own[ROWS:, j * 256 : (j + 1) * 256]
     for b in range(8):
         for copy in leave(b):
             copy.wait()
 
 
-def side_one_kernel(
-    at, first, dz, mine, point, weight_two, local_to, sent, p0, ka, squares, square, local, sems
-):
+def side_one_kernel(at, first, dz, mine, weight_two, sent, p0, ka):
+    for b in range(8):
+        fill_table(ka, mine, b, 256)
+    squares = dot_tn(first[:, :256], dz[:, :256])
+    for b in range(1, 8):
+        squares = squares + dot_tn(first[:, block(b)], dz[:, block(b)])
+    p0[...] = dot(dz[...], ka[...])
+    both = jnp.concatenate([weight_two[...], diagonal_sum(squares)], axis=1) * SCALE_B
+    sent[...] = jnp.concatenate([both[:32], both[32:]], axis=1)
+
+
+def local_kernel(at, dz, point, local_to, square, local, sems):
     fill_point(square, point)
 
     def leave(b):
-        cut = block(b)
-        return pltpu.make_async_copy(local.at[:, cut], local_to.at[:, cut], sems.at[b])
-
-    def step(b, total):
-        cut = block(b)
-        here = dz[:, cut]
-        local[:, cut] = dot_nt(here, square[...])
+        return pltpu.make_async_copy(local.at[:, block(b)], local_to.at[:, block(b)], sems.at[b])
+
+    for b in range(8):
+        local[:, block(b)] = dot_nt(dz[:, block(b)], square[...])
         leave(b).start()
-        squares[...] += dot_tn(first[:, cut], here)
-        fill_table(ka, mine, b, 256)
-        return total + dot(here, ka[...])
-
-    squares[...] = jnp.zeros_like(squares)
-    p0[...] = lax.fori_loop(0, 8, step, jnp.zeros((ROWS, 256), f32))
-    both = jnp.concatenate([weight_two[...], diagonal_sum(squares[...])], axis=1) * SCALE_B
-    sent[...] = jnp.concatenate([both[:32], both[32:]], axis=1)
     for b in range(8):
         leave(b).wait()
 
@@ -312,7 +305,7 @@
 
 def along_x_kernel(at, a, b, tx, out):
     v = a[...] + b[...]
-    modes = table_dot(tx[at_x(at)], v[:, : min(v.shape[1], 768)])
+    modes = table_dot_tn(tx[at_x(at)], v[:, : min(v.shape[1], 768)])
     for i in range(16):
         out[i, :, : modes.shape[1]] = modes[i * 4 : (i + 1) * 4]
     if v.shape[1] > 768:
@@ -382,12 +375,12 @@
 
 def back_x_kernel(at, got, tx, out):
     v = jnp.concatenate([got[i] for i in range(16)], axis=0)
-    out[...] = table_dot_tn(tx[at_x(at)], v)
+    out[...] = table_dot(tx[at_x(at)], v)
 
 
 def back_x_one_kernel(at, got, tx, out, weight):
     v = jnp.concatenate([got[i] for i in range(16)], axis=0)
-    out[...] = table_dot_tn(tx[at_x(at)], v[:, :256])
+    out[...] = table_dot(tx[at_x(at)], v[:, :256])
     weight[...] = jnp.concatenate([v[:32, 256:], v[32:, 256:]], axis=1)
 
 
@@ -408,50 +401,62 @@
 
 
 def middle_kernel(
-    at, a, b, c, d, mine, local, slope, dz_to, p1, p2, p3, modes, total, dz, ka, sems
+    at, local_from, slope_from, a, b, c, d, mine, dz_to, p1, p2, p3,
+    modes, total, dz, ka, local, slope, sems,
 ):
+    def copies(i):
+        cut = block(i)
+        return (
+            pltpu.make_async_copy(local_from.at[:, cut], local.at[:, cut], sems.at[i]),
+            pltpu.make_async_copy(slope_from.at[:, cut], slope.at[:, cut], sems.at[8 + i]),
+        )
+
+    def leave(i):
+        return pltpu.make_async_copy(dz.at[:, block(i)], dz_to.at[:, block(i)], sems.at[16 + i])
+
+    for i in range(8):
+        for copy in copies(i):
+            copy.start()
     stack_modes((a, b, c, d), modes)
-
-    def leave(i):
-        return pltpu.make_async_copy(dz.at[:, block(i)], dz_to.at[:, block(i)], sems.at[i])
-
-    def fill(i):
-        cut = block(i)
-        fill_table(ka, mine, i)
-        down = dot_nt(modes[...], ka[cut, :]) + local[:, cut]
-        dz[:, cut] = (down * slope[:, cut]).astype(bf16)
-
-    def step(i, _):
-        fill(i)
-        leave(i - 1).start()
-        total[...] += dot(dz[:, block(i - 1)], ka[block(i - 1), 256:])
-        return 0
-
     total[...] = jnp.zeros_like(total)
-    fill(0)
-    lax.fori_loop(1, 8, step, 0)
-    leave(7).start()
-    store_parts(total[...] + dot(dz[:, 7 * 256 :], ka[7 * 256 :, 256:]), (p1, p2, p3))
+    fill_table(ka, mine, 0)
+    for i in range(9):
+        if i < 8:
+            if i < 7:
+                fill_table(ka, mine, i + 1)
+            for copy in copies(i):
+                copy.wait()
+            down = dot_nt(modes[...], ka[block(i), :]) + local[:, block(i)]
+            dz[:, block(i)] = (down * slope[:, block(i)]).astype(bf16)
+            leave(i).start()
+        if i > 0:
+            total[...] += dot(dz[:, block(i - 1)], ka[block(i - 1), 256:])
+    store_parts(total[...], (p1, p2, p3))
     for i in range(8):
         leave(i).wait()
 
 
 def end_kernel(
-    at, a, b, c, d, mine, local, out_to, weight_two, weight_one, modes, out, ka, sems
+    at, local_from, a, b, c, d, mine, out_to, weight_two, weight_one,
+    modes, out, ka, local, sems,
 ):
+    def copy(i):
+        return pltpu.make_async_copy(local_from.at[:, block(i)], local.at[:, block(i)], sems.at[i])
+
+    def leave(i):
+        return pltpu.make_async_copy(out.at[:, block(i)], out_to.at[:, block(i)], sems.at[8 + i])
+
+    for i in range(8):
+        copy(i).start()
     stack_modes((a, b, c, d), modes)
-
-    def leave(i):
-        return pltpu.make_async_copy(out.at[:, block(i)], out_to.at[:, block(i)], sems.at[i])
-
-    def step(i, _):
-        cut = block(i)
-        fill_table(ka, mine, i)
-        out[:, cut] = (dot_nt(modes[...], ka[cut, :]) + local[:, cut]).astype(bf16)
+    fill_table(ka, mine, 0)
+    for i in range(8):
+        if i < 7:
+            fill_table(ka, mine, i + 1)
+        copy(i).wait()
+        down = dot_nt(modes[...], ka[block(i), :]) + local[:, block(i)]
+        out[:, block(i)] = down.astype(bf16)
         leave(i).start()
-        return 0
-
-    lax.fori_loop(0, 8, step, 0)
     w = (a[ROWS:] + b[ROWS:]) + (c[ROWS:] + d[ROWS:])
     w = jnp.concatenate([w[:, :128], w[:, 128:]], axis=0)
     weight_two[...] = w[:, :C]
@@ -497,8 +502,6 @@
     grid_input, pre_one, pre_two, grad_output, spectral_one, spectral_two, point_one, point_two
 ):
     tz, ty, tx = [jnp.asarray(t) for t in build_tables()]
-    row = lax.broadcasted_iota(jnp.int32, (C * C, C), 0)
-    fold = (row // C == lax.broadcasted_iota(jnp.int32, (C * C, C), 1)).astype(bf16)
     at = lax.axis_index(("gz", "gy", "gx")).reshape(1)
     first, pre_one, pre_two, upstream = [
         t.reshape(ROWS, WIDE) for t in (grid_input, pre_one, pre_two, grad_output)
@@ -524,24 +527,36 @@
             (big, bf16),
             (big, bf16),
             ((CELLS_Z, 16 * C), bf16),
-            ((CELLS_Z, 16 * C), f32),
             dma((25,)),
         ],
     )
-    slope, local_two, weight_two, own, *ins = call(
+    own, fold = call(
+        own_kernel,
+        [half, ((C * C, C), bf16)],
+        at,
+        mine,
+        dz_two,
+        scratch=[((WIDE, 256), bf16)],
+    )
+    got = exchange([own] + parts, "gx")
+    near, far = call(along_y_kernel, [((64, 256), f32)] * 2, at, *got, ty)
+    got = reduce_y(at, near, far, 256)
+    (modes,) = call(along_x_kernel, [((16, 4, 256), f32)], at, *got, tx)
+    modes, pre_one, dz_side = lax.optimization_barrier((modes, pre_one, dz_two))
+    slope, local_two, weight_two, *ins = call(
         side_kernel,
-        [(big, f32, "raw")] * 2 + [((C, C), f32, 0), half] + [((ROWS, 512), f32)] * 4,
+        [(big, f32, "raw")] * 2 + [((C, C), f32, 0)] + [((ROWS, 512), f32)] * 4,
         at,
         pre_one,
         first,
-        dz_two,
+        dz_side,
         mine,
         point_two,
         limit=14,
         scratch=[
             table,
-            ((8, 2 * ROWS, 256), bf16),
-            ((3 * ROWS, 16 * C), f32),
+            ((2 * ROWS, WIDE), bf16),
+            ((2 * ROWS, 16 * C), f32),
             ((256, 256), f32),
             ((256, 256), bf16),
             (big, f32),
@@ -549,13 +564,9 @@
             dma((16,)),
         ],
     )
-    got = exchange([own] + parts, "gx")
-    near, far = call(along_y_kernel, [((64, 256), f32)] * 2, at, *got, ty)
-    got = reduce_y(at, near, far, 256)
-    (modes,) = call(along_x_kernel, [((16, 4, 256), f32)], at, *got, tx)
+    got = over_x(modes)
+    got, ins = lax.optimization_barrier((got, ins))
     got_in = exchange(ins, "gx")
-    modes, got_in[0] = lax.optimization_barrier((modes, got_in[0]))
-    got = over_x(modes)
     back, hat_two = call(
         mix_two_kernel,
         [((16, 4, 256), f32), ((4, 256), f32)],
@@ -576,28 +587,31 @@
         middle_kernel,
         [(big, bf16, "raw")] + [half] * 3,
         at,
+        local_two,
+        slope,
         *got,
         mine,
-        local_two,
-        slope,
-        scratch=[((ROWS, 16 * C), bf16), ((ROWS, 12 * C), f32), (big, bf16), table, dma((8,))],
-    )
-    local_one, sent, own = call(
+        raw=2,
+        limit=12,
+        scratch=[
+            ((ROWS, 16 * C), bf16),
+            ((ROWS, 12 * C), f32),
+            (big, bf16),
+            table,
+            (big, f32),
+            (big, f32),
+            dma((24,)),
+        ],
+    )
+    sent, own = call(
         side_one_kernel,
-        [(big, f32, "raw"), ((32, 256), f32), half],
+        [((32, 256), f32), half],
         at,
         first,
         dz_one,
         mine,
-        point_one,
         weight_two,
-        scratch=[
-            ((256, 256), bf16),
-            ((256, 256), f32),
-            ((256, 256), bf16),
-            (big, f32),
-            dma((8,)),
-        ],
+        scratch=[((WIDE, 256), bf16)],
     )
     got = exchange([own] + parts, "gx")
     near, far = call(along_y_join_kernel, [((64, 1024), f32)] * 2, at, *got, ty, *ins, sent)
@@ -614,7 +628,18 @@
     )
     (spec_two,) = call(outer_kernel, [(*native, 0)], at, mid_hat, hat_two, fold)
     (spec_one,) = call(outer_kernel, [(*native, 0)], at, first_hat, hat_one, fold)
-    tall, weight = call(back_x_one_kernel, [((32, 256), f32)] * 2, at, over_x(back), tx)
+    back, dz_late = lax.optimization_barrier((back, dz_one))
+    (local_one,) = call(
+        local_kernel,
+        [(big, f32, "raw")],
+        at,
+        dz_late,
+        point_one,
+        scratch=[((256, 256), bf16), (big, f32), dma((8,))],
+    )
+    got = over_x(back)
+    got, local_one = lax.optimization_barrier((got, local_one))
+    tall, weight = call(back_x_one_kernel, [((32, 256), f32)] * 2, at, got, tx)
     got = spread_y(at, tall)
     (tall,) = call(back_y_one_kernel, [((ROWS + 32, 256), f32)], at, *got, ty, weight)
     got = spread(tall, "gx")
@@ -622,10 +647,11 @@
         end_kernel,
         [(big, bf16, "raw"), ((C, C), f32, 0), ((C, C), f32, 0)],
         at,
+        local_one,
         *got,
         mine,
-        local_one,
-        scratch=[((ROWS, 16 * C), bf16), (big, bf16), table, dma((8,))],
+        raw=1,
+        scratch=[((ROWS, 16 * C), bf16), (big, bf16), table, (big, f32), dma((16,))],
     )
     return (
         input_grad.reshape(CELLS_X, CELLS_Y, WIDE),

time: 162 us -> 158 us (0.975)
  Pallas kernels: 34.4 us -> 26.1 us
  waiting for transfers between devices: 45 us -> 48.6 us
  other arithmetic: 3.38 us -> 0 us
  starting transfers between devices: 47.9 us -> 50.9 us
    pallas_call x22 -> x24, Pallas kernels: 34.4 us -> 26.1 us  [call(): pl.pallas_call(body, out_shape=shapes, in_specs=[pl.BlockSpec(memory_spac...]
    ppermute x23, waiting for transfers between devices: 30.4 us -> 36.2 us  [shifted(): return lax.ppermute(v, axis, pairs)]
    convert_element_type x1 -> x0, other arithmetic: 3.37 us -> none  [on_device(): (row // C == lax.broadcasted_iota(jnp.int32, (C * C, C), 1)).astype(bf16)]
    all_to_all x2, waiting for transfers between devices: 14.6 us -> 12.5 us  [over_x(): return lax.all_to_all(v, 'gz', 0, 0, tiled=True)]
    ppermute x23, starting transfers between devices: 35 us -> 36.8 us  [shifted(): return lax.ppermute(v, axis, pairs)]
  transfers between devices with their start and end apart: 25 -> 25, of which waited for: 16 -> 18; matrix products, arithmetic and copies ran while one was open for 2% -> 0% of each run, Pallas kernels for 11% -> 5%
where the time goes in v2:
time: 158 us; the launch traced here: 157 us
  starting transfers between devices  50.9 us (32%)
  waiting for transfers between devices  48.6 us (31%)
  blocking collectives  27.5 us (17%)
  Pallas kernels  26.1 us (17%)
  local copies, waits for them, and re-layouts  3.19 us (2%)
    ppermute x23, starting transfers between devices, shifted(): return lax.ppermute(v, axis, pairs)  36.8 us
    ppermute x23, waiting for transfers between devices, shifted(): return lax.ppermute(v, axis, pairs)  36.2 us
    all_to_all x2, blocking collectives, over_x(): return lax.all_to_all(v, 'gz', 0, 0, tiled=True)  27.5 us
    pallas_call x24, Pallas kernels, call(): pl.pallas_call(body, out_shape=shapes, in_specs=[pl.BlockSpec(memory_spac...  26.1 us
    all_to_all x2, starting transfers between devices, over_x(): return lax.all_to_all(v, 'gz', 0, 0, tiled=True)  14.2 us
    all_to_all x2, waiting for transfers between devices, over_x(): return lax.all_to_all(v, 'gz', 0, 0, tiled=True)  12.5 us
    unnamed x28, local copies, waits for them, and re-layouts  3.19 us
  transfers between devices with their start and end apart: 25, of which 18 were waited for; matrix products, arithmetic and copies ran while one was open for 0% of the time, Pallas kernels for 5%

profile of v2, /device:TPU:1, one launch (start us, length us, event | category | flops | bytes accessed | tf_op | source)
XLA Modules:
  0.0 157.4 jit_solution(3245595761121834895)
XLA Ops:
  0.7 3.2 %shard_map.146 = (bf16[128,2048]{1,0:T(8,128)(2,1)}, f32[128,256]{1,0:T(8,128)S(1)}, f32[128,256]{1,0:T(8,128)S(1)}, f32[128,256]{1,0:T(8,128)S(1)}, f32[32,1024]{1,0:T(8,128)S(1)}) custom-call(s32[1]{0:T(128)} %bitcast.at, bf16[128,2048]{1,0:T(8,128)(2,1)} %bitcast.11, bf16[128,2048]{1,0:T(8,128)(2,1)} %bitcast.12, bf16[4,32,1024]{2,1,0:T(8,128)(2,1)} %constant.22.clone.tz), custom_call_target="tpu_custom_call" | custom-call | tf_op jit(solution)/shard_map/pallas_call | solution.py:106
  3.8 2.2 %collective-permute-start = (f32[128,256]{1,0:T(8,128)S(1)}, f32[128,256]{1,0:T(8,128)S(1)}, u32[]{:S(2)}, u32[]{:S(2)}) collective-permute-start(f32[128,256]{1,0:T(8,128)S(1)} %get-tuple-element.66), channel_id=1, source_target_pairs={{0,1},{1,2},{2,3},{3,0},{4,5},{5,6},{6,7},{7,4},{8,9},{9,10},{10,1... | collective-permute-start | bytes 393224 | tf_op jit(solution)/shard_map/ppermute | solution.py:474
  6.0 2.6 %collective-permute-start.1 = (f32[128,256]{1,0:T(8,128)S(1)}, f32[128,256]{1,0:T(8,128)S(1)}, u32[]{:S(2)}, u32[]{:S(2)}) collective-permute-start(f32[128,256]{1,0:T(8,128)S(1)} %get-tuple-element.67), channel_id=1, source_target_pairs={{0,2},{1,3},{2,0},{3,1},{4,6},{5,7},{6,4},{7,5},{8,10},{9,11},{10,... | collective-permute-start | bytes 393224 | tf_op jit(solution)/shard_map/ppermute | solution.py:474
  8.7 1.1 collective-permute-start.2
  9.7 1.0 copy-done.3
  11.5 2.9 %collective-permute-done.1.c = f32[128,256]{1,0:T(8,128)S(1)} collective-permute-done((f32[128,256]{1,0:T(8,128)S(1)}, f32[128,256]{1,0:T(8,128)S(1)}, u32[]{:S(2)}, u32[]{:S(2)}) %collective-permute-start.1) | collective-permute-done | bytes 131104 | tf_op jit(solution)/shard_map/ppermute | solution.py:474
  14.6 1.8 %collective-permute-start.3 = (f32[64,256]{1,0:T(8,128)S(1)}, f32[64,256]{1,0:T(8,128)S(1)}, u32[]{:S(2)}, u32[]{:S(2)}) collective-permute-start(f32[64,256]{1,0:T(8,128)S(1)} %get-tuple-element.70), channel_id=1, source_target_pairs={{0,4},{4,0},{8,12},{12,8},{1,5},{5,1},{9,13},{13,9},{2,6},{6,2},{1... | collective-permute-start | bytes 196616 | tf_op jit(solution)/shard_map/ppermute | solution.py:474
  16.4 0.9 collective-permute-done.3.got
  17.4 1.5 collective-permute-start.4
  18.9 1.3 collective-permute-done.4.b
  21.0 10.5 %all-to-all-start = ((f32[16,4,256]{2,1,0:T(4,128)}), f32[16,4,256]{2,1,0:T(4,128)S(1)}, u32[]{:S(2)}, u32[]{:S(2)}) async-start(f32[16,4,256]{2,1,0:T(4,128)} %shard_map.150), calls=%async_computation | async-start | bytes 131072 | tf_op jit(solution)/shard_map/all_to_all | solution.py:498
  31.6 2.4 %shard_map.151 = (f32[128,2048]{1,0:T(8,128)}, f32[128,2048]{1,0:T(8,128)}, f32[64,64]{1,0:T(8,128)S(1)}, f32[128,512]{1,0:T(8,128)S(1)}, f32[128,512]{1,0:T(8,1...) custom-call(s32[1]{0:T(128)} %bitcast.at, bf16[128,2048]{1,0:T(8,128)(2,1)S(1)} %bitcast.10, ...), custom_call_target="tpu_custom_call" | custom-call | tf_op jit(solution)/shard_map/pallas_call | solution.py:106
  36.2 4.4 %all-to-all-done.got = f32[16,4,256]{2,1,0:T(4,128)S(1)} async-done(((f32[16,4,256]{2,1,0:T(4,128)}), f32[16,4,256]{2,1,0:T(4,128)S(1)}, u32[]{:S(2)}, u32[]{:S(2)}) %all-to-all-start) | async-done | bytes 65568 | tf_op jit(solution)/shard_map/all_to_all | solution.py:498
  40.6 0.9 collective-permute-start.5
  41.6 2.1 %collective-permute-start.6 = (f32[128,512]{1,0:T(8,128)}, f32[128,512]{1,0:T(8,128)S(1)}, u32[]{:S(2)}, u32[]{:S(2)}) collective-permute-start(f32[128,512]{1,0:T(8,128)} %copy-done.12), channel_id=1, source_target_pairs={{0,2},{1,3},{2,0},{3,1},{4,6},{5,7},{6,4},{7,5},{8,10},{9,11},{10,... | collective-permute-start | bytes 786440 | tf_op jit(solution)/shard_map/ppermute | solution.py:474
  43.7 1.3 collective-permute-start.7
  45.4 13.4 %all_to_all.20.got = f32[16,4,256]{2,1,0:T(4,128)S(1)} all-to-all(f32[16,4,256]{2,1,0:T(4,128)S(1)} %get-tuple-element.84), channel_id=1, replica_groups=mesh['gz'=16,'gy'=4,'gx'=4] {'gz'}, dimensions={0} | all-to-all | bytes 131072 | tf_op jit(solution)/shard_map/all_to_all | solution.py:498
  59.8 2.3 %collective-permute-done.8.b = f32[32,256]{1,0:T(8,128)S(1)} collective-permute-done((f32[32,256]{1,0:T(8,128)S(1)}, f32[32,256]{1,0:T(8,128)S(1)}, u32[]{:S(2)}, u32[]{:S(2)}) %collective-permute-start.8) | collective-permute-done | bytes 32800 | tf_op jit(solution)/shard_map/ppermute | solution.py:474
  62.1 5.4 %collective-permute-start.9 = (f32[64,256]{1,0:T(8,128)S(1)}, f32[64,256]{1,0:T(8,128)S(1)}, u32[]{:S(2)}, u32[]{:S(2)}) collective-permute-start(f32[64,256]{1,0:T(8,128)S(1)} %shard_map.154.a), channel_id=1, source_target_pairs={{0,4},{4,0},{8,12},{12,8},{1,5},{5,1},{9,13},{13,9},{2,6},{6,2},{1... | collective-permute-start | bytes 196616 | tf_op jit(solution)/shard_map/ppermute | solution.py:474
  67.5 0.9 collective-permute-done.9.b
  68.9 1.8 %collective-permute-start.11 = (f32[128,256]{1,0:T(8,128)S(1)}, f32[128,256]{1,0:T(8,128)S(1)}, u32[]{:S(2)}, u32[]{:S(2)}) collective-permute-start(f32[128,256]{1,0:T(8,128)S(1)} %shard_map.155.a), channel_id=1, source_target_pairs={{0,2},{1,3},{2,0},{3,1},{4,6},{5,7},{6,4},{7,5},{8,10},{9,11},{10,... | collective-permute-start | bytes 393224 | tf_op jit(solution)/shard_map/ppermute | solution.py:474
  70.7 2.9 %collective-permute-done.10.b = f32[128,256]{1,0:T(8,128)S(1)} collective-permute-done((f32[128,256]{1,0:T(8,128)S(1)}, f32[128,256]{1,0:T(8,128)S(1)}, u32[]{:S(2)}, u32[]{:S(2)}) %collective-permute-start.10) | collective-permute-done | bytes 131104 | tf_op jit(solution)/shard_map/ppermute | solution.py:474
  73.6 1.6 %collective-permute-done.11.c = f32[128,256]{1,0:T(8,128)S(1)} collective-permute-done((f32[128,256]{1,0:T(8,128)S(1)}, f32[128,256]{1,0:T(8,128)S(1)}, u32[]{:S(2)}, u32[]{:S(2)}) %collective-permute-start.11) | collective-permute-done | bytes 131104 | tf_op jit(solution)/shard_map/ppermute | solution.py:474
  75.2 3.2 %collective-permute-done.12.d = f32[128,256]{1,0:T(8,128)S(1)} collective-permute-done((f32[128,256]{1,0:T(8,128)S(1)}, f32[128,256]{1,0:T(8,128)S(1)}, u32[]{:S(2)}, u32[]{:S(2)}) %collective-permute-start.12) | collective-permute-done | bytes 131104 | tf_op jit(solution)/shard_map/ppermute | solution.py:474
  78.4 5.4 %shard_map.156 = (bf16[128,2048]{1,0:T(8,128)(2,1)}, f32[128,256]{1,0:T(8,128)S(1)}, f32[128,256]{1,0:T(8,128)S(1)}, f32[128,256]{1,0:T(8,128)S(1)}) custom-call(s32[1]{0:T(128)} %bitcast.at, f32[128,2048]{1,0:T(8,128)} %get-tuple-element.75.local_from, f32[128,2048]{1,0:T(8,128)} %get-tuple-element.76.slope_from, f32[128,256]{1,0:T(8,128)S(1)} %shard_map.155.a, ...), custom_call_target="tpu_custom_call" | custom-call | tf_op jit(solution)/shard_map/pallas_call | solution.py:106
  84.0 1.6 %collective-permute-start.14 = (f32[128,256]{1,0:T(8,128)S(1)}, f32[128,256]{1,0:T(8,128)S(1)}, u32[]{:S(2)}, u32[]{:S(2)}) collective-permute-start(f32[128,256]{1,0:T(8,128)S(1)} %get-tuple-element.94), channel_id=1, source_target_pairs={{0,2},{1,3},{2,0},{3,1},{4,6},{5,7},{6,4},{7,5},{8,10},{9,11},{10,... | collective-permute-start | bytes 393224 | tf_op jit(solution)/shard_map/ppermute | solution.py:474
  85.6 2.0 %collective-permute-start.15 = (f32[128,256]{1,0:T(8,128)S(1)}, f32[128,256]{1,0:T(8,128)S(1)}, u32[]{:S(2)}, u32[]{:S(2)}) collective-permute-start(f32[128,256]{1,0:T(8,128)S(1)} %get-tuple-element.95), channel_id=1, source_target_pairs={{0,3},{1,0},{2,1},{3,2},{4,7},{5,4},{6,5},{7,6},{8,11},{9,8},{10,9... | collective-permute-start | bytes 393224 | tf_op jit(solution)/shard_map/ppermute | solution.py:474
  88.6 4.2 %collective-permute-done.13.b = f32[128,256]{1,0:T(8,128)S(1)} collective-permute-done((f32[128,256]{1,0:T(8,128)S(1)}, f32[128,256]{1,0:T(8,128)S(1)}, u32[]{:S(2)}, u32[]{:S(2)}) %collective-permute-start.13) | collective-permute-done | bytes 131104 | tf_op jit(solution)/shard_map/ppermute | solution.py:474
  93.0 1.8 %collective-permute-start.16 = (f32[64,1024]{1,0:T(8,128)S(1)}, f32[64,1024]{1,0:T(8,128)S(1)}, u32[]{:S(2)}, u32[]{:S(2)}) collective-permute-start(f32[64,1024]{1,0:T(8,128)S(1)} %get-tuple-element.104), channel_id=1, source_target_pairs={{0,4},{4,0},{8,12},{12,8},{1,5},{5,1},{9,13},{13,9},{2,6},{6,2},{1... | collective-permute-start | bytes 786440 | tf_op jit(solution)/shard_map/ppermute | solution.py:474
  94.8 1.2 collective-permute-done.16.got
  96.0 0.9 collective-permute-start.17
  96.8 3.9 %collective-permute-done.17.b = f32[32,1024]{1,0:T(8,128)S(1)} collective-permute-done((f32[32,1024]{1,0:T(8,128)S(1)}, f32[32,1024]{1,0:T(8,128)S(1)}, u32[]{:S(2)}, u32[]{:S(2)}) %collective-permute-start.17) | collective-permute-done | bytes 131104 | tf_op jit(solution)/shard_map/ppermute | solution.py:474
  101.0 14.1 %all_to_all.21.got = f32[16,4,896]{2,1,0:T(4,128)S(1)} all-to-all(f32[16,4,896]{2,1,0:T(4,128)S(1)} %shard_map.161), channel_id=1, replica_groups=mesh['gz'=16,'gy'=4,'gx'=4] {'gz'}, dimensions={0} | all-to-all | bytes 458752 | tf_op jit(solution)/shard_map/all_to_all | solution.py:498
  115.1 1.1 shard_map.162
  116.1 3.6 %all-to-all-start.3 = ((f32[16,4,384]{2,1,0:T(4,128)}), f32[16,4,384]{2,1,0:T(4,128)S(1)}, u32[]{:S(2)}, u32[]{:S(2)}) async-start(f32[16,4,384]{2,1,0:T(4,128)} %get-tuple-element.108), calls=%async_computation.3 | async-start | bytes 196608 | tf_op jit(solution)/shard_map/all_to_all | solution.py:498
  119.8 1.4 shard_map.163.local_from
  121.2 8.0 %all-to-all-done.3.got = f32[16,4,384]{2,1,0:T(4,128)S(1)} async-done(((f32[16,4,384]{2,1,0:T(4,128)}), f32[16,4,384]{2,1,0:T(4,128)S(1)}, u32[]{:S(2)}, u32[]{:S(2)}) %all-to-all-start.3) | async-done | bytes 98336 | tf_op jit(solution)/shard_map/all_to_all | solution.py:498
  129.4 1.0 collective-permute-start.18
  130.4 1.9 %collective-permute-done.18.b = f32[32,256]{1,0:T(8,128)S(1)} collective-permute-done((f32[32,256]{1,0:T(8,128)S(1)}, f32[32,256]{1,0:T(8,128)S(1)}, u32[]{:S(2)}, u32[]{:S(2)}) %collective-permute-start.18) | collective-permute-done | bytes 32800 | tf_op jit(solution)/shard_map/ppermute | solution.py:474
  132.2 4.4 %collective-permute-start.19 = (f32[64,256]{1,0:T(8,128)S(1)}, f32[64,256]{1,0:T(8,128)S(1)}, u32[]{:S(2)}, u32[]{:S(2)}) collective-permute-start(f32[64,256]{1,0:T(8,128)S(1)} %shard_map.165.a), channel_id=1, source_target_pairs={{0,4},{4,0},{8,12},{12,8},{1,5},{5,1},{9,13},{13,9},{2,6},{6,2},{1... | collective-permute-start | bytes 196616 | tf_op jit(solution)/shard_map/ppermute | solution.py:474
  136.6 0.9 collective-permute-done.19.b
  137.7 2.5 %collective-permute-start.20 = (f32[160,256]{1,0:T(8,128)S(1)}, f32[160,256]{1,0:T(8,128)S(1)}, u32[]{:S(2)}, u32[]{:S(2)}) collective-permute-start(f32[160,256]{1,0:T(8,128)S(1)} %shard_map.166.a), channel_id=1, source_target_pairs={{0,3},{1,0},{2,1},{3,2},{4,7},{5,4},{6,5},{7,6},{8,11},{9,8},{10,9... | collective-permute-start | bytes 491528 | tf_op jit(solution)/shard_map/ppermute | solution.py:474
  140.9 1.2 shard_map.169
  142.1 1.2 shard_map.168
  143.3 0.8 collective-permute-done.20.b
  144.1 2.8 %collective-permute-done.21.c = f32[160,256]{1,0:T(8,128)S(1)} collective-permute-done((f32[160,256]{1,0:T(8,128)S(1)}, f32[160,256]{1,0:T(8,128)S(1)}, u32[]{:S(2)}, u32[]{:S(2)}) %collective-permute-start.21) | collective-permute-done | bytes 163872 | tf_op jit(solution)/shard_map/ppermute | solution.py:474
  146.9 4.5 %collective-permute-done.22.d = f32[160,256]{1,0:T(8,128)S(1)} collective-permute-done((f32[160,256]{1,0:T(8,128)S(1)}, f32[160,256]{1,0:T(8,128)S(1)}, u32[]{:S(2)}, u32[]{:S(2)}) %collective-permute-start.22) | collective-permute-done | bytes 163872 | tf_op jit(solution)/shard_map/ppermute | solution.py:474
  151.3 5.9 %shard_map.167 = (bf16[128,2048]{1,0:T(8,128)(2,1)}, f32[64,64]{1,0:T(8,128)}, f32[64,64]{1,0:T(8,128)}) custom-call(s32[1]{0:T(128)} %bitcast.at, f32[128,2048]{1,0:T(8,128)} %shard_map.163.local_from, f32[160,256]{1,0:T(8,128)S(1)} %shard_map.166.a, f32[160,256]{1,0:T(8,128)S(1)} %collective-permute-done.20.b, f32[160,256]{1,0:T(8,128)S(1)} %collective-permute-done.21.c, ...), custom_call_target="tpu_custom_call" | custom-call | tf_op jit(solution)/shard_map/pallas_call | solution.py:106
  (56 shorter events, 8.3 us)
Async XLA Ops:
  0.6 30.9 %copy-start.9 = (bf16[64,64]{1,0:T(8,128)(2,1)S(1)}, bf16[64,64]{1,0:T(8,128)(2,1)}, u32[]{:S(2)}) copy-start(bf16[64,64]{1,0:T(8,128)(2,1)} %point.2) | copy-start | bytes 24580
  3.8 7.6 %collective-permute-start = (f32[128,256]{1,0:T(8,128)S(1)}, f32[128,256]{1,0:T(8,128)S(1)}, u32[]{:S(2)}, u32[]{:S(2)}) collective-permute-start(f32[128,256]{1,0:T(8,128)S(1)} %get-tuple-element.66), channel_id=1, source_target_pairs={{0,1},{1,2},{2,3},{3,0},{4,5},{5,6},{6,7},{7,4},{8,9},{9,10},{10,1... | collective-permute-start | bytes 393224 | tf_op jit(solution)/shard_map/ppermute | solution.py:474
  6.0 8.3 %collective-permute-start.1 = (f32[128,256]{1,0:T(8,128)S(1)}, f32[128,256]{1,0:T(8,128)S(1)}, u32[]{:S(2)}, u32[]{:S(2)}) collective-permute-start(f32[128,256]{1,0:T(8,128)S(1)} %get-tuple-element.67), channel_id=1, source_target_pairs={{0,2},{1,3},{2,0},{3,1},{4,6},{5,7},{6,4},{7,5},{8,10},{9,11},{10,... | collective-permute-start | bytes 393224 | tf_op jit(solution)/shard_map/ppermute | solution.py:474
  8.7 5.7 %collective-permute-start.2 = (f32[128,256]{1,0:T(8,128)S(1)}, f32[128,256]{1,0:T(8,128)S(1)}, u32[]{:S(2)}, u32[]{:S(2)}) collective-permute-start(f32[128,256]{1,0:T(8,128)S(1)} %get-tuple-element.68), channel_id=1, source_target_pairs={{0,3},{1,0},{2,1},{3,2},{4,7},{5,4},{6,5},{7,6},{8,11},{9,8},{10,9... | collective-permute-start | bytes 393224 | tf_op jit(solution)/shard_map/ppermute | solution.py:474
  9.7 1.0 copy-start.3
  10.8 3.6 %copy-start = (bf16[4,128,128]{2,1,0:T(8,128)(2,1)S(1)}, bf16[4,128,128]{2,1,0:T(8,128)(2,1)}, u32[]{:S(2)}) copy-start(bf16[4,128,128]{2,1,0:T(8,128)(2,1)} %constant.23.clone.ty) | copy-start | bytes 393220
  10.8 20.8 %copy-start.6 = (bf16[8,16,2048]{2,1,0:T(8,128)(2,1)S(1)}, bf16[8,16,2048]{2,1,0:T(8,128)(2,1)}, u32[]{:S(2)}) copy-start(bf16[8,16,2048]{2,1,0:T(8,128)(2,1)} %param.12) | copy-start | bytes 1572868
  14.4 5.8 %copy-start.5 = (bf16[16,32,64]{2,1,0:T(8,128)(2,1)S(1)}, bf16[16,32,64]{2,1,0:T(8,128)(2,1)}, u32[]{:S(2)}) copy-start(bf16[16,32,64]{2,1,0:T(8,128)(2,1)} %constant.24.clone.tx) | copy-start | bytes 196612
  14.4 17.2 %copy-start.1 = (bf16[8,16,2048]{2,1,0:T(8,128)(2,1)S(1)}, bf16[8,16,2048]{2,1,0:T(8,128)(2,1)}, u32[]{:S(2)}) copy-start(bf16[8,16,2048]{2,1,0:T(8,128)(2,1)} %param.11) | copy-start | bytes 1572868
  14.4 17.2 %copy-start.4 = (bf16[128,2048]{1,0:T(8,128)(2,1)S(1)}, bf16[128,2048]{1,0:T(8,128)(2,1)}, u32[]{:S(2)}) copy-start(bf16[128,2048]{1,0:T(8,128)(2,1)} %get-tuple-element.74.dz) | copy-start | bytes 1572868
  14.6 2.7 %collective-permute-start.3 = (f32[64,256]{1,0:T(8,128)S(1)}, f32[64,256]{1,0:T(8,128)S(1)}, u32[]{:S(2)}, u32[]{:S(2)}) collective-permute-start(f32[64,256]{1,0:T(8,128)S(1)} %get-tuple-element.70), channel_id=1, source_target_pairs={{0,4},{4,0},{8,12},{12,8},{1,5},{5,1},{9,13},{13,9},{2,6},{6,2},{1... | collective-permute-start | bytes 196616 | tf_op jit(solution)/shard_map/ppermute | solution.py:474
  17.4 2.9 %collective-permute-start.4 = (f32[32,256]{1,0:T(8,128)S(1)}, f32[32,256]{1,0:T(8,128)S(1)}, u32[]{:S(2)}, u32[]{:S(2)}) collective-permute-start(f32[32,256]{1,0:T(8,128)S(1)} %get-tuple-element.72), channel_id=1, source_target_pairs={{0,8},{4,12},{8,0},{12,4},{1,9},{5,13},{9,1},{13,5},{2,10},{6,14},... | collective-permute-start | bytes 98312 | tf_op jit(solution)/shard_map/ppermute | solution.py:474
  21.0 19.6 %all-to-all-start = ((f32[16,4,256]{2,1,0:T(4,128)}), f32[16,4,256]{2,1,0:T(4,128)S(1)}, u32[]{:S(2)}, u32[]{:S(2)}) async-start(f32[16,4,256]{2,1,0:T(4,128)} %shard_map.150), calls=%async_computation | async-start | bytes 131072 | tf_op jit(solution)/shard_map/all_to_all | solution.py:498
  31.6 13.3 %copy-start.7 = (bf16[1,4,4,4096]{3,2,1,0:T(4,128)(2,1)S(1)}, bf16[1,4,4,4096]{3,2,1,0:T(4,128)(2,1)}, u32[]{:S(2)}) copy-start(bf16[1,4,4,4096]{3,2,1,0:T(4,128)(2,1)} %spectral.2) | copy-start | bytes 393220
  34.0 0.7 copy-start.11
  34.8 0.7 copy-start.12
  35.5 0.7 copy-start.13
  40.6 18.2 %collective-permute-start.5 = (f32[128,512]{1,0:T(8,128)}, f32[128,512]{1,0:T(8,128)S(1)}, u32[]{:S(2)}, u32[]{:S(2)}) collective-permute-start(f32[128,512]{1,0:T(8,128)} %copy-done.13), channel_id=1, source_target_pairs={{0,1},{1,2},{2,3},{3,0},{4,5},{5,6},{6,7},{7,4},{8,9},{9,10},{10,1... | collective-permute-start | bytes 786440 | tf_op jit(solution)/shard_map/ppermute | solution.py:474
  41.6 17.3 %collective-permute-start.6 = (f32[128,512]{1,0:T(8,128)}, f32[128,512]{1,0:T(8,128)S(1)}, u32[]{:S(2)}, u32[]{:S(2)}) collective-permute-start(f32[128,512]{1,0:T(8,128)} %copy-done.12), channel_id=1, source_target_pairs={{0,2},{1,3},{2,0},{3,1},{4,6},{5,7},{6,4},{7,5},{8,10},{9,11},{10,... | collective-permute-start | bytes 786440 | tf_op jit(solution)/shard_map/ppermute | solution.py:474
  43.7 15.2 %collective-permute-start.7 = (f32[128,512]{1,0:T(8,128)}, f32[128,512]{1,0:T(8,128)S(1)}, u32[]{:S(2)}, u32[]{:S(2)}) collective-permute-start(f32[128,512]{1,0:T(8,128)} %copy-done.11), channel_id=1, source_target_pairs={{0,3},{1,0},{2,1},{3,2},{4,7},{5,4},{6,5},{7,6},{8,11},{9,8},{10,9... | collective-permute-start | bytes 786440 | tf_op jit(solution)/shard_map/ppermute | solution.py:474
  59.0 3.1 %collective-permute-start.8 = (f32[32,256]{1,0:T(8,128)S(1)}, f32[32,256]{1,0:T(8,128)S(1)}, u32[]{:S(2)}, u32[]{:S(2)}) collective-permute-start(f32[32,256]{1,0:T(8,128)S(1)} %shard_map.153.a), channel_id=1, source_target_pairs={{0,8},{4,12},{8,0},{12,4},{1,9},{5,13},{9,1},{13,5},{2,10},{6,14},... | collective-permute-start | bytes 98312 | tf_op jit(solution)/shard_map/ppermute | solution.py:474
  62.1 6.3 %collective-permute-start.9 = (f32[64,256]{1,0:T(8,128)S(1)}, f32[64,256]{1,0:T(8,128)S(1)}, u32[]{:S(2)}, u32[]{:S(2)}) collective-permute-start(f32[64,256]{1,0:T(8,128)S(1)} %shard_map.154.a), channel_id=1, source_target_pairs={{0,4},{4,0},{8,12},{12,8},{1,5},{5,1},{9,13},{13,9},{2,6},{6,2},{1... | collective-permute-start | bytes 196616 | tf_op jit(solution)/shard_map/ppermute | solution.py:474
  68.7 5.0 %collective-permute-start.10 = (f32[128,256]{1,0:T(8,128)S(1)}, f32[128,256]{1,0:T(8,128)S(1)}, u32[]{:S(2)}, u32[]{:S(2)}) collective-permute-start(f32[128,256]{1,0:T(8,128)S(1)} %shard_map.155.a), channel_id=1, source_target_pairs={{0,3},{1,0},{2,1},{3,2},{4,7},{5,4},{6,5},{7,6},{8,11},{9,8},{10,9... | collective-permute-start | bytes 393224 | tf_op jit(solution)/shard_map/ppermute | solution.py:474
  68.9 6.3 %collective-permute-start.11 = (f32[128,256]{1,0:T(8,128)S(1)}, f32[128,256]{1,0:T(8,128)S(1)}, u32[]{:S(2)}, u32[]{:S(2)}) collective-permute-start(f32[128,256]{1,0:T(8,128)S(1)} %shard_map.155.a), channel_id=1, source_target_pairs={{0,2},{1,3},{2,0},{3,1},{4,6},{5,7},{6,4},{7,5},{8,10},{9,11},{10,... | collective-permute-start | bytes 393224 | tf_op jit(solution)/shard_map/ppermute | solution.py:474
  70.7 7.7 %collective-permute-start.12 = (f32[128,256]{1,0:T(8,128)S(1)}, f32[128,256]{1,0:T(8,128)S(1)}, u32[]{:S(2)}, u32[]{:S(2)}) collective-permute-start(f32[128,256]{1,0:T(8,128)S(1)} %shard_map.155.a), channel_id=1, source_target_pairs={{0,1},{1,2},{2,3},{3,0},{4,5},{5,6},{6,7},{7,4},{8,9},{9,10},{10,1... | collective-permute-start | bytes 393224 | tf_op jit(solution)/shard_map/ppermute | solution.py:474
  83.9 8.9 %collective-permute-start.13 = (f32[128,256]{1,0:T(8,128)S(1)}, f32[128,256]{1,0:T(8,128)S(1)}, u32[]{:S(2)}, u32[]{:S(2)}) collective-permute-start(f32[128,256]{1,0:T(8,128)S(1)} %get-tuple-element.93), channel_id=1, source_target_pairs={{0,1},{1,2},{2,3},{3,0},{4,5},{5,6},{6,7},{7,4},{8,9},{9,10},{10,1... | collective-permute-start | bytes 393224 | tf_op jit(solution)/shard_map/ppermute | solution.py:474
  84.0 8.8 %collective-permute-start.14 = (f32[128,256]{1,0:T(8,128)S(1)}, f32[128,256]{1,0:T(8,128)S(1)}, u32[]{:S(2)}, u32[]{:S(2)}) collective-permute-start(f32[128,256]{1,0:T(8,128)S(1)} %get-tuple-element.94), channel_id=1, source_target_pairs={{0,2},{1,3},{2,0},{3,1},{4,6},{5,7},{6,4},{7,5},{8,10},{9,11},{10,... | collective-permute-start | bytes 393224 | tf_op jit(solution)/shard_map/ppermute | solution.py:474
  85.6 2.2 %copy-start.2 = (bf16[128,2048]{1,0:T(8,128)(2,1)S(1)}, bf16[128,2048]{1,0:T(8,128)(2,1)}, u32[]{:S(2)}) copy-start(bf16[128,2048]{1,0:T(8,128)(2,1)} %get-tuple-element.109.dz) | copy-start | bytes 1572868
  85.6 7.2 %collective-permute-start.15 = (f32[128,256]{1,0:T(8,128)S(1)}, f32[128,256]{1,0:T(8,128)S(1)}, u32[]{:S(2)}, u32[]{:S(2)}) collective-permute-start(f32[128,256]{1,0:T(8,128)S(1)} %get-tuple-element.95), channel_id=1, source_target_pairs={{0,3},{1,0},{2,1},{3,2},{4,7},{5,4},{6,5},{7,6},{8,11},{9,8},{10,9... | collective-permute-start | bytes 393224 | tf_op jit(solution)/shard_map/ppermute | solution.py:474
  93.0 3.0 %collective-permute-start.16 = (f32[64,1024]{1,0:T(8,128)S(1)}, f32[64,1024]{1,0:T(8,128)S(1)}, u32[]{:S(2)}, u32[]{:S(2)}) collective-permute-start(f32[64,1024]{1,0:T(8,128)S(1)} %get-tuple-element.104), channel_id=1, source_target_pairs={{0,4},{4,0},{8,12},{12,8},{1,5},{5,1},{9,13},{13,9},{2,6},{6,2},{1... | collective-permute-start | bytes 786440 | tf_op jit(solution)/shard_map/ppermute | solution.py:474
  96.0 4.8 %collective-permute-start.17 = (f32[32,1024]{1,0:T(8,128)S(1)}, f32[32,1024]{1,0:T(8,128)S(1)}, u32[]{:S(2)}, u32[]{:S(2)}) collective-permute-start(f32[32,1024]{1,0:T(8,128)S(1)} %get-tuple-element.106), channel_id=1, source_target_pairs={{0,8},{4,12},{8,0},{12,4},{1,9},{5,13},{9,1},{13,5},{2,10},{6,14},... | collective-permute-start | bytes 393224 | tf_op jit(solution)/shard_map/ppermute | solution.py:474
  101.0 14.1 %copy-start.8 = (bf16[1,4,4,4096]{3,2,1,0:T(4,128)(2,1)S(1)}, bf16[1,4,4,4096]{3,2,1,0:T(4,128)(2,1)}, u32[]{:S(2)}) copy-start(bf16[1,4,4,4096]{3,2,1,0:T(4,128)(2,1)} %spectral.3) | copy-start | bytes 393220
  116.1 3.7 %copy-start.10 = (bf16[64,64]{1,0:T(8,128)(2,1)S(1)}, bf16[64,64]{1,0:T(8,128)(2,1)}, u32[]{:S(2)}) copy-start(bf16[64,64]{1,0:T(8,128)(2,1)} %point.3) | copy-start | bytes 24580
  116.1 13.1 %all-to-all-start.3 = ((f32[16,4,384]{2,1,0:T(4,128)}), f32[16,4,384]{2,1,0:T(4,128)S(1)}, u32[]{:S(2)}, u32[]{:S(2)}) async-start(f32[16,4,384]{2,1,0:T(4,128)} %get-tuple-element.108), calls=%async_computation.3 | async-start | bytes 196608 | tf_op jit(solution)/shard_map/all_to_all | solution.py:498
  129.4 2.9 %collective-permute-start.18 = (f32[32,256]{1,0:T(8,128)S(1)}, f32[32,256]{1,0:T(8,128)S(1)}, u32[]{:S(2)}, u32[]{:S(2)}) collective-permute-start(f32[32,256]{1,0:T(8,128)S(1)} %get-tuple-element.112.a), channel_id=1, source_target_pairs={{0,8},{4,12},{8,0},{12,4},{1,9},{5,13},{9,1},{13,5},{2,10},{6,14},... | collective-permute-start | bytes 98312 | tf_op jit(solution)/shard_map/ppermute | solution.py:474
  132.2 5.3 %collective-permute-start.19 = (f32[64,256]{1,0:T(8,128)S(1)}, f32[64,256]{1,0:T(8,128)S(1)}, u32[]{:S(2)}, u32[]{:S(2)}) collective-permute-start(f32[64,256]{1,0:T(8,128)S(1)} %shard_map.165.a), channel_id=1, source_target_pairs={{0,4},{4,0},{8,12},{12,8},{1,5},{5,1},{9,13},{13,9},{2,6},{6,2},{1... | collective-permute-start | bytes 196616 | tf_op jit(solution)/shard_map/ppermute | solution.py:474
  137.7 6.4 %collective-permute-start.20 = (f32[160,256]{1,0:T(8,128)S(1)}, f32[160,256]{1,0:T(8,128)S(1)}, u32[]{:S(2)}, u32[]{:S(2)}) collective-permute-start(f32[160,256]{1,0:T(8,128)S(1)} %shard_map.166.a), channel_id=1, source_target_pairs={{0,3},{1,0},{2,1},{3,2},{4,7},{5,4},{6,5},{7,6},{8,11},{9,8},{10,9... | collective-permute-start | bytes 491528 | tf_op jit(solution)/shard_map/ppermute | solution.py:474
  140.2 6.7 %collective-permute-start.21 = (f32[160,256]{1,0:T(8,128)S(1)}, f32[160,256]{1,0:T(8,128)S(1)}, u32[]{:S(2)}, u32[]{:S(2)}) collective-permute-start(f32[160,256]{1,0:T(8,128)S(1)} %shard_map.166.a), channel_id=1, source_target_pairs={{0,2},{1,3},{2,0},{3,1},{4,6},{5,7},{6,4},{7,5},{8,10},{9,11},{10,... | collective-permute-start | bytes 491528 | tf_op jit(solution)/shard_map/ppermute | solution.py:474
  140.5 10.8 %collective-permute-start.22 = (f32[160,256]{1,0:T(8,128)S(1)}, f32[160,256]{1,0:T(8,128)S(1)}, u32[]{:S(2)}, u32[]{:S(2)}) collective-permute-start(f32[160,256]{1,0:T(8,128)S(1)} %shard_map.166.a), channel_id=1, source_target_pairs={{0,1},{1,2},{2,3},{3,0},{4,5},{5,6},{6,7},{7,4},{8,9},{9,10},{10,1... | collective-permute-start | bytes 491528 | tf_op jit(solution)/shard_map/ppermute | solution.py:474

commit v3 on v2

--- a/solution.py
+++ b/solution.py
@@ -39,7 +39,8 @@
     for d in range(DEV_Z):
         modes = (((d + four) % 4)[:, None] * 4 + four[None, :]).reshape(-1)
         tz[d] = cas(modes[None, :], CELLS_Z * DEV_Z, z[:, None] * DEV_Z + d)
-    tz = np.repeat(tz, C, axis=2).astype(np.float32)
+    tz_back = np.repeat(tz.transpose(0, 2, 1), C, axis=2)
+    tz = np.repeat(tz, C, axis=2)
     y = np.arange(CELLS_Y)
     ty = np.zeros((DEV_Y, 4, CELLS_X, 4, CELLS_X, CELLS_Y), np.float32)
     for d in range(DEV_Y):
@@ -55,7 +56,7 @@
         for l in range(4):
             tx[d, :, l, :, l] = small
     tx = tx.reshape(DEV_X, 64, CELLS_X * 4).transpose(0, 2, 1)
-    return tuple(t.astype(bf16) for t in (tz, ty, tx))
+    return tuple(t.astype(bf16) for t in (tz, tz_back, ty, tx))
 
 
 def dot(left, right):
@@ -148,9 +149,17 @@
         ka[z * C : (z + 1) * C, :] = (eye * mine[z : z + 1, :wide]).astype(bf16)
 
 
+def fill_back(ka, mine, b):
+    lane = lax.broadcasted_iota(jnp.int32, (C, 256), 1) & (C - 1)
+    row = lax.broadcasted_iota(jnp.int32, (C, 256), 0)
+    eye = jnp.where(lane == row, 1.0, 0.0)
+    for k in range(16):
+        ka[k * C : (k + 1) * C, block(b)] = (eye * mine[k : k + 1, block(b)]).astype(bf16)
+
+
 def start_kernel(
-    at, pre_from, grad_from, tz, dz_to, p1, p2, p3, mine,
-    ka, total, pre, grad, dz, short, sems,
+    at, pre_from, grad_from, tz, tz_back, dz_to, p1, p2, p3, mine, mine_back,
+    ka, total, pre, grad, dz, short, short_back, sems,
 ):
     def copies(b):
         cut = block(b)
@@ -167,6 +176,8 @@
     for b in range(8):
         for copy in copies(b):
             copy.start()
+    second = pltpu.make_async_copy(tz_back.at[at_z(at)], short_back, sems.at[25])
+    second.start()
     first.wait()
     mine[...] = short[...].astype(f32)
     total[...] = jnp.zeros_like(total)
@@ -182,6 +193,8 @@
         if b > 0:
             total[...] += dot(dz[:, block(b - 1)], ka[block(b - 1), 256:])
     store_parts(total[...], (p1, p2, p3))
+    second.wait()
+    mine_back[...] = short_back[...].astype(f32)
     for b in range(8):
         leave(b).wait()
 
@@ -401,8 +414,8 @@
 
 
 def middle_kernel(
-    at, local_from, slope_from, a, b, c, d, mine, dz_to, p1, p2, p3,
-    modes, total, dz, ka, local, slope, sems,
+    at, local_from, slope_from, a, b, c, d, mine, mine_back, dz_to, p1, p2, p3,
+    modes, total, dz, ka, ka_back, local, slope, sems,
 ):
     def copies(i):
         cut = block(i)
@@ -419,14 +432,15 @@
             copy.start()
     stack_modes((a, b, c, d), modes)
     total[...] = jnp.zeros_like(total)
-    fill_table(ka, mine, 0)
+    fill_back(ka_back, mine_back, 0)
     for i in range(9):
         if i < 8:
             if i < 7:
-                fill_table(ka, mine, i + 1)
+                fill_back(ka_back, mine_back, i + 1)
+            fill_table(ka, mine, i)
             for copy in copies(i):
                 copy.wait()
-            down = dot_nt(modes[...], ka[block(i), :]) + local[:, block(i)]
+            down = dot(modes[...], ka_back[:, block(i)]) + local[:, block(i)]
             dz[:, block(i)] = (down * slope[:, block(i)]).astype(bf16)
             leave(i).start()
         if i > 0:
@@ -437,24 +451,17 @@
 
 
 def end_kernel(
-    at, local_from, a, b, c, d, mine, out_to, weight_two, weight_one,
-    modes, out, ka, local, sems,
+    at, a, b, c, d, mine, local, out_to, weight_two, weight_one, modes, out, ka, sems
 ):
-    def copy(i):
-        return pltpu.make_async_copy(local_from.at[:, block(i)], local.at[:, block(i)], sems.at[i])
-
     def leave(i):
-        return pltpu.make_async_copy(out.at[:, block(i)], out_to.at[:, block(i)], sems.at[8 + i])
-
-    for i in range(8):
-        copy(i).start()
+        return pltpu.make_async_copy(out.at[:, block(i)], out_to.at[:, block(i)], sems.at[i])
+
     stack_modes((a, b, c, d), modes)
-    fill_table(ka, mine, 0)
+    fill_back(ka, mine, 0)
     for i in range(8):
         if i < 7:
-            fill_table(ka, mine, i + 1)
-        copy(i).wait()
-        down = dot_nt(modes[...], ka[block(i), :]) + local[:, block(i)]
+            fill_back(ka, mine, i + 1)
+        down = dot(modes[...], ka[:, block(i)]) + local[:, block(i)]
         out[:, block(i)] = down.astype(bf16)
         leave(i).start()
     w = (a[ROWS:] + b[ROWS:]) + (c[ROWS:] + d[ROWS:])
@@ -501,7 +508,7 @@
 def on_device(
     grid_input, pre_one, pre_two, grad_output, spectral_one, spectral_two, point_one, point_two
 ):
-    tz, ty, tx = [jnp.asarray(t) for t in build_tables()]
+    tz, tz_back, ty, tx = [jnp.asarray(t) for t in build_tables()]
     at = lax.axis_index(("gz", "gy", "gx")).reshape(1)
     first, pre_one, pre_two, upstream = [
         t.reshape(ROWS, WIDE) for t in (grid_input, pre_one, pre_two, grad_output)
@@ -509,17 +516,19 @@
     big = (ROWS, WIDE)
     half = ((ROWS, 256), f32)
     table = ((WIDE, 16 * C), bf16)
+    table_back = ((16 * C, WIDE), bf16)
     native = ((4, 4, C * C), f32)
     dma = pltpu.SemaphoreType.DMA
 
-    dz_two, *parts, mine = call(
+    dz_two, *parts, mine, mine_back = call(
         start_kernel,
-        [(big, bf16, "raw")] + [half] * 3 + [((CELLS_Z, 16 * C), f32)],
+        [(big, bf16, "raw")] + [half] * 3 + [((CELLS_Z, 16 * C), f32), ((16, WIDE), f32)],
         at,
         pre_two,
         upstream,
         tz,
-        raw=3,
+        tz_back,
+        raw=4,
         scratch=[
             table,
             ((ROWS, 12 * C), f32),
@@ -527,7 +536,8 @@
             (big, bf16),
             (big, bf16),
             ((CELLS_Z, 16 * C), bf16),
-            dma((25,)),
+            ((16, WIDE), bf16),
+            dma((26,)),
         ],
     )
     own, fold = call(
@@ -577,7 +587,6 @@
         scratch=[native],
     )
     got = over_x(back)
-    got, got_in = lax.optimization_barrier((got, got_in))
     (tall,) = call(back_x_kernel, [((32, 256), f32)], at, got, tx)
     got = spread_y(at, tall)
     (tall,) = call(back_y_kernel, [half], at, *got, ty)
@@ -591,13 +600,15 @@
         slope,
         *got,
         mine,
+        mine_back,
         raw=2,
-        limit=12,
+        limit=16,
         scratch=[
             ((ROWS, 16 * C), bf16),
             ((ROWS, 12 * C), f32),
             (big, bf16),
             table,
+            table_back,
             (big, f32),
             (big, f32),
             dma((24,)),
@@ -647,11 +658,10 @@
         end_kernel,
         [(big, bf16, "raw"), ((C, C), f32, 0), ((C, C), f32, 0)],
         at,
+        *got,
+        mine_back,
         local_one,
-        *got,
-        mine,
-        raw=1,
-        scratch=[((ROWS, 16 * C), bf16), (big, bf16), table, (big, f32), dma((16,))],
+        scratch=[((ROWS, 16 * C), bf16), (big, bf16), table_back, dma((8,))],
     )
     return (
         input_grad.reshape(CELLS_X, CELLS_Y, WIDE),

time: 158 us -> 160 us (1.013)
  waiting for transfers between devices: 48.6 us -> 54.4 us
  Pallas kernels: 26.1 us -> 21.3 us
    ppermute x23, waiting for transfers between devices: 36.2 us -> 41.9 us  [shifted(): return lax.ppermute(v, axis, pairs)]
    pallas_call x24, Pallas kernels: 26.1 us -> 21.3 us  [call(): pl.pallas_call(body, out_shape=shapes, in_specs=[pl.BlockSpec(memory_spac...]
    unnamed x28 -> x36, local copies, waits for them, and re-layouts: 3.19 us -> 4.11 us
  transfers between devices with their start and end apart: 25 -> 25, of which waited for: 18 -> 17; matrix products, arithmetic and copies ran while one was open for 0% -> 0% of each run, Pallas kernels for 5% -> 8%
where the time goes in v3:
time: 160 us; the launch traced here: 159 us
  waiting for transfers between devices  54.4 us (34%)
  starting transfers between devices  50.7 us (32%)
  blocking collectives  27.6 us (17%)
  Pallas kernels  21.3 us (13%)
  local copies, waits for them, and re-layouts  4.11 us (3%)
    ppermute x23, waiting for transfers between devices, shifted(): return lax.ppermute(v, axis, pairs)  41.9 us
    ppermute x23, starting transfers between devices, shifted(): return lax.ppermute(v, axis, pairs)  36.6 us
    all_to_all x2, blocking collectives, over_x(): return lax.all_to_all(v, 'gz', 0, 0, tiled=True)  27.6 us
    pallas_call x24, Pallas kernels, call(): pl.pallas_call(body, out_shape=shapes, in_specs=[pl.BlockSpec(memory_spac...  21.3 us
    all_to_all x2, starting transfers between devices, over_x(): return lax.all_to_all(v, 'gz', 0, 0, tiled=True)  14.2 us
    all_to_all x2, waiting for transfers between devices, over_x(): return lax.all_to_all(v, 'gz', 0, 0, tiled=True)  12.6 us
    unnamed x36, local copies, waits for them, and re-layouts  4.11 us
  transfers between devices with their start and end apart: 25, of which 17 were waited for; matrix products, arithmetic and copies ran while one was open for 0% of the time, Pallas kernels for 8%

profile of v3, /device:TPU:1, one launch (start us, length us, event | category | flops | bytes accessed | tf_op | source)
XLA Modules:
  0.0 159.3 jit_solution(8558391968960202283)
XLA Ops:
  0.7 3.2 %shard_map.155 = (bf16[128,2048]{1,0:T(8,128)(2,1)}, f32[128,256]{1,0:T(8,128)S(1)}, f32[128,256]{1,0:T(8,128)S(1)}, f32[128,256]{1,0:T(8,128)S(1)}, f32[32,1024]{1,0:T(8,128)S(1)}, /*index=5*/f32[16,2048]{1,0:T(8,128)S(1)}) custom-call(s32[1]{0:T(128)} %bitcast.at, bf16[128,2048]{1,0:T(8,128)(2,1)} %bitcast.11, bf16[128,2048]{1,0:T(8,128)(2,1)} %bitcast.12, ...), custom_call_target="tpu_custom_call" | custom-call | tf_op jit(solution)/shard_map/pallas_call | solution.py:107
  3.9 2.2 %collective-permute-start = (f32[128,256]{1,0:T(8,128)S(1)}, f32[128,256]{1,0:T(8,128)S(1)}, u32[]{:S(2)}, u32[]{:S(2)}) collective-permute-start(f32[128,256]{1,0:T(8,128)S(1)} %get-tuple-element.62), channel_id=1, source_target_pairs={{0,1},{1,2},{2,3},{3,0},{4,5},{5,6},{6,7},{7,4},{8,9},{9,10},{10,1... | collective-permute-start | bytes 393224 | tf_op jit(solution)/shard_map/ppermute | solution.py:481
  6.0 2.6 %collective-permute-start.1 = (f32[128,256]{1,0:T(8,128)S(1)}, f32[128,256]{1,0:T(8,128)S(1)}, u32[]{:S(2)}, u32[]{:S(2)}) collective-permute-start(f32[128,256]{1,0:T(8,128)S(1)} %get-tuple-element.63), channel_id=1, source_target_pairs={{0,2},{1,3},{2,0},{3,1},{4,6},{5,7},{6,4},{7,5},{8,10},{9,11},{10,... | collective-permute-start | bytes 393224 | tf_op jit(solution)/shard_map/ppermute | solution.py:481
  8.7 1.1 collective-permute-start.2
  9.7 1.0 copy-done.4
  11.5 2.9 %collective-permute-done.1.c = f32[128,256]{1,0:T(8,128)S(1)} collective-permute-done((f32[128,256]{1,0:T(8,128)S(1)}, f32[128,256]{1,0:T(8,128)S(1)}, u32[]{:S(2)}, u32[]{:S(2)}) %collective-permute-start.1) | collective-permute-done | bytes 131104 | tf_op jit(solution)/shard_map/ppermute | solution.py:481
  14.6 1.8 %collective-permute-start.3 = (f32[64,256]{1,0:T(8,128)S(1)}, f32[64,256]{1,0:T(8,128)S(1)}, u32[]{:S(2)}, u32[]{:S(2)}) collective-permute-start(f32[64,256]{1,0:T(8,128)S(1)} %get-tuple-element.66), channel_id=1, source_target_pairs={{0,4},{4,0},{8,12},{12,8},{1,5},{5,1},{9,13},{13,9},{2,6},{6,2},{1... | collective-permute-start | bytes 196616 | tf_op jit(solution)/shard_map/ppermute | solution.py:481
  16.4 0.9 collective-permute-done.3.got
  17.4 1.5 collective-permute-start.4
  18.9 1.3 collective-permute-done.4.b
  20.2 0.8 shard_map.159
  21.0 10.5 %all-to-all-start = ((f32[16,4,256]{2,1,0:T(4,128)}), f32[16,4,256]{2,1,0:T(4,128)S(1)}, u32[]{:S(2)}, u32[]{:S(2)}) async-start(f32[16,4,256]{2,1,0:T(4,128)} %shard_map.159), calls=%async_computation | async-start | bytes 131072 | tf_op jit(solution)/shard_map/all_to_all | solution.py:505
  31.6 2.4 %shard_map.160 = (f32[128,2048]{1,0:T(8,128)}, f32[128,2048]{1,0:T(8,128)}, f32[64,64]{1,0:T(8,128)S(1)}, f32[128,512]{1,0:T(8,128)S(1)}, f32[128,512]{1,0:T(8,1...) custom-call(s32[1]{0:T(128)} %bitcast.at, bf16[128,2048]{1,0:T(8,128)(2,1)S(1)} %bitcast.10, ...), custom_call_target="tpu_custom_call" | custom-call | tf_op jit(solution)/shard_map/pallas_call | solution.py:107
  36.2 4.5 %all-to-all-done.got = f32[16,4,256]{2,1,0:T(4,128)S(1)} async-done(((f32[16,4,256]{2,1,0:T(4,128)}), f32[16,4,256]{2,1,0:T(4,128)S(1)}, u32[]{:S(2)}, u32[]{:S(2)}) %all-to-all-start) | async-done | bytes 65568 | tf_op jit(solution)/shard_map/all_to_all | solution.py:505
  40.6 0.9 copy-done.8
  41.9 13.6 %all_to_all.20.got = f32[16,4,256]{2,1,0:T(4,128)S(1)} all-to-all(f32[16,4,256]{2,1,0:T(4,128)S(1)} %get-tuple-element.80), channel_id=1, replica_groups=mesh['gz'=16,'gy'=4,'gx'=4] {'gz'}, dimensions={0} | all-to-all | bytes 131072 | tf_op jit(solution)/shard_map/all_to_all | solution.py:505
  55.7 0.8 collective-permute-start.5
  56.5 2.1 %collective-permute-done.5.b = f32[32,256]{1,0:T(8,128)S(1)} collective-permute-done((f32[32,256]{1,0:T(8,128)S(1)}, f32[32,256]{1,0:T(8,128)S(1)}, u32[]{:S(2)}, u32[]{:S(2)}) %collective-permute-start.5) | collective-permute-done | bytes 32800 | tf_op jit(solution)/shard_map/ppermute | solution.py:481
  58.6 4.6 %collective-permute-start.6 = (f32[64,256]{1,0:T(8,128)S(1)}, f32[64,256]{1,0:T(8,128)S(1)}, u32[]{:S(2)}, u32[]{:S(2)}) collective-permute-start(f32[64,256]{1,0:T(8,128)S(1)} %shard_map.163.a), channel_id=1, source_target_pairs={{0,4},{4,0},{8,12},{12,8},{1,5},{5,1},{9,13},{13,9},{2,6},{6,2},{1... | collective-permute-start | bytes 196616 | tf_op jit(solution)/shard_map/ppermute | solution.py:481
  63.1 0.9 collective-permute-done.6.b
  64.3 1.9 %collective-permute-start.7 = (f32[128,256]{1,0:T(8,128)S(1)}, f32[128,256]{1,0:T(8,128)S(1)}, u32[]{:S(2)}, u32[]{:S(2)}) collective-permute-start(f32[128,256]{1,0:T(8,128)S(1)} %shard_map.164.a), channel_id=1, source_target_pairs={{0,3},{1,0},{2,1},{3,2},{4,7},{5,4},{6,5},{7,6},{8,11},{9,8},{10,9... | collective-permute-start | bytes 393224 | tf_op jit(solution)/shard_map/ppermute | solution.py:481
  66.2 1.9 %collective-permute-start.14 = (f32[128,512]{1,0:T(8,128)S(1)}, f32[128,512]{1,0:T(8,128)S(1)}, u32[]{:S(2)}, u32[]{:S(2)}) collective-permute-start(f32[128,512]{1,0:T(8,128)S(1)} %copy-done.15), channel_id=1, source_target_pairs={{0,2},{1,3},{2,0},{3,1},{4,6},{5,7},{6,4},{7,5},{8,10},{9,11},{10,... | collective-permute-start | bytes 786440 | tf_op jit(solution)/shard_map/ppermute | solution.py:481
  68.1 1.2 collective-permute-start.8
  69.7 2.4 %collective-permute-start.15 = (f32[128,512]{1,0:T(8,128)S(1)}, f32[128,512]{1,0:T(8,128)S(1)}, u32[]{:S(2)}, u32[]{:S(2)}) collective-permute-start(f32[128,512]{1,0:T(8,128)S(1)} %copy-done.13), channel_id=1, source_target_pairs={{0,3},{1,0},{2,1},{3,2},{4,7},{5,4},{6,5},{7,6},{8,11},{9,8},{10,9... | collective-permute-start | bytes 786440 | tf_op jit(solution)/shard_map/ppermute | solution.py:481
  72.1 10.2 %collective-permute-done.8.c = f32[128,256]{1,0:T(8,128)S(1)} collective-permute-done((f32[128,256]{1,0:T(8,128)S(1)}, f32[128,256]{1,0:T(8,128)S(1)}, u32[]{:S(2)}, u32[]{:S(2)}) %collective-permute-start.8) | collective-permute-done | bytes 131104 | tf_op jit(solution)/shard_map/ppermute | solution.py:481
  82.3 3.6 %collective-permute-done.9.d = f32[128,256]{1,0:T(8,128)S(1)} collective-permute-done((f32[128,256]{1,0:T(8,128)S(1)}, f32[128,256]{1,0:T(8,128)S(1)}, u32[]{:S(2)}, u32[]{:S(2)}) %collective-permute-start.9) | collective-permute-done | bytes 131104 | tf_op jit(solution)/shard_map/ppermute | solution.py:481
  85.9 4.5 %shard_map.165 = (bf16[128,2048]{1,0:T(8,128)(2,1)}, f32[128,256]{1,0:T(8,128)S(1)}, f32[128,256]{1,0:T(8,128)S(1)}, f32[128,256]{1,0:T(8,128)S(1)}) custom-call(s32[1]{0:T(128)} %bitcast.at, f32[128,2048]{1,0:T(8,128)} %get-tuple-element.71.local_from, f32[128,2048]{1,0:T(8,128)} %get-tuple-element.72.slope_from, f32[128,256]{1,0:T(8,128)S(1)} %shard_map.164.a, ...), custom_call_target="tpu_custom_call" | custom-call | tf_op jit(solution)/shard_map/pallas_call | solution.py:107
  91.2 2.1 %collective-permute-start.12 = (f32[128,256]{1,0:T(8,128)S(1)}, f32[128,256]{1,0:T(8,128)S(1)}, u32[]{:S(2)}, u32[]{:S(2)}) collective-permute-start(f32[128,256]{1,0:T(8,128)S(1)} %get-tuple-element.87), channel_id=1, source_target_pairs={{0,3},{1,0},{2,1},{3,2},{4,7},{5,4},{6,5},{7,6},{8,11},{9,8},{10,9... | collective-permute-start | bytes 393224 | tf_op jit(solution)/shard_map/ppermute | solution.py:481
  94.3 4.6 %collective-permute-done.10.b = f32[128,256]{1,0:T(8,128)S(1)} collective-permute-done((f32[128,256]{1,0:T(8,128)S(1)}, f32[128,256]{1,0:T(8,128)S(1)}, u32[]{:S(2)}, u32[]{:S(2)}) %collective-permute-start.10) | collective-permute-done | bytes 131104 | tf_op jit(solution)/shard_map/ppermute | solution.py:481
  99.0 2.3 %collective-permute-start.16 = (f32[64,1024]{1,0:T(8,128)S(1)}, f32[64,1024]{1,0:T(8,128)S(1)}, u32[]{:S(2)}, u32[]{:S(2)}) collective-permute-start(f32[64,1024]{1,0:T(8,128)S(1)} %get-tuple-element.96), channel_id=1, source_target_pairs={{0,4},{4,0},{8,12},{12,8},{1,5},{5,1},{9,13},{13,9},{2,6},{6,2},{1... | collective-permute-start | bytes 786440 | tf_op jit(solution)/shard_map/ppermute | solution.py:481
  101.3 1.2 collective-permute-done.16.got
  102.5 0.8 collective-permute-start.17
  103.3 3.9 %collective-permute-done.17.b = f32[32,1024]{1,0:T(8,128)S(1)} collective-permute-done((f32[32,1024]{1,0:T(8,128)S(1)}, f32[32,1024]{1,0:T(8,128)S(1)}, u32[]{:S(2)}, u32[]{:S(2)}) %collective-permute-start.17) | collective-permute-done | bytes 131104 | tf_op jit(solution)/shard_map/ppermute | solution.py:481
  107.5 14.1 %all_to_all.21.got = f32[16,4,896]{2,1,0:T(4,128)S(1)} all-to-all(f32[16,4,896]{2,1,0:T(4,128)S(1)} %shard_map.170), channel_id=1, replica_groups=mesh['gz'=16,'gy'=4,'gx'=4] {'gz'}, dimensions={0} | all-to-all | bytes 458752 | tf_op jit(solution)/shard_map/all_to_all | solution.py:505
  121.6 1.1 shard_map.171
  122.6 3.6 %all-to-all-start.3 = ((f32[16,4,384]{2,1,0:T(4,128)}), f32[16,4,384]{2,1,0:T(4,128)S(1)}, u32[]{:S(2)}, u32[]{:S(2)}) async-start(f32[16,4,384]{2,1,0:T(4,128)} %get-tuple-element.100), calls=%async_computation.3 | async-start | bytes 196608 | tf_op jit(solution)/shard_map/all_to_all | solution.py:505
  126.3 1.4 shard_map.172.local
  127.7 8.1 %all-to-all-done.3.got = f32[16,4,384]{2,1,0:T(4,128)S(1)} async-done(((f32[16,4,384]{2,1,0:T(4,128)}), f32[16,4,384]{2,1,0:T(4,128)S(1)}, u32[]{:S(2)}, u32[]{:S(2)}) %all-to-all-start.3) | async-done | bytes 98336 | tf_op jit(solution)/shard_map/all_to_all | solution.py:505
  135.9 1.0 collective-permute-start.18
  136.9 1.9 %collective-permute-done.18.b = f32[32,256]{1,0:T(8,128)S(1)} collective-permute-done((f32[32,256]{1,0:T(8,128)S(1)}, f32[32,256]{1,0:T(8,128)S(1)}, u32[]{:S(2)}, u32[]{:S(2)}) %collective-permute-start.18) | collective-permute-done | bytes 32800 | tf_op jit(solution)/shard_map/ppermute | solution.py:481
  138.8 4.3 %collective-permute-start.19 = (f32[64,256]{1,0:T(8,128)S(1)}, f32[64,256]{1,0:T(8,128)S(1)}, u32[]{:S(2)}, u32[]{:S(2)}) collective-permute-start(f32[64,256]{1,0:T(8,128)S(1)} %shard_map.174.a), channel_id=1, source_target_pairs={{0,4},{4,0},{8,12},{12,8},{1,5},{5,1},{9,13},{13,9},{2,6},{6,2},{1... | collective-permute-start | bytes 196616 | tf_op jit(solution)/shard_map/ppermute | solution.py:481
  143.1 0.9 collective-permute-done.19.b
  144.2 2.2 %collective-permute-start.20 = (f32[160,256]{1,0:T(8,128)S(1)}, f32[160,256]{1,0:T(8,128)S(1)}, u32[]{:S(2)}, u32[]{:S(2)}) collective-permute-start(f32[160,256]{1,0:T(8,128)S(1)} %shard_map.175.a), channel_id=1, source_target_pairs={{0,3},{1,0},{2,1},{3,2},{4,7},{5,4},{6,5},{7,6},{8,11},{9,8},{10,9... | collective-permute-start | bytes 491528 | tf_op jit(solution)/shard_map/ppermute | solution.py:481
  147.1 1.2 shard_map.178
  148.3 1.2 shard_map.177
  150.1 3.1 %collective-permute-done.21.c = f32[160,256]{1,0:T(8,128)S(1)} collective-permute-done((f32[160,256]{1,0:T(8,128)S(1)}, f32[160,256]{1,0:T(8,128)S(1)}, u32[]{:S(2)}, u32[]{:S(2)}) %collective-permute-start.21) | collective-permute-done | bytes 163872 | tf_op jit(solution)/shard_map/ppermute | solution.py:481
  153.2 3.8 %collective-permute-done.22.d = f32[160,256]{1,0:T(8,128)S(1)} collective-permute-done((f32[160,256]{1,0:T(8,128)S(1)}, f32[160,256]{1,0:T(8,128)S(1)}, u32[]{:S(2)}, u32[]{:S(2)}) %collective-permute-start.22) | collective-permute-done | bytes 163872 | tf_op jit(solution)/shard_map/ppermute | solution.py:481
  157.0 2.2 %shard_map.176 = (bf16[128,2048]{1,0:T(8,128)(2,1)}, f32[64,64]{1,0:T(8,128)}, f32[64,64]{1,0:T(8,128)}) custom-call(s32[1]{0:T(128)} %bitcast.at, f32[160,256]{1,0:T(8,128)S(1)} %shard_map.175.a, f32[160,256]{1,0:T(8,128)S(1)} %collective-permute-done.20.b, f32[160,256]{1,0:T(8,128)S(1)} %collective-permute-done.21.c, ...), custom_call_target="tpu_custom_call" | custom-call | tf_op jit(solution)/shard_map/pallas_call | solution.py:107
  (64 shorter events, 8.1 us)
Async XLA Ops:
  0.6 30.9 %copy-start.10 = (bf16[64,64]{1,0:T(8,128)(2,1)S(1)}, bf16[64,64]{1,0:T(8,128)(2,1)}, u32[]{:S(2)}) copy-start(bf16[64,64]{1,0:T(8,128)(2,1)} %point.2) | copy-start | bytes 24580
  3.9 7.6 %collective-permute-start = (f32[128,256]{1,0:T(8,128)S(1)}, f32[128,256]{1,0:T(8,128)S(1)}, u32[]{:S(2)}, u32[]{:S(2)}) collective-permute-start(f32[128,256]{1,0:T(8,128)S(1)} %get-tuple-element.62), channel_id=1, source_target_pairs={{0,1},{1,2},{2,3},{3,0},{4,5},{5,6},{6,7},{7,4},{8,9},{9,10},{10,1... | collective-permute-start | bytes 393224 | tf_op jit(solution)/shard_map/ppermute | solution.py:481
  6.0 8.3 %collective-permute-start.1 = (f32[128,256]{1,0:T(8,128)S(1)}, f32[128,256]{1,0:T(8,128)S(1)}, u32[]{:S(2)}, u32[]{:S(2)}) collective-permute-start(f32[128,256]{1,0:T(8,128)S(1)} %get-tuple-element.63), channel_id=1, source_target_pairs={{0,2},{1,3},{2,0},{3,1},{4,6},{5,7},{6,4},{7,5},{8,10},{9,11},{10,... | collective-permute-start | bytes 393224 | tf_op jit(solution)/shard_map/ppermute | solution.py:481
  8.7 5.7 %collective-permute-start.2 = (f32[128,256]{1,0:T(8,128)S(1)}, f32[128,256]{1,0:T(8,128)S(1)}, u32[]{:S(2)}, u32[]{:S(2)}) collective-permute-start(f32[128,256]{1,0:T(8,128)S(1)} %get-tuple-element.64), channel_id=1, source_target_pairs={{0,3},{1,0},{2,1},{3,2},{4,7},{5,4},{6,5},{7,6},{8,11},{9,8},{10,9... | collective-permute-start | bytes 393224 | tf_op jit(solution)/shard_map/ppermute | solution.py:481
  9.7 1.0 copy-start.4
  10.8 3.6 %copy-start.1 = (bf16[4,128,128]{2,1,0:T(8,128)(2,1)S(1)}, bf16[4,128,128]{2,1,0:T(8,128)(2,1)}, u32[]{:S(2)}) copy-start(bf16[4,128,128]{2,1,0:T(8,128)(2,1)} %constant.26.clone.ty) | copy-start | bytes 393220
  10.8 20.8 %copy-start.7 = (bf16[8,16,2048]{2,1,0:T(8,128)(2,1)S(1)}, bf16[8,16,2048]{2,1,0:T(8,128)(2,1)}, u32[]{:S(2)}) copy-start(bf16[8,16,2048]{2,1,0:T(8,128)(2,1)} %param.13) | copy-start | bytes 1572868
  14.4 5.8 %copy-start.6 = (bf16[16,32,64]{2,1,0:T(8,128)(2,1)S(1)}, bf16[16,32,64]{2,1,0:T(8,128)(2,1)}, u32[]{:S(2)}) copy-start(bf16[16,32,64]{2,1,0:T(8,128)(2,1)} %constant.27.clone.tx) | copy-start | bytes 196612
  14.4 17.2 %copy-start.2 = (bf16[8,16,2048]{2,1,0:T(8,128)(2,1)S(1)}, bf16[8,16,2048]{2,1,0:T(8,128)(2,1)}, u32[]{:S(2)}) copy-start(bf16[8,16,2048]{2,1,0:T(8,128)(2,1)} %param.12) | copy-start | bytes 1572868
  14.4 17.2 %copy-start.5 = (bf16[128,2048]{1,0:T(8,128)(2,1)S(1)}, bf16[128,2048]{1,0:T(8,128)(2,1)}, u32[]{:S(2)}) copy-start(bf16[128,2048]{1,0:T(8,128)(2,1)} %get-tuple-element.70.dz) | copy-start | bytes 1572868
  14.6 2.7 %collective-permute-start.3 = (f32[64,256]{1,0:T(8,128)S(1)}, f32[64,256]{1,0:T(8,128)S(1)}, u32[]{:S(2)}, u32[]{:S(2)}) collective-permute-start(f32[64,256]{1,0:T(8,128)S(1)} %get-tuple-element.66), channel_id=1, source_target_pairs={{0,4},{4,0},{8,12},{12,8},{1,5},{5,1},{9,13},{13,9},{2,6},{6,2},{1... | collective-permute-start | bytes 196616 | tf_op jit(solution)/shard_map/ppermute | solution.py:481
  17.4 2.9 %collective-permute-start.4 = (f32[32,256]{1,0:T(8,128)S(1)}, f32[32,256]{1,0:T(8,128)S(1)}, u32[]{:S(2)}, u32[]{:S(2)}) collective-permute-start(f32[32,256]{1,0:T(8,128)S(1)} %get-tuple-element.68), channel_id=1, source_target_pairs={{0,8},{4,12},{8,0},{12,4},{1,9},{5,13},{9,1},{13,5},{2,10},{6,14},... | collective-permute-start | bytes 98312 | tf_op jit(solution)/shard_map/ppermute | solution.py:481
  21.0 19.6 %all-to-all-start = ((f32[16,4,256]{2,1,0:T(4,128)}), f32[16,4,256]{2,1,0:T(4,128)S(1)}, u32[]{:S(2)}, u32[]{:S(2)}) async-start(f32[16,4,256]{2,1,0:T(4,128)} %shard_map.159), calls=%async_computation | async-start | bytes 131072 | tf_op jit(solution)/shard_map/all_to_all | solution.py:505
  34.0 0.7 copy-start.12
  34.8 0.7 copy-start.14
  35.5 0.7 copy-start.16
  40.6 0.9 copy-start.8
  41.9 24.3 %copy-start.17 = (f32[128,512]{1,0:T(8,128)S(1)}, f32[128,512]{1,0:T(8,128)}, u32[]{:S(2)}) copy-start(f32[128,512]{1,0:T(8,128)} %copy-done.16) | copy-start | bytes 786436
  55.6 10.6 %copy-start.15 = (f32[128,512]{1,0:T(8,128)S(1)}, f32[128,512]{1,0:T(8,128)}, u32[]{:S(2)}) copy-start(f32[128,512]{1,0:T(8,128)} %copy-done.14) | copy-start | bytes 786436
  55.6 14.1 %copy-start.13 = (f32[128,512]{1,0:T(8,128)S(1)}, f32[128,512]{1,0:T(8,128)}, u32[]{:S(2)}) copy-start(f32[128,512]{1,0:T(8,128)} %copy-done.12) | copy-start | bytes 786436
  55.7 2.9 %collective-permute-start.5 = (f32[32,256]{1,0:T(8,128)S(1)}, f32[32,256]{1,0:T(8,128)S(1)}, u32[]{:S(2)}, u32[]{:S(2)}) collective-permute-start(f32[32,256]{1,0:T(8,128)S(1)} %shard_map.162.a), channel_id=1, source_target_pairs={{0,8},{4,12},{8,0},{12,4},{1,9},{5,13},{9,1},{13,5},{2,10},{6,14},... | collective-permute-start | bytes 98312 | tf_op jit(solution)/shard_map/ppermute | solution.py:481
  58.6 5.5 %collective-permute-start.6 = (f32[64,256]{1,0:T(8,128)S(1)}, f32[64,256]{1,0:T(8,128)S(1)}, u32[]{:S(2)}, u32[]{:S(2)}) collective-permute-start(f32[64,256]{1,0:T(8,128)S(1)} %shard_map.163.a), channel_id=1, source_target_pairs={{0,4},{4,0},{8,12},{12,8},{1,5},{5,1},{9,13},{13,9},{2,6},{6,2},{1... | collective-permute-start | bytes 196616 | tf_op jit(solution)/shard_map/ppermute | solution.py:481
  64.3 5.5 %collective-permute-start.7 = (f32[128,256]{1,0:T(8,128)S(1)}, f32[128,256]{1,0:T(8,128)S(1)}, u32[]{:S(2)}, u32[]{:S(2)}) collective-permute-start(f32[128,256]{1,0:T(8,128)S(1)} %shard_map.164.a), channel_id=1, source_target_pairs={{0,3},{1,0},{2,1},{3,2},{4,7},{5,4},{6,5},{7,6},{8,11},{9,8},{10,9... | collective-permute-start | bytes 393224 | tf_op jit(solution)/shard_map/ppermute | solution.py:481
  66.2 24.9 %collective-permute-start.13 = (f32[128,512]{1,0:T(8,128)S(1)}, f32[128,512]{1,0:T(8,128)S(1)}, u32[]{:S(2)}, u32[]{:S(2)}) collective-permute-start(f32[128,512]{1,0:T(8,128)S(1)} %copy-done.17), channel_id=1, source_target_pairs={{0,1},{1,2},{2,3},{3,0},{4,5},{5,6},{6,7},{7,4},{8,9},{9,10},{10,1... | collective-permute-start | bytes 786440 | tf_op jit(solution)/shard_map/ppermute | solution.py:481
  66.2 27.0 %collective-permute-start.14 = (f32[128,512]{1,0:T(8,128)S(1)}, f32[128,512]{1,0:T(8,128)S(1)}, u32[]{:S(2)}, u32[]{:S(2)}) collective-permute-start(f32[128,512]{1,0:T(8,128)S(1)} %copy-done.15), channel_id=1, source_target_pairs={{0,2},{1,3},{2,0},{3,1},{4,6},{5,7},{6,4},{7,5},{8,10},{9,11},{10,... | collective-permute-start | bytes 786440 | tf_op jit(solution)/shard_map/ppermute | solution.py:481
  68.1 14.2 %collective-permute-start.8 = (f32[128,256]{1,0:T(8,128)S(1)}, f32[128,256]{1,0:T(8,128)S(1)}, u32[]{:S(2)}, u32[]{:S(2)}) collective-permute-start(f32[128,256]{1,0:T(8,128)S(1)} %shard_map.164.a), channel_id=1, source_target_pairs={{0,2},{1,3},{2,0},{3,1},{4,6},{5,7},{6,4},{7,5},{8,10},{9,11},{10,... | collective-permute-start | bytes 393224 | tf_op jit(solution)/shard_map/ppermute | solution.py:481
  69.3 16.6 %collective-permute-start.9 = (f32[128,256]{1,0:T(8,128)S(1)}, f32[128,256]{1,0:T(8,128)S(1)}, u32[]{:S(2)}, u32[]{:S(2)}) collective-permute-start(f32[128,256]{1,0:T(8,128)S(1)} %shard_map.164.a), channel_id=1, source_target_pairs={{0,1},{1,2},{2,3},{3,0},{4,5},{5,6},{6,7},{7,4},{8,9},{9,10},{10,1... | collective-permute-start | bytes 393224 | tf_op jit(solution)/shard_map/ppermute | solution.py:481
  69.7 23.5 %collective-permute-start.15 = (f32[128,512]{1,0:T(8,128)S(1)}, f32[128,512]{1,0:T(8,128)S(1)}, u32[]{:S(2)}, u32[]{:S(2)}) collective-permute-start(f32[128,512]{1,0:T(8,128)S(1)} %copy-done.13), channel_id=1, source_target_pairs={{0,3},{1,0},{2,1},{3,2},{4,7},{5,4},{6,5},{7,6},{8,11},{9,8},{10,9... | collective-permute-start | bytes 786440 | tf_op jit(solution)/shard_map/ppermute | solution.py:481
  90.4 8.4 %collective-permute-start.10 = (f32[128,256]{1,0:T(8,128)S(1)}, f32[128,256]{1,0:T(8,128)S(1)}, u32[]{:S(2)}, u32[]{:S(2)}) collective-permute-start(f32[128,256]{1,0:T(8,128)S(1)} %get-tuple-element.85), channel_id=1, source_target_pairs={{0,1},{1,2},{2,3},{3,0},{4,5},{5,6},{6,7},{7,4},{8,9},{9,10},{10,1... | collective-permute-start | bytes 393224 | tf_op jit(solution)/shard_map/ppermute | solution.py:481
  90.5 8.4 %collective-permute-start.11 = (f32[128,256]{1,0:T(8,128)S(1)}, f32[128,256]{1,0:T(8,128)S(1)}, u32[]{:S(2)}, u32[]{:S(2)}) collective-permute-start(f32[128,256]{1,0:T(8,128)S(1)} %get-tuple-element.86), channel_id=1, source_target_pairs={{0,2},{1,3},{2,0},{3,1},{4,6},{5,7},{6,4},{7,5},{8,10},{9,11},{10,... | collective-permute-start | bytes 393224 | tf_op jit(solution)/shard_map/ppermute | solution.py:481
  91.2 2.3 %copy-start.3 = (bf16[128,2048]{1,0:T(8,128)(2,1)S(1)}, bf16[128,2048]{1,0:T(8,128)(2,1)}, u32[]{:S(2)}) copy-start(bf16[128,2048]{1,0:T(8,128)(2,1)} %get-tuple-element.101.dz) | copy-start | bytes 1572868
  91.2 7.7 %collective-permute-start.12 = (f32[128,256]{1,0:T(8,128)S(1)}, f32[128,256]{1,0:T(8,128)S(1)}, u32[]{:S(2)}, u32[]{:S(2)}) collective-permute-start(f32[128,256]{1,0:T(8,128)S(1)} %get-tuple-element.87), channel_id=1, source_target_pairs={{0,3},{1,0},{2,1},{3,2},{4,7},{5,4},{6,5},{7,6},{8,11},{9,8},{10,9... | collective-permute-start | bytes 393224 | tf_op jit(solution)/shard_map/ppermute | solution.py:481
  99.0 3.4 %collective-permute-start.16 = (f32[64,1024]{1,0:T(8,128)S(1)}, f32[64,1024]{1,0:T(8,128)S(1)}, u32[]{:S(2)}, u32[]{:S(2)}) collective-permute-start(f32[64,1024]{1,0:T(8,128)S(1)} %get-tuple-element.96), channel_id=1, source_target_pairs={{0,4},{4,0},{8,12},{12,8},{1,5},{5,1},{9,13},{13,9},{2,6},{6,2},{1... | collective-permute-start | bytes 786440 | tf_op jit(solution)/shard_map/ppermute | solution.py:481
  102.5 4.8 %collective-permute-start.17 = (f32[32,1024]{1,0:T(8,128)S(1)}, f32[32,1024]{1,0:T(8,128)S(1)}, u32[]{:S(2)}, u32[]{:S(2)}) collective-permute-start(f32[32,1024]{1,0:T(8,128)S(1)} %get-tuple-element.98), channel_id=1, source_target_pairs={{0,8},{4,12},{8,0},{12,4},{1,9},{5,13},{9,1},{13,5},{2,10},{6,14},... | collective-permute-start | bytes 393224 | tf_op jit(solution)/shard_map/ppermute | solution.py:481
  107.5 14.1 %copy-start.9 = (bf16[1,4,4,4096]{3,2,1,0:T(4,128)(2,1)S(1)}, bf16[1,4,4,4096]{3,2,1,0:T(4,128)(2,1)}, u32[]{:S(2)}) copy-start(bf16[1,4,4,4096]{3,2,1,0:T(4,128)(2,1)} %spectral.3) | copy-start | bytes 393220
  122.6 3.7 %copy-start.11 = (bf16[64,64]{1,0:T(8,128)(2,1)S(1)}, bf16[64,64]{1,0:T(8,128)(2,1)}, u32[]{:S(2)}) copy-start(bf16[64,64]{1,0:T(8,128)(2,1)} %point.3) | copy-start | bytes 24580
  122.6 13.2 %all-to-all-start.3 = ((f32[16,4,384]{2,1,0:T(4,128)}), f32[16,4,384]{2,1,0:T(4,128)S(1)}, u32[]{:S(2)}, u32[]{:S(2)}) async-start(f32[16,4,384]{2,1,0:T(4,128)} %get-tuple-element.100), calls=%async_computation.3 | async-start | bytes 196608 | tf_op jit(solution)/shard_map/all_to_all | solution.py:505
  135.9 2.9 %collective-permute-start.18 = (f32[32,256]{1,0:T(8,128)S(1)}, f32[32,256]{1,0:T(8,128)S(1)}, u32[]{:S(2)}, u32[]{:S(2)}) collective-permute-start(f32[32,256]{1,0:T(8,128)S(1)} %get-tuple-element.103.a), channel_id=1, source_target_pairs={{0,8},{4,12},{8,0},{12,4},{1,9},{5,13},{9,1},{13,5},{2,10},{6,14},... | collective-permute-start | bytes 98312 | tf_op jit(solution)/shard_map/ppermute | solution.py:481
  138.8 5.2 %collective-permute-start.19 = (f32[64,256]{1,0:T(8,128)S(1)}, f32[64,256]{1,0:T(8,128)S(1)}, u32[]{:S(2)}, u32[]{:S(2)}) collective-permute-start(f32[64,256]{1,0:T(8,128)S(1)} %shard_map.174.a), channel_id=1, source_target_pairs={{0,4},{4,0},{8,12},{12,8},{1,5},{5,1},{9,13},{13,9},{2,6},{6,2},{1... | collective-permute-start | bytes 196616 | tf_op jit(solution)/shard_map/ppermute | solution.py:481
  144.2 5.9 %collective-permute-start.20 = (f32[160,256]{1,0:T(8,128)S(1)}, f32[160,256]{1,0:T(8,128)S(1)}, u32[]{:S(2)}, u32[]{:S(2)}) collective-permute-start(f32[160,256]{1,0:T(8,128)S(1)} %shard_map.175.a), channel_id=1, source_target_pairs={{0,3},{1,0},{2,1},{3,2},{4,7},{5,4},{6,5},{7,6},{8,11},{9,8},{10,9... | collective-permute-start | bytes 491528 | tf_op jit(solution)/shard_map/ppermute | solution.py:481
  146.4 6.7 %collective-permute-start.21 = (f32[160,256]{1,0:T(8,128)S(1)}, f32[160,256]{1,0:T(8,128)S(1)}, u32[]{:S(2)}, u32[]{:S(2)}) collective-permute-start(f32[160,256]{1,0:T(8,128)S(1)} %shard_map.175.a), channel_id=1, source_target_pairs={{0,2},{1,3},{2,0},{3,1},{4,6},{5,7},{6,4},{7,5},{8,10},{9,11},{10,... | collective-permute-start | bytes 491528 | tf_op jit(solution)/shard_map/ppermute | solution.py:481
  146.4 10.6 %collective-permute-start.22 = (f32[160,256]{1,0:T(8,128)S(1)}, f32[160,256]{1,0:T(8,128)S(1)}, u32[]{:S(2)}, u32[]{:S(2)}) collective-permute-start(f32[160,256]{1,0:T(8,128)S(1)} %shard_map.175.a), channel_id=1, source_target_pairs={{0,1},{1,2},{2,3},{3,0},{4,5},{5,6},{6,7},{7,4},{8,9},{9,10},{10,1... | collective-permute-start | bytes 491528 | tf_op jit(solution)/shard_map/ppermute | solution.py:481
  147.1 9.9 %copy-start = (f32[128,2048]{1,0:T(8,128)S(1)}, f32[128,2048]{1,0:T(8,128)}, u32[]{:S(2)}) copy-start(f32[128,2048]{1,0:T(8,128)} %shard_map.172.local) | copy-start | bytes 3145732

commit v4 on v3

--- a/solution.py
+++ b/solution.py
@@ -49,14 +49,23 @@
         for x in range(CELLS_X):
             ty[d, :, x, :, x, :] = small
     ty = ty.reshape(DEV_Y, ROWS, ROWS)
+    flat = np.zeros((DEV_Y, CELLS_X, 16, CELLS_X, CELLS_Y), np.float32)
+    for d in range(DEV_Y):
+        for x in range(CELLS_X):
+            flat[d, x, :, x] = cas(np.arange(16)[:, None], CELLS_Y * DEV_Y, y * DEV_Y + d)
+    flat = flat.reshape(DEV_Y, ROWS, ROWS)
     x = np.arange(CELLS_X)
     tx = np.zeros((DEV_X, 16, 4, CELLS_X, 4), np.float32)
+    few = np.zeros((DEV_X, 16, CELLS_X), np.float32)
     for d in range(DEV_X):
         small = cas(np.arange(16)[:, None], CELLS_X * DEV_X, x * DEV_X + d)
+        few[d] = small
         for l in range(4):
             tx[d, :, l, :, l] = small
     tx = tx.reshape(DEV_X, 64, CELLS_X * 4).transpose(0, 2, 1)
-    return tuple(t.astype(bf16) for t in (tz, tz_back, ty, tx))
+    return tuple(t.astype(bf16) for t in (tz, tz_back, ty, flat, tx)) + (
+        few.reshape(DEV_X, 128).astype(bf16).astype(np.float32),
+    )
 
 
 def dot(left, right):
@@ -199,7 +208,11 @@
         leave(b).wait()
 
 
-def own_kernel(at, mine, dz, p0, fold, ka):
+def own_kernel(at, mine, dz, few, p0, fold, coef, ka):
+    side = lax.broadcasted_iota(jnp.int32, (128, 128), 0)
+    same = jnp.where(side == lax.broadcasted_iota(jnp.int32, (128, 128), 1), 1.0, 0.0)
+    same = (same * few[pl.ds(at_x(at), 1), :]).astype(bf16)
+    coef[...] = dot(same, jnp.ones((128, 128), bf16))
     for b in range(8):
         fill_table(ka, mine, b, 256)
     p0[...] = dot(dz[...], ka[...])
@@ -287,6 +300,41 @@
     return (refs[0][...] + refs[1][...]) + (refs[2][...] + refs[3][...])
 
 
+def factor(coef, k, x):
+    c = coef[k * 8 + x : k * 8 + x + 1, :]
+    return jnp.concatenate([c, c], axis=1)
+
+
+def along_yx_kernel(at, a, b, c, d, flat, coef, out):
+    v = table_dot(flat[at_y(at)], total_of((a, b, c, d)))
+    for k in range(16):
+        here = factor(coef, k, 0) * v[:16]
+        for x in range(1, 8):
+            here = here + factor(coef, k, x) * v[x * 16 : (x + 1) * 16]
+        for g in range(4):
+            out[k * 4 + g] = here[g * 4 : (g + 1) * 4]
+
+
+def back_xy(at, got, flat, coef, tall):
+    for k in range(16):
+        here = jnp.concatenate([got[k * 4 + g, :, :256] for g in range(4)], axis=0)
+        for x in range(8):
+            rows = slice(x * 16, (x + 1) * 16)
+            more = factor(coef, k, x) * here
+            tall[rows] = more if k == 0 else tall[rows] + more
+    return table_dot_tn(flat[at_y(at)], tall[...])
+
+
+def back_xy_kernel(at, got, flat, coef, out, tall):
+    out[...] = back_xy(at, got, flat, coef, tall)
+
+
+def back_xy_one_kernel(at, got, flat, coef, out, tall):
+    out[:ROWS] = back_xy(at, got, flat, coef, tall)
+    weight = jnp.concatenate([got[k * 4, :, 256:] for k in range(16)], axis=0)
+    out[ROWS:] = jnp.concatenate([weight[:32], weight[32:]], axis=1)
+
+
 def along_y_kernel(at, a, b, c, d, ty, near, far):
     out = table_dot(ty[at_y(at)], total_of((a, b, c, d)))
     near[...] = out[:64]
@@ -309,11 +357,6 @@
     send[:, :wide] = v[32:, :wide]
     if v.shape[1] > 768:
         send[:, 768:] = v[:32, 768:]
-
-
-def pair_kernel(at, a, b, out):
-    out[:32] = a[...]
-    out[32:] = b[...]
 
 
 def along_x_kernel(at, a, b, tx, out):
@@ -340,29 +383,29 @@
     return jnp.concatenate([out[k * 4 : (k + 1) * 4] for k in range(4)], axis=1)
 
 
-def sixteen(got):
-    v = [got[i] for i in range(16)]
+def sum_of(got):
+    v = [got[i] for i in range(got.shape[0])]
     while len(v) > 1:
         v = [v[i] + v[i + 1] for i in range(0, len(v), 2)]
     return v[0]
 
 
 def mix_two_kernel(at, got, spectral, fold, back, hat_out, wide):
-    hat = sixteen(got) * SCALE_B
+    hat = sum_of(got) * SCALE_B
     hat_out[...] = hat
     out = mixed(hat, spectral, wide, fold)
-    for i in range(16):
+    for i in range(64):
         back[i] = out
 
 
 def mix_one_kernel(at, got, spectral, fold, back, hat_out, mid_out, first_out, wide):
-    v = sixteen(got)
+    v = sum_of(got)
     hat = v[:, :256] * SCALE_B
     hat_out[...] = hat
     mid_out[...] = v[:, 256:512] * SCALE_A
     first_out[...] = v[:, 512:768] * SCALE_A
     out = mixed(hat, spectral, wide, fold)
-    for i in range(16):
+    for i in range(64):
         back[i, :, :256] = out
         back[i, :, 256:] = v[:, 768:]
 
@@ -384,28 +427,6 @@
     whole = whole * jnp.concatenate([tall] * 32, axis=1)
     for k in range(4):
         out[:, k, :] = whole[k * 4 : (k + 1) * 4]
-
-
-def back_x_kernel(at, got, tx, out):
-    v = jnp.concatenate([got[i] for i in range(16)], axis=0)
-    out[...] = table_dot(tx[at_x(at)], v)
-
-
-def back_x_one_kernel(at, got, tx, out, weight):
-    v = jnp.concatenate([got[i] for i in range(16)], axis=0)
-    out[...] = table_dot(tx[at_x(at)], v[:, :256])
-    weight[...] = jnp.concatenate([v[:32, 256:], v[32:, 256:]], axis=1)
-
-
-def back_y_kernel(at, a, b, ty, out):
-    v = jnp.concatenate([a[...], b[...]], axis=0)
-    out[...] = table_dot_tn(ty[at_y(at)], v)
-
-
-def back_y_one_kernel(at, a, b, ty, weight, out):
-    v = jnp.concatenate([a[...], b[...]], axis=0)
-    out[:ROWS] = table_dot_tn(ty[at_y(at)], v)
-    out[ROWS:] = weight[...]
 
 
 def stack_modes(refs, modes):
@@ -496,19 +517,14 @@
     return keep, shifted(send, "gy", 2)
 
 
-def spread_y(at, v):
-    (pair,) = call(pair_kernel, [((64, 256), f32)], at, v, shifted(v, "gy", 2))
-    return pair, shifted(pair, "gy", 1)
-
-
-def over_x(v):
-    return lax.all_to_all(v, "gz", 0, 0, tiled=True)
+def over(v, axes):
+    return lax.all_to_all(v, axes, 0, 0, tiled=True)
 
 
 def on_device(
     grid_input, pre_one, pre_two, grad_output, spectral_one, spectral_two, point_one, point_two
 ):
-    tz, tz_back, ty, tx = [jnp.asarray(t) for t in build_tables()]
+    tz, tz_back, ty, flat, tx, few = [jnp.asarray(t) for t in build_tables()]
     at = lax.axis_index(("gz", "gy", "gx")).reshape(1)
     first, pre_one, pre_two, upstream = [
         t.reshape(ROWS, WIDE) for t in (grid_input, pre_one, pre_two, grad_output)
@@ -540,18 +556,17 @@
             dma((26,)),
         ],
     )
-    own, fold = call(
+    own, fold, coef = call(
         own_kernel,
-        [half, ((C * C, C), bf16)],
+        [half, ((C * C, C), bf16), ((128, 128), f32)],
         at,
         mine,
         dz_two,
+        few,
         scratch=[((WIDE, 256), bf16)],
     )
     got = exchange([own] + parts, "gx")
-    near, far = call(along_y_kernel, [((64, 256), f32)] * 2, at, *got, ty)
-    got = reduce_y(at, near, far, 256)
-    (modes,) = call(along_x_kernel, [((16, 4, 256), f32)], at, *got, tx)
+    (modes,) = call(along_yx_kernel, [((64, 4, 256), f32)], at, *got, flat, coef)
     modes, pre_one, dz_side = lax.optimization_barrier((modes, pre_one, dz_two))
     slope, local_two, weight_two, *ins = call(
         side_kernel,
@@ -574,22 +589,20 @@
             dma((16,)),
         ],
     )
-    got = over_x(modes)
+    got = over(modes, ("gz", "gy"))
     got, ins = lax.optimization_barrier((got, ins))
     got_in = exchange(ins, "gx")
     back, hat_two = call(
         mix_two_kernel,
-        [((16, 4, 256), f32), ((4, 256), f32)],
+        [((64, 4, 256), f32), ((4, 256), f32)],
         at,
         got,
         spectral_two,
         fold,
         scratch=[native],
     )
-    got = over_x(back)
-    (tall,) = call(back_x_kernel, [((32, 256), f32)], at, got, tx)
-    got = spread_y(at, tall)
-    (tall,) = call(back_y_kernel, [half], at, *got, ty)
+    got = over(back, ("gz", "gy"))
+    (tall,) = call(back_xy_kernel, [half], at, got, flat, coef, scratch=[half])
     got = spread(tall, "gx")
     ins = call(along_y_kernel, [((64, 512), f32)] * 2, at, *got_in, ty)
     dz_one, *parts = call(
@@ -630,9 +643,9 @@
     (modes,) = call(along_x_kernel, [((16, 4, 896), f32)], at, *got, tx)
     back, hat_one, mid_hat, first_hat = call(
         mix_one_kernel,
-        [((16, 4, 384), f32)] + [((4, 256), f32)] * 3,
-        at,
-        over_x(modes),
+        [((64, 4, 384), f32)] + [((4, 256), f32)] * 3,
+        at,
+        over(modes, "gz"),
         spectral_one,
         fold,
         scratch=[native],
@@ -648,11 +661,11 @@
         point_one,
         scratch=[((256, 256), bf16), (big, f32), dma((8,))],
     )
-    got = over_x(back)
+    got = over(back, ("gz", "gy"))
     got, local_one = lax.optimization_barrier((got, local_one))
-    tall, weight = call(back_x_one_kernel, [((32, 256), f32)] * 2, at, got, tx)
-    got = spread_y(at, tall)
-    (tall,) = call(back_y_one_kernel, [((ROWS + 32, 256), f32)], at, *got, ty, weight)
+    (tall,) = call(
+        back_xy_one_kernel, [((ROWS + 32, 256), f32)], at, got, flat, coef, scratch=[half]
+    )
     got = spread(tall, "gx")
     input_grad, weight_two, weight_one = call(
         end_kernel,

time: 160 us -> 155 us (0.969)
  starting transfers between devices: 50.7 us -> 43.9 us
  blocking collectives: 27.6 us -> 34.2 us
  waiting for transfers between devices: 54.4 us -> 49.9 us
    ppermute x23 -> x17, starting transfers between devices: 36.6 us -> 24.2 us  [shifted(): return lax.ppermute(v, axis, pairs)]
    ppermute x23 -> x17, waiting for transfers between devices: 41.9 us -> 29.9 us  [shifted(): return lax.ppermute(v, axis, pairs)]
    all_to_all x2, waiting for transfers between devices: 12.6 us -> 20 us  [over(): return lax.all_to_all(v, axes, 0, 0, tiled=True)]
    all_to_all x2, blocking collectives: 27.6 us -> 34.2 us  [over(): return lax.all_to_all(v, axes, 0, 0, tiled=True)]
    all_to_all x2, starting transfers between devices: 14.2 us -> 19.7 us  [over(): return lax.all_to_all(v, axes, 0, 0, tiled=True)]
    pallas_call x24 -> x18, Pallas kernels: 21.3 us -> 21.4 us  [call(): pl.pallas_call(body, out_shape=shapes, in_specs=[pl.BlockSpec(memory_spac...]
    unnamed x36 -> x44, local copies, waits for them, and re-layouts: 4.11 us -> 4.1 us
  transfers between devices with their start and end apart: 25 -> 19, of which waited for: 17 -> 12; matrix products, arithmetic and copies ran while one was open for 0% -> 0% of each run, Pallas kernels for 8% -> 8%
where the time goes in v4:
time: 155 us
  waiting for transfers between devices  49.9 us (32%)
  starting transfers between devices  43.9 us (28%)
  blocking collectives  34.2 us (22%)
  Pallas kernels  21.4 us (14%)
  local copies, waits for them, and re-layouts  4.1 us (3%)
    all_to_all x2, blocking collectives, over(): return lax.all_to_all(v, axes, 0, 0, tiled=True)  34.2 us
    ppermute x17, waiting for transfers between devices, shifted(): return lax.ppermute(v, axis, pairs)  29.9 us
    ppermute x17, starting transfers between devices, shifted(): return lax.ppermute(v, axis, pairs)  24.2 us
    pallas_call x18, Pallas kernels, call(): pl.pallas_call(body, out_shape=shapes, in_specs=[pl.BlockSpec(memory_spac...  21.4 us
    all_to_all x2, waiting for transfers between devices, over(): return lax.all_to_all(v, axes, 0, 0, tiled=True)  20 us
    all_to_all x2, starting transfers between devices, over(): return lax.all_to_all(v, axes, 0, 0, tiled=True)  19.7 us
    unnamed x44, local copies, waits for them, and re-layouts  4.1 us
  transfers between devices with their start and end apart: 19, of which 12 were waited for; matrix products, arithmetic and copies ran while one was open for 0% of the time, Pallas kernels for 8%

profile of v4, /device:TPU:1, one launch (start us, length us, event | category | flops | bytes accessed | tf_op | source)
XLA Modules:
  0.0 154.6 jit_solution(9545295023617176589)
XLA Ops:
  0.6 3.2 %shard_map.173 = (bf16[128,2048]{1,0:T(8,128)(2,1)}, f32[128,256]{1,0:T(8,128)S(1)}, f32[128,256]{1,0:T(8,128)S(1)}, f32[128,256]{1,0:T(8,128)S(1)}, f32[32,1024]{1,0:T(8,128)S(1)}, /*index=5*/f32[16,2048]{1,0:T(8,128)S(1)}) custom-call(s32[1]{0:T(128)} %bitcast.at, bf16[128,2048]{1,0:T(8,128)(2,1)} %bitcast.11, bf16[128,2048]{1,0:T(8,128)(2,1)} %bitcast.12, ...), custom_call_target="tpu_custom_call" | custom-call | tf_op jit(solution)/shard_map/pallas_call | solution.py:116
  3.9 2.2 %collective-permute-start = (f32[128,256]{1,0:T(8,128)S(1)}, f32[128,256]{1,0:T(8,128)S(1)}, u32[]{:S(2)}, u32[]{:S(2)}) collective-permute-start(f32[128,256]{1,0:T(8,128)S(1)} %get-tuple-element.57), channel_id=1, source_target_pairs={{0,1},{1,2},{2,3},{3,0},{4,5},{5,6},{6,7},{7,4},{8,9},{9,10},{10,1... | collective-permute-start | bytes 393224 | tf_op jit(solution)/shard_map/ppermute | solution.py:502
  6.1 2.6 %collective-permute-start.1 = (f32[128,256]{1,0:T(8,128)S(1)}, f32[128,256]{1,0:T(8,128)S(1)}, u32[]{:S(2)}, u32[]{:S(2)}) collective-permute-start(f32[128,256]{1,0:T(8,128)S(1)} %get-tuple-element.58), channel_id=1, source_target_pairs={{0,2},{1,3},{2,0},{3,1},{4,6},{5,7},{6,4},{7,5},{8,10},{9,11},{10,... | collective-permute-start | bytes 393224 | tf_op jit(solution)/shard_map/ppermute | solution.py:502
  8.7 1.1 collective-permute-start.2
  9.7 1.0 copy-done.3
  10.8 0.6 shard_map.174
  11.4 3.0 %collective-permute-done.1.c = f32[128,256]{1,0:T(8,128)S(1)} collective-permute-done((f32[128,256]{1,0:T(8,128)S(1)}, f32[128,256]{1,0:T(8,128)S(1)}, u32[]{:S(2)}, u32[]{:S(2)}) %collective-permute-start.1) | collective-permute-done | bytes 131104 | tf_op jit(solution)/shard_map/ppermute | solution.py:502
  14.4 1.1 shard_map.175
  15.5 13.1 %all-to-all-start = ((f32[64,4,256]{2,1,0:T(4,128)}), f32[64,4,256]{2,1,0:T(4,128)S(1)}, u32[]{:S(2)}, u32[]{:S(2)}) async-start(f32[64,4,256]{2,1,0:T(4,128)} %shard_map.175), calls=%async_computation | async-start | bytes 524288 | tf_op jit(solution)/shard_map/all_to_all | solution.py:521
  28.7 2.4 %shard_map.176 = (f32[128,2048]{1,0:T(8,128)}, f32[128,2048]{1,0:T(8,128)}, f32[64,64]{1,0:T(8,128)S(1)}, f32[128,512]{1,0:T(8,128)S(1)}, f32[128,512]{1,0:T(8,1...) custom-call(s32[1]{0:T(128)} %bitcast.at, bf16[128,2048]{1,0:T(8,128)(2,1)S(1)} %bitcast.10, ...), custom_call_target="tpu_custom_call" | custom-call | tf_op jit(solution)/shard_map/pallas_call | solution.py:116
  31.1 0.7 copy-done.8
  31.8 0.7 copy-done.16
  32.5 0.7 copy-done.18
  33.2 0.7 copy-done.20
  33.9 6.7 %all-to-all-done.got = f32[64,4,256]{2,1,0:T(4,128)S(1)} async-done(((f32[64,4,256]{2,1,0:T(4,128)}), f32[64,4,256]{2,1,0:T(4,128)S(1)}, u32[]{:S(2)}, u32[]{:S(2)}) %all-to-all-start) | async-done | bytes 262176 | tf_op jit(solution)/shard_map/all_to_all | solution.py:521
  40.6 0.4 shard_map.177
  41.1 17.9 %all_to_all.20.got = f32[64,4,256]{2,1,0:T(4,128)S(1)} all-to-all(f32[64,4,256]{2,1,0:T(4,128)S(1)} %get-tuple-element.72), channel_id=1, replica_groups=mesh['gz'=16,'gy'=4,'gx'=4] {'gz','gy'}, dimensions={0} | all-to-all | bytes 524288 | tf_op jit(solution)/shard_map/all_to_all | solution.py:521
  59.3 1.9 %collective-permute-start.3 = (f32[128,256]{1,0:T(8,128)S(1)}, f32[128,256]{1,0:T(8,128)S(1)}, u32[]{:S(2)}, u32[]{:S(2)}) collective-permute-start(f32[128,256]{1,0:T(8,128)S(1)} %shard_map.178.a), channel_id=1, source_target_pairs={{0,3},{1,0},{2,1},{3,2},{4,7},{5,4},{6,5},{7,6},{8,11},{9,8},{10,9... | collective-permute-start | bytes 393224 | tf_op jit(solution)/shard_map/ppermute | solution.py:502
  61.3 0.9 collective-permute-start.10
  62.1 1.1 collective-permute-start.11
  63.3 1.1 collective-permute-start.4
  64.3 0.8 collective-permute-start.5
  65.1 0.8 collective-permute-start.9
  65.9 6.8 %collective-permute-done.4.c = f32[128,256]{1,0:T(8,128)S(1)} collective-permute-done((f32[128,256]{1,0:T(8,128)S(1)}, f32[128,256]{1,0:T(8,128)S(1)}, u32[]{:S(2)}, u32[]{:S(2)}) %collective-permute-start.4) | collective-permute-done | bytes 131104 | tf_op jit(solution)/shard_map/ppermute | solution.py:502
  72.8 3.9 %collective-permute-done.5.d = f32[128,256]{1,0:T(8,128)S(1)} collective-permute-done((f32[128,256]{1,0:T(8,128)S(1)}, f32[128,256]{1,0:T(8,128)S(1)}, u32[]{:S(2)}, u32[]{:S(2)}) %collective-permute-start.5) | collective-permute-done | bytes 131104 | tf_op jit(solution)/shard_map/ppermute | solution.py:502
  76.6 4.5 %shard_map.179 = (bf16[128,2048]{1,0:T(8,128)(2,1)}, f32[128,256]{1,0:T(8,128)S(1)}, f32[128,256]{1,0:T(8,128)S(1)}, f32[128,256]{1,0:T(8,128)S(1)}) custom-call(s32[1]{0:T(128)} %bitcast.at, f32[128,2048]{1,0:T(8,128)} %get-tuple-element.63.local_from, f32[128,2048]{1,0:T(8,128)} %get-tuple-element.64.slope_from, f32[128,256]{1,0:T(8,128)S(1)} %shard_map.178.a, ...), custom_call_target="tpu_custom_call" | custom-call | tf_op jit(solution)/shard_map/pallas_call | solution.py:116
  81.2 3.2 %collective-permute-start.6 = (f32[128,256]{1,0:T(8,128)S(1)}, f32[128,256]{1,0:T(8,128)S(1)}, u32[]{:S(2)}, u32[]{:S(2)}) collective-permute-start(f32[128,256]{1,0:T(8,128)S(1)} %get-tuple-element.77), channel_id=1, source_target_pairs={{0,1},{1,2},{2,3},{3,0},{4,5},{5,6},{6,7},{7,4},{8,9},{9,10},{10,1... | collective-permute-start | bytes 393224 | tf_op jit(solution)/shard_map/ppermute | solution.py:502
  84.4 1.9 %collective-permute-start.7 = (f32[128,256]{1,0:T(8,128)S(1)}, f32[128,256]{1,0:T(8,128)S(1)}, u32[]{:S(2)}, u32[]{:S(2)}) collective-permute-start(f32[128,256]{1,0:T(8,128)S(1)} %get-tuple-element.78), channel_id=1, source_target_pairs={{0,2},{1,3},{2,0},{3,1},{4,6},{5,7},{6,4},{7,5},{8,10},{9,11},{10,... | collective-permute-start | bytes 393224 | tf_op jit(solution)/shard_map/ppermute | solution.py:502
  86.3 0.5 collective-permute-start.8
  87.4 0.7 shard_map.180
  88.1 2.9 %collective-permute-done.7.c = f32[128,256]{1,0:T(8,128)S(1)} collective-permute-done((f32[128,256]{1,0:T(8,128)S(1)}, f32[128,256]{1,0:T(8,128)S(1)}, u32[]{:S(2)}, u32[]{:S(2)}) %collective-permute-start.7) | collective-permute-done | bytes 131104 | tf_op jit(solution)/shard_map/ppermute | solution.py:502
  91.1 0.8 collective-permute-done.8.d
  92.1 1.8 %collective-permute-start.12 = (f32[64,1024]{1,0:T(8,128)S(1)}, f32[64,1024]{1,0:T(8,128)S(1)}, u32[]{:S(2)}, u32[]{:S(2)}) collective-permute-start(f32[64,1024]{1,0:T(8,128)S(1)} %get-tuple-element.88), channel_id=1, source_target_pairs={{0,4},{4,0},{8,12},{12,8},{1,5},{5,1},{9,13},{13,9},{2,6},{6,2},{1... | collective-permute-start | bytes 786440 | tf_op jit(solution)/shard_map/ppermute | solution.py:502
  93.9 1.2 collective-permute-done.12.got
  95.1 1.3 collective-permute-start.13
  96.4 3.4 %collective-permute-done.13.b = f32[32,1024]{1,0:T(8,128)S(1)} collective-permute-done((f32[32,1024]{1,0:T(8,128)S(1)}, f32[32,1024]{1,0:T(8,128)S(1)}, u32[]{:S(2)}, u32[]{:S(2)}) %collective-permute-start.13) | collective-permute-done | bytes 131104 | tf_op jit(solution)/shard_map/ppermute | solution.py:502
  100.1 16.2 %all_to_all.21.got = f32[16,4,896]{2,1,0:T(4,128)S(1)} all-to-all(f32[16,4,896]{2,1,0:T(4,128)S(1)} %shard_map.184), channel_id=1, replica_groups=mesh['gz'=16,'gy'=4,'gx'=4] {'gz'}, dimensions={0} | all-to-all | bytes 458752 | tf_op jit(solution)/shard_map/all_to_all | solution.py:521
  116.4 1.2 shard_map.185
  117.5 6.6 %all-to-all-start.3 = ((f32[64,4,384]{2,1,0:T(4,128)}), f32[64,4,384]{2,1,0:T(4,128)S(1)}, u32[]{:S(2)}, u32[]{:S(2)}) async-start(f32[64,4,384]{2,1,0:T(4,128)} %get-tuple-element.92), calls=%async_computation.3 | async-start | bytes 786432 | tf_op jit(solution)/shard_map/all_to_all | solution.py:521
  124.2 1.4 shard_map.186.local
  125.5 13.3 %all-to-all-done.3.got = f32[64,4,384]{2,1,0:T(4,128)S(1)} async-done(((f32[64,4,384]{2,1,0:T(4,128)}), f32[64,4,384]{2,1,0:T(4,128)S(1)}, u32[]{:S(2)}, u32[]{:S(2)}) %all-to-all-start.3) | async-done | bytes 393248 | tf_op jit(solution)/shard_map/all_to_all | solution.py:521
  139.2 2.0 %collective-permute-start.14 = (f32[160,256]{1,0:T(8,128)S(1)}, f32[160,256]{1,0:T(8,128)S(1)}, u32[]{:S(2)}, u32[]{:S(2)}) collective-permute-start(f32[160,256]{1,0:T(8,128)S(1)} %shard_map.187.a), channel_id=1, source_target_pairs={{0,3},{1,0},{2,1},{3,2},{4,7},{5,4},{6,5},{7,6},{8,11},{9,8},{10,9... | collective-permute-start | bytes 491528 | tf_op jit(solution)/shard_map/ppermute | solution.py:502
  141.1 0.9 collective-permute-start.15
  142.0 1.2 shard_map.190
  143.2 1.2 shard_map.189
  144.6 3.1 %collective-permute-done.15.c = f32[160,256]{1,0:T(8,128)S(1)} collective-permute-done((f32[160,256]{1,0:T(8,128)S(1)}, f32[160,256]{1,0:T(8,128)S(1)}, u32[]{:S(2)}, u32[]{:S(2)}) %collective-permute-start.15) | collective-permute-done | bytes 163872 | tf_op jit(solution)/shard_map/ppermute | solution.py:502
  147.7 4.5 %collective-permute-done.16.d = f32[160,256]{1,0:T(8,128)S(1)} collective-permute-done((f32[160,256]{1,0:T(8,128)S(1)}, f32[160,256]{1,0:T(8,128)S(1)}, u32[]{:S(2)}, u32[]{:S(2)}) %collective-permute-start.16) | collective-permute-done | bytes 163872 | tf_op jit(solution)/shard_map/ppermute | solution.py:502
  152.3 2.2 %shard_map.188 = (bf16[128,2048]{1,0:T(8,128)(2,1)}, f32[64,64]{1,0:T(8,128)}, f32[64,64]{1,0:T(8,128)}) custom-call(s32[1]{0:T(128)} %bitcast.at, f32[160,256]{1,0:T(8,128)S(1)} %shard_map.187.a, f32[160,256]{1,0:T(8,128)S(1)} %collective-permute-done.14.b, f32[160,256]{1,0:T(8,128)S(1)} %collective-permute-done.15.c, ...), custom_call_target="tpu_custom_call" | custom-call | tf_op jit(solution)/shard_map/pallas_call | solution.py:116
  (54 shorter events, 1.9 us)
Async XLA Ops:
  3.8 5.9 %copy-start.15 = (f32[16,128]{1,0:T(8,128)S(1)}, f32[16,128]{1,0:T(8,128)}, u32[]{:S(2)}) copy-start(f32[16,128]{1,0:T(8,128)} %constant.33.clone.few) | copy-start | bytes 24580
  3.9 7.6 %collective-permute-start = (f32[128,256]{1,0:T(8,128)S(1)}, f32[128,256]{1,0:T(8,128)S(1)}, u32[]{:S(2)}, u32[]{:S(2)}) collective-permute-start(f32[128,256]{1,0:T(8,128)S(1)} %get-tuple-element.57), channel_id=1, source_target_pairs={{0,1},{1,2},{2,3},{3,0},{4,5},{5,6},{6,7},{7,4},{8,9},{9,10},{10,1... | collective-permute-start | bytes 393224 | tf_op jit(solution)/shard_map/ppermute | solution.py:502
  6.1 8.3 %collective-permute-start.1 = (f32[128,256]{1,0:T(8,128)S(1)}, f32[128,256]{1,0:T(8,128)S(1)}, u32[]{:S(2)}, u32[]{:S(2)}) collective-permute-start(f32[128,256]{1,0:T(8,128)S(1)} %get-tuple-element.58), channel_id=1, source_target_pairs={{0,2},{1,3},{2,0},{3,1},{4,6},{5,7},{6,4},{7,5},{8,10},{9,11},{10,... | collective-permute-start | bytes 393224 | tf_op jit(solution)/shard_map/ppermute | solution.py:502
  8.7 5.7 %collective-permute-start.2 = (f32[128,256]{1,0:T(8,128)S(1)}, f32[128,256]{1,0:T(8,128)S(1)}, u32[]{:S(2)}, u32[]{:S(2)}) collective-permute-start(f32[128,256]{1,0:T(8,128)S(1)} %get-tuple-element.59), channel_id=1, source_target_pairs={{0,3},{1,0},{2,1},{3,2},{4,7},{5,4},{6,5},{7,6},{8,11},{9,8},{10,9... | collective-permute-start | bytes 393224 | tf_op jit(solution)/shard_map/ppermute | solution.py:502
  9.7 1.0 copy-start.3
  10.8 3.6 %copy-start.5 = (bf16[4,128,128]{2,1,0:T(8,128)(2,1)S(1)}, bf16[4,128,128]{2,1,0:T(8,128)(2,1)}, u32[]{:S(2)}) copy-start(bf16[4,128,128]{2,1,0:T(8,128)(2,1)} %constant.31.clone.flat) | copy-start | bytes 393220
  10.8 17.8 %copy-start.7 = (bf16[8,16,2048]{2,1,0:T(8,128)(2,1)S(1)}, bf16[8,16,2048]{2,1,0:T(8,128)(2,1)}, u32[]{:S(2)}) copy-start(bf16[8,16,2048]{2,1,0:T(8,128)(2,1)} %param.15) | copy-start | bytes 1572868
  14.4 14.2 %copy-start.1 = (bf16[8,16,2048]{2,1,0:T(8,128)(2,1)S(1)}, bf16[8,16,2048]{2,1,0:T(8,128)(2,1)}, u32[]{:S(2)}) copy-start(bf16[8,16,2048]{2,1,0:T(8,128)(2,1)} %param.14) | copy-start | bytes 1572868
  14.4 14.2 %copy-start.4 = (bf16[128,2048]{1,0:T(8,128)(2,1)S(1)}, bf16[128,2048]{1,0:T(8,128)(2,1)}, u32[]{:S(2)}) copy-start(bf16[128,2048]{1,0:T(8,128)(2,1)} %get-tuple-element.62.dz) | copy-start | bytes 1572868
  15.5 13.2 %copy-start.13 = (bf16[64,64]{1,0:T(8,128)(2,1)S(1)}, bf16[64,64]{1,0:T(8,128)(2,1)}, u32[]{:S(2)}) copy-start(bf16[64,64]{1,0:T(8,128)(2,1)} %point.2) | copy-start | bytes 24580
  15.5 25.1 %all-to-all-start = ((f32[64,4,256]{2,1,0:T(4,128)}), f32[64,4,256]{2,1,0:T(4,128)S(1)}, u32[]{:S(2)}, u32[]{:S(2)}) async-start(f32[64,4,256]{2,1,0:T(4,128)} %shard_map.175), calls=%async_computation | async-start | bytes 524288 | tf_op jit(solution)/shard_map/all_to_all | solution.py:521
  28.7 11.9 %copy-start.12 = (bf16[1,4,4,4096]{3,2,1,0:T(4,128)(2,1)S(1)}, bf16[1,4,4,4096]{3,2,1,0:T(4,128)(2,1)}, u32[]{:S(2)}) copy-start(bf16[1,4,4,4096]{3,2,1,0:T(4,128)(2,1)} %spectral.2) | copy-start | bytes 393220
  31.1 0.7 copy-start.8
  31.8 0.7 copy-start.16
  32.5 0.7 copy-start.18
  33.2 0.7 copy-start.20
  41.0 20.2 %copy-start.21 = (f32[128,512]{1,0:T(8,128)S(1)}, f32[128,512]{1,0:T(8,128)}, u32[]{:S(2)}) copy-start(f32[128,512]{1,0:T(8,128)} %copy-done.20) | copy-start | bytes 786436
  59.0 3.2 %copy-start.19 = (f32[128,512]{1,0:T(8,128)S(1)}, f32[128,512]{1,0:T(8,128)}, u32[]{:S(2)}) copy-start(f32[128,512]{1,0:T(8,128)} %copy-done.18) | copy-start | bytes 786436
  59.0 6.1 %copy-start.17 = (f32[128,512]{1,0:T(8,128)S(1)}, f32[128,512]{1,0:T(8,128)}, u32[]{:S(2)}) copy-start(f32[128,512]{1,0:T(8,128)} %copy-done.16) | copy-start | bytes 786436
  59.3 5.8 %collective-permute-start.3 = (f32[128,256]{1,0:T(8,128)S(1)}, f32[128,256]{1,0:T(8,128)S(1)}, u32[]{:S(2)}, u32[]{:S(2)}) collective-permute-start(f32[128,256]{1,0:T(8,128)S(1)} %shard_map.178.a), channel_id=1, source_target_pairs={{0,3},{1,0},{2,1},{3,2},{4,7},{5,4},{6,5},{7,6},{8,11},{9,8},{10,9... | collective-permute-start | bytes 393224 | tf_op jit(solution)/shard_map/ppermute | solution.py:502
  61.3 25.1 %collective-permute-start.10 = (f32[128,512]{1,0:T(8,128)S(1)}, f32[128,512]{1,0:T(8,128)S(1)}, u32[]{:S(2)}, u32[]{:S(2)}) collective-permute-start(f32[128,512]{1,0:T(8,128)S(1)} %copy-done.21), channel_id=1, source_target_pairs={{0,2},{1,3},{2,0},{3,1},{4,6},{5,7},{6,4},{7,5},{8,10},{9,11},{10,... | collective-permute-start | bytes 786440 | tf_op jit(solution)/shard_map/ppermute | solution.py:502
  62.1 24.7 %collective-permute-start.11 = (f32[128,512]{1,0:T(8,128)S(1)}, f32[128,512]{1,0:T(8,128)S(1)}, u32[]{:S(2)}, u32[]{:S(2)}) collective-permute-start(f32[128,512]{1,0:T(8,128)S(1)} %copy-done.19), channel_id=1, source_target_pairs={{0,3},{1,0},{2,1},{3,2},{4,7},{5,4},{6,5},{7,6},{8,11},{9,8},{10,9... | collective-permute-start | bytes 786440 | tf_op jit(solution)/shard_map/ppermute | solution.py:502
  63.3 9.5 %collective-permute-start.4 = (f32[128,256]{1,0:T(8,128)S(1)}, f32[128,256]{1,0:T(8,128)S(1)}, u32[]{:S(2)}, u32[]{:S(2)}) collective-permute-start(f32[128,256]{1,0:T(8,128)S(1)} %shard_map.178.a), channel_id=1, source_target_pairs={{0,2},{1,3},{2,0},{3,1},{4,6},{5,7},{6,4},{7,5},{8,10},{9,11},{10,... | collective-permute-start | bytes 393224 | tf_op jit(solution)/shard_map/ppermute | solution.py:502
  64.3 12.3 %collective-permute-start.5 = (f32[128,256]{1,0:T(8,128)S(1)}, f32[128,256]{1,0:T(8,128)S(1)}, u32[]{:S(2)}, u32[]{:S(2)}) collective-permute-start(f32[128,256]{1,0:T(8,128)S(1)} %shard_map.178.a), channel_id=1, source_target_pairs={{0,1},{1,2},{2,3},{3,0},{4,5},{5,6},{6,7},{7,4},{8,9},{9,10},{10,1... | collective-permute-start | bytes 393224 | tf_op jit(solution)/shard_map/ppermute | solution.py:502
  65.1 21.8 %collective-permute-start.9 = (f32[128,512]{1,0:T(8,128)S(1)}, f32[128,512]{1,0:T(8,128)S(1)}, u32[]{:S(2)}, u32[]{:S(2)}) collective-permute-start(f32[128,512]{1,0:T(8,128)S(1)} %copy-done.17), channel_id=1, source_target_pairs={{0,1},{1,2},{2,3},{3,0},{4,5},{5,6},{6,7},{7,4},{8,9},{9,10},{10,1... | collective-permute-start | bytes 786440 | tf_op jit(solution)/shard_map/ppermute | solution.py:502
  76.6 10.3 %copy-start.6 = (bf16[4,128,128]{2,1,0:T(8,128)(2,1)S(1)}, bf16[4,128,128]{2,1,0:T(8,128)(2,1)}, u32[]{:S(2)}) copy-start(bf16[4,128,128]{2,1,0:T(8,128)(2,1)} %constant.30.clone.ty) | copy-start | bytes 393220
  76.6 10.3 %copy-start.9 = (f32[128,512]{1,0:T(8,128)S(1)}, f32[128,512]{1,0:T(8,128)}, u32[]{:S(2)}) copy-start(f32[128,512]{1,0:T(8,128)} %copy-done.8) | copy-start | bytes 786436
  81.2 7.0 %collective-permute-start.6 = (f32[128,256]{1,0:T(8,128)S(1)}, f32[128,256]{1,0:T(8,128)S(1)}, u32[]{:S(2)}, u32[]{:S(2)}) collective-permute-start(f32[128,256]{1,0:T(8,128)S(1)} %get-tuple-element.77), channel_id=1, source_target_pairs={{0,1},{1,2},{2,3},{3,0},{4,5},{5,6},{6,7},{7,4},{8,9},{9,10},{10,1... | collective-permute-start | bytes 393224 | tf_op jit(solution)/shard_map/ppermute | solution.py:502
  84.4 6.7 %collective-permute-start.7 = (f32[128,256]{1,0:T(8,128)S(1)}, f32[128,256]{1,0:T(8,128)S(1)}, u32[]{:S(2)}, u32[]{:S(2)}) collective-permute-start(f32[128,256]{1,0:T(8,128)S(1)} %get-tuple-element.78), channel_id=1, source_target_pairs={{0,2},{1,3},{2,0},{3,1},{4,6},{5,7},{6,4},{7,5},{8,10},{9,11},{10,... | collective-permute-start | bytes 393224 | tf_op jit(solution)/shard_map/ppermute | solution.py:502
  86.3 1.0 copy-start.2
  86.3 5.5 %collective-permute-start.8 = (f32[128,256]{1,0:T(8,128)S(1)}, f32[128,256]{1,0:T(8,128)S(1)}, u32[]{:S(2)}, u32[]{:S(2)}) collective-permute-start(f32[128,256]{1,0:T(8,128)S(1)} %get-tuple-element.79), channel_id=1, source_target_pairs={{0,3},{1,0},{2,1},{3,2},{4,7},{5,4},{6,5},{7,6},{8,11},{9,8},{10,9... | collective-permute-start | bytes 393224 | tf_op jit(solution)/shard_map/ppermute | solution.py:502
  92.1 3.0 %collective-permute-start.12 = (f32[64,1024]{1,0:T(8,128)S(1)}, f32[64,1024]{1,0:T(8,128)S(1)}, u32[]{:S(2)}, u32[]{:S(2)}) collective-permute-start(f32[64,1024]{1,0:T(8,128)S(1)} %get-tuple-element.88), channel_id=1, source_target_pairs={{0,4},{4,0},{8,12},{12,8},{1,5},{5,1},{9,13},{13,9},{2,6},{6,2},{1... | collective-permute-start | bytes 786440 | tf_op jit(solution)/shard_map/ppermute | solution.py:502
  95.0 4.8 %copy-start.11 = (bf16[16,32,64]{2,1,0:T(8,128)(2,1)S(1)}, bf16[16,32,64]{2,1,0:T(8,128)(2,1)}, u32[]{:S(2)}) copy-start(bf16[16,32,64]{2,1,0:T(8,128)(2,1)} %constant.32.clone.tx) | copy-start | bytes 196612
  95.1 4.8 %collective-permute-start.13 = (f32[32,1024]{1,0:T(8,128)S(1)}, f32[32,1024]{1,0:T(8,128)S(1)}, u32[]{:S(2)}, u32[]{:S(2)}) collective-permute-start(f32[32,1024]{1,0:T(8,128)S(1)} %get-tuple-element.90), channel_id=1, source_target_pairs={{0,8},{4,12},{8,0},{12,4},{1,9},{5,13},{9,1},{13,5},{2,10},{6,14},... | collective-permute-start | bytes 393224 | tf_op jit(solution)/shard_map/ppermute | solution.py:502
  100.1 16.3 %copy-start.10 = (bf16[1,4,4,4096]{3,2,1,0:T(4,128)(2,1)S(1)}, bf16[1,4,4,4096]{3,2,1,0:T(4,128)(2,1)}, u32[]{:S(2)}) copy-start(bf16[1,4,4,4096]{3,2,1,0:T(4,128)(2,1)} %spectral.3) | copy-start | bytes 393220
  117.5 6.6 %copy-start.14 = (bf16[64,64]{1,0:T(8,128)(2,1)S(1)}, bf16[64,64]{1,0:T(8,128)(2,1)}, u32[]{:S(2)}) copy-start(bf16[64,64]{1,0:T(8,128)(2,1)} %point.3) | copy-start | bytes 24580
  117.5 21.3 %all-to-all-start.3 = ((f32[64,4,384]{2,1,0:T(4,128)}), f32[64,4,384]{2,1,0:T(4,128)S(1)}, u32[]{:S(2)}, u32[]{:S(2)}) async-start(f32[64,4,384]{2,1,0:T(4,128)} %get-tuple-element.92), calls=%async_computation.3 | async-start | bytes 786432 | tf_op jit(solution)/shard_map/all_to_all | solution.py:521
  139.2 5.4 %collective-permute-start.14 = (f32[160,256]{1,0:T(8,128)S(1)}, f32[160,256]{1,0:T(8,128)S(1)}, u32[]{:S(2)}, u32[]{:S(2)}) collective-permute-start(f32[160,256]{1,0:T(8,128)S(1)} %shard_map.187.a), channel_id=1, source_target_pairs={{0,3},{1,0},{2,1},{3,2},{4,7},{5,4},{6,5},{7,6},{8,11},{9,8},{10,9... | collective-permute-start | bytes 491528 | tf_op jit(solution)/shard_map/ppermute | solution.py:502
  141.1 6.6 %collective-permute-start.15 = (f32[160,256]{1,0:T(8,128)S(1)}, f32[160,256]{1,0:T(8,128)S(1)}, u32[]{:S(2)}, u32[]{:S(2)}) collective-permute-start(f32[160,256]{1,0:T(8,128)S(1)} %shard_map.187.a), channel_id=1, source_target_pairs={{0,2},{1,3},{2,0},{3,1},{4,6},{5,7},{6,4},{7,5},{8,10},{9,11},{10,... | collective-permute-start | bytes 491528 | tf_op jit(solution)/shard_map/ppermute | solution.py:502
  142.0 10.3 %collective-permute-start.16 = (f32[160,256]{1,0:T(8,128)S(1)}, f32[160,256]{1,0:T(8,128)S(1)}, u32[]{:S(2)}, u32[]{:S(2)}) collective-permute-start(f32[160,256]{1,0:T(8,128)S(1)} %shard_map.187.a), channel_id=1, source_target_pairs={{0,1},{1,2},{2,3},{3,0},{4,5},{5,6},{6,7},{7,4},{8,9},{9,10},{10,1... | collective-permute-start | bytes 491528 | tf_op jit(solution)/shard_map/ppermute | solution.py:502
  142.0 10.3 %copy-start = (f32[128,2048]{1,0:T(8,128)S(1)}, f32[128,2048]{1,0:T(8,128)}, u32[]{:S(2)}) copy-start(f32[128,2048]{1,0:T(8,128)} %shard_map.186.local) | copy-start | bytes 3145732

commit v5 on v4

--- a/solution.py
+++ b/solution.py
@@ -566,15 +566,13 @@
         scratch=[((WIDE, 256), bf16)],
     )
     got = exchange([own] + parts, "gx")
-    (modes,) = call(along_yx_kernel, [((64, 4, 256), f32)], at, *got, flat, coef)
-    modes, pre_one, dz_side = lax.optimization_barrier((modes, pre_one, dz_two))
     slope, local_two, weight_two, *ins = call(
         side_kernel,
         [(big, f32, "raw")] * 2 + [((C, C), f32, 0)] + [((ROWS, 512), f32)] * 4,
         at,
         pre_one,
         first,
-        dz_side,
+        dz_two,
         mine,
         point_two,
         limit=14,
@@ -589,8 +587,9 @@
             dma((16,)),
         ],
     )
+    got, ins, slope, local_two = lax.optimization_barrier((got, ins, slope, local_two))
+    (modes,) = call(along_yx_kernel, [((64, 4, 256), f32)], at, *got, flat, coef)
     got = over(modes, ("gz", "gy"))
-    got, ins = lax.optimization_barrier((got, ins))
     got_in = exchange(ins, "gx")
     back, hat_two = call(
         mix_two_kernel,

time: 155 us -> 155 us (level)
  blocking collectives: 34.2 us -> 58.9 us
  starting transfers between devices: 43.9 us -> 30.6 us
  waiting for transfers between devices: 49.9 us -> 39.8 us
    all_to_all x2 -> x3, blocking collectives: 34.2 us -> 58.9 us  [over(): return lax.all_to_all(v, axes, 0, 0, tiled=True)]
    all_to_all x2 -> x1, starting transfers between devices: 19.7 us -> 6.61 us  [over(): return lax.all_to_all(v, axes, 0, 0, tiled=True)]
    all_to_all x2 -> x1, waiting for transfers between devices: 20 us -> 13.3 us  [over(): return lax.all_to_all(v, axes, 0, 0, tiled=True)]
    ppermute x17, waiting for transfers between devices: 29.9 us -> 26.5 us  [shifted(): return lax.ppermute(v, axis, pairs)]
    unnamed x44 -> x28, local copies, waits for them, and re-layouts: 4.1 us -> 2.93 us
  transfers between devices with their start and end apart: 19 -> 18, of which waited for: 12 -> 10; matrix products, arithmetic and copies ran while one was open for 0% -> 0% of each run, Pallas kernels for 8% -> 8%
where the time goes in v5:
time: 155 us; the launch traced here: 154 us
  blocking collectives  58.9 us (38%)
  waiting for transfers between devices  39.8 us (26%)
  starting transfers between devices  30.6 us (20%)
  Pallas kernels  20.8 us (13%)
  local copies, waits for them, and re-layouts  2.93 us (2%)
    all_to_all x3, blocking collectives, over(): return lax.all_to_all(v, axes, 0, 0, tiled=True)  58.9 us
    ppermute x17, waiting for transfers between devices, shifted(): return lax.ppermute(v, axis, pairs)  26.5 us
    ppermute x17, starting transfers between devices, shifted(): return lax.ppermute(v, axis, pairs)  24 us
    pallas_call x18, Pallas kernels, call(): pl.pallas_call(body, out_shape=shapes, in_specs=[pl.BlockSpec(memory_spac...  20.8 us
    all_to_all x1, waiting for transfers between devices, over(): return lax.all_to_all(v, axes, 0, 0, tiled=True)  13.3 us
    all_to_all x1, starting transfers between devices, over(): return lax.all_to_all(v, axes, 0, 0, tiled=True)  6.61 us
  transfers between devices with their start and end apart: 18, of which 10 were waited for; matrix products, arithmetic and copies ran while one was open for 0% of the time, Pallas kernels for 8%

profile of v5, /device:TPU:1, one launch (start us, length us, event | category | flops | bytes accessed | tf_op | source)
XLA Modules:
  0.0 154.1 jit_solution(7645326245541056569)
XLA Ops:
  0.7 3.3 %shard_map.173 = (bf16[128,2048]{1,0:T(8,128)(2,1)}, f32[128,256]{1,0:T(8,128)S(1)}, f32[128,256]{1,0:T(8,128)S(1)}, f32[128,256]{1,0:T(8,128)S(1)}, f32[32,1024]{1,0:T(8,128)S(1)}, /*index=5*/f32[16,2048]{1,0:T(8,128)S(1)}) custom-call(s32[1]{0:T(128)} %bitcast.at, bf16[128,2048]{1,0:T(8,128)(2,1)} %bitcast.11, bf16[128,2048]{1,0:T(8,128)(2,1)} %bitcast.12, ...), custom_call_target="tpu_custom_call" | custom-call | tf_op jit(solution)/shard_map/pallas_call | solution.py:116
  3.9 2.2 %collective-permute-start = (f32[128,256]{1,0:T(8,128)S(1)}, f32[128,256]{1,0:T(8,128)S(1)}, u32[]{:S(2)}, u32[]{:S(2)}) collective-permute-start(f32[128,256]{1,0:T(8,128)S(1)} %get-tuple-element.59), channel_id=1, source_target_pairs={{0,1},{1,2},{2,3},{3,0},{4,5},{5,6},{6,7},{7,4},{8,9},{9,10},{10,1... | collective-permute-start | bytes 393224 | tf_op jit(solution)/shard_map/ppermute | solution.py:502
  6.1 2.6 %collective-permute-start.1 = (f32[128,256]{1,0:T(8,128)S(1)}, f32[128,256]{1,0:T(8,128)S(1)}, u32[]{:S(2)}, u32[]{:S(2)}) collective-permute-start(f32[128,256]{1,0:T(8,128)S(1)} %get-tuple-element.60), channel_id=1, source_target_pairs={{0,2},{1,3},{2,0},{3,1},{4,6},{5,7},{6,4},{7,5},{8,10},{9,11},{10,... | collective-permute-start | bytes 393224 | tf_op jit(solution)/shard_map/ppermute | solution.py:502
  8.7 1.1 collective-permute-start.2
  9.8 1.0 copy-done.3
  10.9 0.6 shard_map.174
  11.6 1.0 copy-done.4
  12.6 2.4 %shard_map.175 = (f32[128,2048]{1,0:T(8,128)}, f32[128,2048]{1,0:T(8,128)}, f32[64,64]{1,0:T(8,128)S(1)}, f32[128,512]{1,0:T(8,128)S(1)}, f32[128,512]{1,0:T(8,1...) custom-call(s32[1]{0:T(128)} %bitcast.at, bf16[128,2048]{1,0:T(8,128)(2,1)S(1)} %bitcast.10, ...), custom_call_target="tpu_custom_call" | custom-call | tf_op jit(solution)/shard_map/pallas_call | solution.py:116
  15.1 0.3 shard_map.176
  15.4 24.9 %all_to_all.20.got = f32[64,4,256]{2,1,0:T(4,128)S(1)} all-to-all(f32[64,4,256]{2,1,0:T(4,128)S(1)} %shard_map.176), channel_id=1, replica_groups=mesh['gz'=16,'gy'=4,'gx'=4] {'gz','gy'}, dimensions={0} | all-to-all | bytes 524288 | tf_op jit(solution)/shard_map/all_to_all | solution.py:521
  40.3 0.4 shard_map.177
  40.8 17.8 %all_to_all.21.got = f32[64,4,256]{2,1,0:T(4,128)S(1)} all-to-all(f32[64,4,256]{2,1,0:T(4,128)S(1)} %get-tuple-element.76), channel_id=1, replica_groups=mesh['gz'=16,'gy'=4,'gx'=4] {'gz','gy'}, dimensions={0} | all-to-all | bytes 524288 | tf_op jit(solution)/shard_map/all_to_all | solution.py:521
  58.6 0.3 shard_map.178.a
  58.9 1.4 collective-permute-start.3
  60.3 0.9 collective-permute-start.10
  61.2 1.7 %collective-permute-start.11 = (f32[128,512]{1,0:T(8,128)S(1)}, f32[128,512]{1,0:T(8,128)S(1)}, u32[]{:S(2)}, u32[]{:S(2)}) collective-permute-start(f32[128,512]{1,0:T(8,128)S(1)} %get-tuple-element.87), channel_id=1, source_target_pairs={{0,3},{1,0},{2,1},{3,2},{4,7},{5,4},{6,5},{7,6},{8,11},{9,8},{10,9... | collective-permute-start | bytes 786440 | tf_op jit(solution)/shard_map/ppermute | solution.py:502
  62.9 0.5 collective-permute-start.4
  63.4 0.8 collective-permute-start.5
  64.1 1.4 collective-permute-start.9
  65.5 6.3 %collective-permute-done.4.c = f32[128,256]{1,0:T(8,128)S(1)} collective-permute-done((f32[128,256]{1,0:T(8,128)S(1)}, f32[128,256]{1,0:T(8,128)S(1)}, u32[]{:S(2)}, u32[]{:S(2)}) %collective-permute-start.4) | collective-permute-done | bytes 131104 | tf_op jit(solution)/shard_map/ppermute | solution.py:502
  71.8 3.9 %collective-permute-done.5.d = f32[128,256]{1,0:T(8,128)S(1)} collective-permute-done((f32[128,256]{1,0:T(8,128)S(1)}, f32[128,256]{1,0:T(8,128)S(1)}, u32[]{:S(2)}, u32[]{:S(2)}) %collective-permute-start.5) | collective-permute-done | bytes 131104 | tf_op jit(solution)/shard_map/ppermute | solution.py:502
  75.7 4.5 %shard_map.179 = (bf16[128,2048]{1,0:T(8,128)(2,1)}, f32[128,256]{1,0:T(8,128)S(1)}, f32[128,256]{1,0:T(8,128)S(1)}, f32[128,256]{1,0:T(8,128)S(1)}) custom-call(s32[1]{0:T(128)} %bitcast.at, f32[128,2048]{1,0:T(8,128)} %get-tuple-element.68.local_from, f32[128,2048]{1,0:T(8,128)} %get-tuple-element.69.slope_from, f32[128,256]{1,0:T(8,128)S(1)} %shard_map.178.a, ...), custom_call_target="tpu_custom_call" | custom-call | tf_op jit(solution)/shard_map/pallas_call | solution.py:116
  80.2 3.2 %collective-permute-start.6 = (f32[128,256]{1,0:T(8,128)S(1)}, f32[128,256]{1,0:T(8,128)S(1)}, u32[]{:S(2)}, u32[]{:S(2)}) collective-permute-start(f32[128,256]{1,0:T(8,128)S(1)} %get-tuple-element.81), channel_id=1, source_target_pairs={{0,1},{1,2},{2,3},{3,0},{4,5},{5,6},{6,7},{7,4},{8,9},{9,10},{10,1... | collective-permute-start | bytes 393224 | tf_op jit(solution)/shard_map/ppermute | solution.py:502
  83.4 2.5 %collective-permute-start.7 = (f32[128,256]{1,0:T(8,128)S(1)}, f32[128,256]{1,0:T(8,128)S(1)}, u32[]{:S(2)}, u32[]{:S(2)}) collective-permute-start(f32[128,256]{1,0:T(8,128)S(1)} %get-tuple-element.82), channel_id=1, source_target_pairs={{0,2},{1,3},{2,0},{3,1},{4,6},{5,7},{6,4},{7,5},{8,10},{9,11},{10,... | collective-permute-start | bytes 393224 | tf_op jit(solution)/shard_map/ppermute | solution.py:502
  85.9 0.3 shard_map.181
  86.2 0.7 copy-done.2
  86.9 0.7 shard_map.180
  87.7 2.9 %collective-permute-done.7.c = f32[128,256]{1,0:T(8,128)S(1)} collective-permute-done((f32[128,256]{1,0:T(8,128)S(1)}, f32[128,256]{1,0:T(8,128)S(1)}, u32[]{:S(2)}, u32[]{:S(2)}) %collective-permute-start.7) | collective-permute-done | bytes 131104 | tf_op jit(solution)/shard_map/ppermute | solution.py:502
  90.6 0.8 collective-permute-done.8.d
  91.6 1.8 %collective-permute-start.12 = (f32[64,1024]{1,0:T(8,128)S(1)}, f32[64,1024]{1,0:T(8,128)S(1)}, u32[]{:S(2)}, u32[]{:S(2)}) collective-permute-start(f32[64,1024]{1,0:T(8,128)S(1)} %get-tuple-element.92), channel_id=1, source_target_pairs={{0,4},{4,0},{8,12},{12,8},{1,5},{5,1},{9,13},{13,9},{2,6},{6,2},{1... | collective-permute-start | bytes 786440 | tf_op jit(solution)/shard_map/ppermute | solution.py:502
  93.4 1.2 collective-permute-done.12.got
  94.6 1.3 collective-permute-start.13
  96.0 3.4 %collective-permute-done.13.b = f32[32,1024]{1,0:T(8,128)S(1)} collective-permute-done((f32[32,1024]{1,0:T(8,128)S(1)}, f32[32,1024]{1,0:T(8,128)S(1)}, u32[]{:S(2)}, u32[]{:S(2)}) %collective-permute-start.13) | collective-permute-done | bytes 131104 | tf_op jit(solution)/shard_map/ppermute | solution.py:502
  99.4 0.2 shard_map.184
  99.7 16.3 %all_to_all.22.got = f32[16,4,896]{2,1,0:T(4,128)S(1)} all-to-all(f32[16,4,896]{2,1,0:T(4,128)S(1)} %shard_map.184), channel_id=1, replica_groups=mesh['gz'=16,'gy'=4,'gx'=4] {'gz'}, dimensions={0} | all-to-all | bytes 458752 | tf_op jit(solution)/shard_map/all_to_all | solution.py:521
  115.9 1.2 shard_map.185
  117.1 6.6 %all-to-all-start.3 = ((f32[64,4,384]{2,1,0:T(4,128)}), f32[64,4,384]{2,1,0:T(4,128)S(1)}, u32[]{:S(2)}, u32[]{:S(2)}) async-start(f32[64,4,384]{2,1,0:T(4,128)} %get-tuple-element.96), calls=%async_computation.3 | async-start | bytes 786432 | tf_op jit(solution)/shard_map/all_to_all | solution.py:521
  123.7 1.4 shard_map.186.local
  125.1 13.3 %all-to-all-done.3.got = f32[64,4,384]{2,1,0:T(4,128)S(1)} async-done(((f32[64,4,384]{2,1,0:T(4,128)}), f32[64,4,384]{2,1,0:T(4,128)S(1)}, u32[]{:S(2)}, u32[]{:S(2)}) %all-to-all-start.3) | async-done | bytes 393248 | tf_op jit(solution)/shard_map/all_to_all | solution.py:521
  138.4 0.3 shard_map.187.a
  138.7 2.0 %collective-permute-start.14 = (f32[160,256]{1,0:T(8,128)S(1)}, f32[160,256]{1,0:T(8,128)S(1)}, u32[]{:S(2)}, u32[]{:S(2)}) collective-permute-start(f32[160,256]{1,0:T(8,128)S(1)} %shard_map.187.a), channel_id=1, source_target_pairs={{0,3},{1,0},{2,1},{3,2},{4,7},{5,4},{6,5},{7,6},{8,11},{9,8},{10,9... | collective-permute-start | bytes 491528 | tf_op jit(solution)/shard_map/ppermute | solution.py:502
  140.7 0.5 collective-permute-start.15
  141.4 1.2 shard_map.190
  142.5 1.2 shard_map.189
  143.7 0.4 collective-permute-done.14.b
  144.2 3.2 %collective-permute-done.15.c = f32[160,256]{1,0:T(8,128)S(1)} collective-permute-done((f32[160,256]{1,0:T(8,128)S(1)}, f32[160,256]{1,0:T(8,128)S(1)}, u32[]{:S(2)}, u32[]{:S(2)}) %collective-permute-start.15) | collective-permute-done | bytes 163872 | tf_op jit(solution)/shard_map/ppermute | solution.py:502
  147.3 4.5 %collective-permute-done.16.d = f32[160,256]{1,0:T(8,128)S(1)} collective-permute-done((f32[160,256]{1,0:T(8,128)S(1)}, f32[160,256]{1,0:T(8,128)S(1)}, u32[]{:S(2)}, u32[]{:S(2)}) %collective-permute-start.16) | collective-permute-done | bytes 163872 | tf_op jit(solution)/shard_map/ppermute | solution.py:502
  151.8 2.2 %shard_map.188 = (bf16[128,2048]{1,0:T(8,128)(2,1)}, f32[64,64]{1,0:T(8,128)}, f32[64,64]{1,0:T(8,128)}) custom-call(s32[1]{0:T(128)} %bitcast.at, f32[160,256]{1,0:T(8,128)S(1)} %shard_map.187.a, f32[160,256]{1,0:T(8,128)S(1)} %collective-permute-done.14.b, f32[160,256]{1,0:T(8,128)S(1)} %collective-permute-done.15.c, ...), custom_call_target="tpu_custom_call" | custom-call | tf_op jit(solution)/shard_map/pallas_call | solution.py:116
  (37 shorter events, 0.6 us)
Async XLA Ops:
  0.6 9.2 %copy-start.13 = (f32[16,128]{1,0:T(8,128)S(1)}, f32[16,128]{1,0:T(8,128)}, u32[]{:S(2)}) copy-start(f32[16,128]{1,0:T(8,128)} %constant.33.clone.few) | copy-start | bytes 24580
  0.7 10.8 %copy-start.7 = (bf16[8,16,2048]{2,1,0:T(8,128)(2,1)S(1)}, bf16[8,16,2048]{2,1,0:T(8,128)(2,1)}, u32[]{:S(2)}) copy-start(bf16[8,16,2048]{2,1,0:T(8,128)(2,1)} %param.15) | copy-start | bytes 1572868
  3.9 7.6 %copy-start.1 = (bf16[8,16,2048]{2,1,0:T(8,128)(2,1)S(1)}, bf16[8,16,2048]{2,1,0:T(8,128)(2,1)}, u32[]{:S(2)}) copy-start(bf16[8,16,2048]{2,1,0:T(8,128)(2,1)} %param.14) | copy-start | bytes 1572868
  3.9 11.1 %collective-permute-start = (f32[128,256]{1,0:T(8,128)S(1)}, f32[128,256]{1,0:T(8,128)S(1)}, u32[]{:S(2)}, u32[]{:S(2)}) collective-permute-start(f32[128,256]{1,0:T(8,128)S(1)} %get-tuple-element.59), channel_id=1, source_target_pairs={{0,1},{1,2},{2,3},{3,0},{4,5},{5,6},{6,7},{7,4},{8,9},{9,10},{10,1... | collective-permute-start | bytes 393224 | tf_op jit(solution)/shard_map/ppermute | solution.py:502
  6.1 8.9 %collective-permute-start.1 = (f32[128,256]{1,0:T(8,128)S(1)}, f32[128,256]{1,0:T(8,128)S(1)}, u32[]{:S(2)}, u32[]{:S(2)}) collective-permute-start(f32[128,256]{1,0:T(8,128)S(1)} %get-tuple-element.60), channel_id=1, source_target_pairs={{0,2},{1,3},{2,0},{3,1},{4,6},{5,7},{6,4},{7,5},{8,10},{9,11},{10,... | collective-permute-start | bytes 393224 | tf_op jit(solution)/shard_map/ppermute | solution.py:502
  8.7 6.3 %collective-permute-start.2 = (f32[128,256]{1,0:T(8,128)S(1)}, f32[128,256]{1,0:T(8,128)S(1)}, u32[]{:S(2)}, u32[]{:S(2)}) collective-permute-start(f32[128,256]{1,0:T(8,128)S(1)} %get-tuple-element.61), channel_id=1, source_target_pairs={{0,3},{1,0},{2,1},{3,2},{4,7},{5,4},{6,5},{7,6},{8,11},{9,8},{10,9... | collective-permute-start | bytes 393224 | tf_op jit(solution)/shard_map/ppermute | solution.py:502
  9.8 1.0 copy-start.3
  10.9 0.7 copy-start.11
  11.6 1.0 copy-start.4
  12.6 2.4 %copy-start.5 = (bf16[4,128,128]{2,1,0:T(8,128)(2,1)S(1)}, bf16[4,128,128]{2,1,0:T(8,128)(2,1)}, u32[]{:S(2)}) copy-start(bf16[4,128,128]{2,1,0:T(8,128)(2,1)} %constant.31.clone.flat) | copy-start | bytes 393220
  15.4 24.9 %copy-start.10 = (bf16[1,4,4,4096]{3,2,1,0:T(4,128)(2,1)S(1)}, bf16[1,4,4,4096]{3,2,1,0:T(4,128)(2,1)}, u32[]{:S(2)}) copy-start(bf16[1,4,4,4096]{3,2,1,0:T(4,128)(2,1)} %spectral.2) | copy-start | bytes 393220
  58.9 5.2 %collective-permute-start.3 = (f32[128,256]{1,0:T(8,128)S(1)}, f32[128,256]{1,0:T(8,128)S(1)}, u32[]{:S(2)}, u32[]{:S(2)}) collective-permute-start(f32[128,256]{1,0:T(8,128)S(1)} %shard_map.178.a), channel_id=1, source_target_pairs={{0,3},{1,0},{2,1},{3,2},{4,7},{5,4},{6,5},{7,6},{8,11},{9,8},{10,9... | collective-permute-start | bytes 393224 | tf_op jit(solution)/shard_map/ppermute | solution.py:502
  60.3 25.6 %collective-permute-start.10 = (f32[128,512]{1,0:T(8,128)S(1)}, f32[128,512]{1,0:T(8,128)S(1)}, u32[]{:S(2)}, u32[]{:S(2)}) collective-permute-start(f32[128,512]{1,0:T(8,128)S(1)} %get-tuple-element.86), channel_id=1, source_target_pairs={{0,2},{1,3},{2,0},{3,1},{4,6},{5,7},{6,4},{7,5},{8,10},{9,11},{10,... | collective-permute-start | bytes 786440 | tf_op jit(solution)/shard_map/ppermute | solution.py:502
  61.2 24.7 %collective-permute-start.11 = (f32[128,512]{1,0:T(8,128)S(1)}, f32[128,512]{1,0:T(8,128)S(1)}, u32[]{:S(2)}, u32[]{:S(2)}) collective-permute-start(f32[128,512]{1,0:T(8,128)S(1)} %get-tuple-element.87), channel_id=1, source_target_pairs={{0,3},{1,0},{2,1},{3,2},{4,7},{5,4},{6,5},{7,6},{8,11},{9,8},{10,9... | collective-permute-start | bytes 786440 | tf_op jit(solution)/shard_map/ppermute | solution.py:502
  62.9 8.9 %collective-permute-start.4 = (f32[128,256]{1,0:T(8,128)S(1)}, f32[128,256]{1,0:T(8,128)S(1)}, u32[]{:S(2)}, u32[]{:S(2)}) collective-permute-start(f32[128,256]{1,0:T(8,128)S(1)} %shard_map.178.a), channel_id=1, source_target_pairs={{0,2},{1,3},{2,0},{3,1},{4,6},{5,7},{6,4},{7,5},{8,10},{9,11},{10,... | collective-permute-start | bytes 393224 | tf_op jit(solution)/shard_map/ppermute | solution.py:502
  63.4 12.3 %collective-permute-start.5 = (f32[128,256]{1,0:T(8,128)S(1)}, f32[128,256]{1,0:T(8,128)S(1)}, u32[]{:S(2)}, u32[]{:S(2)}) collective-permute-start(f32[128,256]{1,0:T(8,128)S(1)} %shard_map.178.a), channel_id=1, source_target_pairs={{0,1},{1,2},{2,3},{3,0},{4,5},{5,6},{6,7},{7,4},{8,9},{9,10},{10,1... | collective-permute-start | bytes 393224 | tf_op jit(solution)/shard_map/ppermute | solution.py:502
  64.1 21.8 %collective-permute-start.9 = (f32[128,512]{1,0:T(8,128)S(1)}, f32[128,512]{1,0:T(8,128)S(1)}, u32[]{:S(2)}, u32[]{:S(2)}) collective-permute-start(f32[128,512]{1,0:T(8,128)S(1)} %get-tuple-element.85), channel_id=1, source_target_pairs={{0,1},{1,2},{2,3},{3,0},{4,5},{5,6},{6,7},{7,4},{8,9},{9,10},{10,1... | collective-permute-start | bytes 786440 | tf_op jit(solution)/shard_map/ppermute | solution.py:502
  75.7 10.3 %copy-start.6 = (bf16[4,128,128]{2,1,0:T(8,128)(2,1)S(1)}, bf16[4,128,128]{2,1,0:T(8,128)(2,1)}, u32[]{:S(2)}) copy-start(bf16[4,128,128]{2,1,0:T(8,128)(2,1)} %constant.30.clone.ty) | copy-start | bytes 393220
  80.2 7.5 %collective-permute-start.6 = (f32[128,256]{1,0:T(8,128)S(1)}, f32[128,256]{1,0:T(8,128)S(1)}, u32[]{:S(2)}, u32[]{:S(2)}) collective-permute-start(f32[128,256]{1,0:T(8,128)S(1)} %get-tuple-element.81), channel_id=1, source_target_pairs={{0,1},{1,2},{2,3},{3,0},{4,5},{5,6},{6,7},{7,4},{8,9},{9,10},{10,1... | collective-permute-start | bytes 393224 | tf_op jit(solution)/shard_map/ppermute | solution.py:502
  83.4 7.2 %collective-permute-start.7 = (f32[128,256]{1,0:T(8,128)S(1)}, f32[128,256]{1,0:T(8,128)S(1)}, u32[]{:S(2)}, u32[]{:S(2)}) collective-permute-start(f32[128,256]{1,0:T(8,128)S(1)} %get-tuple-element.82), channel_id=1, source_target_pairs={{0,2},{1,3},{2,0},{3,1},{4,6},{5,7},{6,4},{7,5},{8,10},{9,11},{10,... | collective-permute-start | bytes 393224 | tf_op jit(solution)/shard_map/ppermute | solution.py:502
  85.9 1.0 copy-start.2
  85.9 5.5 %collective-permute-start.8 = (f32[128,256]{1,0:T(8,128)S(1)}, f32[128,256]{1,0:T(8,128)S(1)}, u32[]{:S(2)}, u32[]{:S(2)}) collective-permute-start(f32[128,256]{1,0:T(8,128)S(1)} %get-tuple-element.83), channel_id=1, source_target_pairs={{0,3},{1,0},{2,1},{3,2},{4,7},{5,4},{6,5},{7,6},{8,11},{9,8},{10,9... | collective-permute-start | bytes 393224 | tf_op jit(solution)/shard_map/ppermute | solution.py:502
  91.6 3.0 %collective-permute-start.12 = (f32[64,1024]{1,0:T(8,128)S(1)}, f32[64,1024]{1,0:T(8,128)S(1)}, u32[]{:S(2)}, u32[]{:S(2)}) collective-permute-start(f32[64,1024]{1,0:T(8,128)S(1)} %get-tuple-element.92), channel_id=1, source_target_pairs={{0,4},{4,0},{8,12},{12,8},{1,5},{5,1},{9,13},{13,9},{2,6},{6,2},{1... | collective-permute-start | bytes 786440 | tf_op jit(solution)/shard_map/ppermute | solution.py:502
  94.6 4.8 %copy-start.9 = (bf16[16,32,64]{2,1,0:T(8,128)(2,1)S(1)}, bf16[16,32,64]{2,1,0:T(8,128)(2,1)}, u32[]{:S(2)}) copy-start(bf16[16,32,64]{2,1,0:T(8,128)(2,1)} %constant.32.clone.tx) | copy-start | bytes 196612
  94.6 4.8 %collective-permute-start.13 = (f32[32,1024]{1,0:T(8,128)S(1)}, f32[32,1024]{1,0:T(8,128)S(1)}, u32[]{:S(2)}, u32[]{:S(2)}) collective-permute-start(f32[32,1024]{1,0:T(8,128)S(1)} %get-tuple-element.94), channel_id=1, source_target_pairs={{0,8},{4,12},{8,0},{12,4},{1,9},{5,13},{9,1},{13,5},{2,10},{6,14},... | collective-permute-start | bytes 393224 | tf_op jit(solution)/shard_map/ppermute | solution.py:502
  99.6 16.3 %copy-start.8 = (bf16[1,4,4,4096]{3,2,1,0:T(4,128)(2,1)S(1)}, bf16[1,4,4,4096]{3,2,1,0:T(4,128)(2,1)}, u32[]{:S(2)}) copy-start(bf16[1,4,4,4096]{3,2,1,0:T(4,128)(2,1)} %spectral.3) | copy-start | bytes 393220
  117.1 6.6 %copy-start.12 = (bf16[64,64]{1,0:T(8,128)(2,1)S(1)}, bf16[64,64]{1,0:T(8,128)(2,1)}, u32[]{:S(2)}) copy-start(bf16[64,64]{1,0:T(8,128)(2,1)} %point.3) | copy-start | bytes 24580
  117.1 21.3 %all-to-all-start.3 = ((f32[64,4,384]{2,1,0:T(4,128)}), f32[64,4,384]{2,1,0:T(4,128)S(1)}, u32[]{:S(2)}, u32[]{:S(2)}) async-start(f32[64,4,384]{2,1,0:T(4,128)} %get-tuple-element.96), calls=%async_computation.3 | async-start | bytes 786432 | tf_op jit(solution)/shard_map/all_to_all | solution.py:521
  138.7 5.4 %collective-permute-start.14 = (f32[160,256]{1,0:T(8,128)S(1)}, f32[160,256]{1,0:T(8,128)S(1)}, u32[]{:S(2)}, u32[]{:S(2)}) collective-permute-start(f32[160,256]{1,0:T(8,128)S(1)} %shard_map.187.a), channel_id=1, source_target_pairs={{0,3},{1,0},{2,1},{3,2},{4,7},{5,4},{6,5},{7,6},{8,11},{9,8},{10,9... | collective-permute-start | bytes 491528 | tf_op jit(solution)/shard_map/ppermute | solution.py:502
  140.7 6.6 %collective-permute-start.15 = (f32[160,256]{1,0:T(8,128)S(1)}, f32[160,256]{1,0:T(8,128)S(1)}, u32[]{:S(2)}, u32[]{:S(2)}) collective-permute-start(f32[160,256]{1,0:T(8,128)S(1)} %shard_map.187.a), channel_id=1, source_target_pairs={{0,2},{1,3},{2,0},{3,1},{4,6},{5,7},{6,4},{7,5},{8,10},{9,11},{10,... | collective-permute-start | bytes 491528 | tf_op jit(solution)/shard_map/ppermute | solution.py:502
  141.2 10.7 %collective-permute-start.16 = (f32[160,256]{1,0:T(8,128)S(1)}, f32[160,256]{1,0:T(8,128)S(1)}, u32[]{:S(2)}, u32[]{:S(2)}) collective-permute-start(f32[160,256]{1,0:T(8,128)S(1)} %shard_map.187.a), channel_id=1, source_target_pairs={{0,1},{1,2},{2,3},{3,0},{4,5},{5,6},{6,7},{7,4},{8,9},{9,10},{10,1... | collective-permute-start | bytes 491528 | tf_op jit(solution)/shard_map/ppermute | solution.py:502
  141.4 10.5 %copy-start = (f32[128,2048]{1,0:T(8,128)S(1)}, f32[128,2048]{1,0:T(8,128)}, u32[]{:S(2)}) copy-start(f32[128,2048]{1,0:T(8,128)} %shard_map.186.local) | copy-start | bytes 3145732

commit v6 on v4

--- a/solution.py
+++ b/solution.py
@@ -503,11 +503,13 @@
 
 
 def exchange(parts, kind):
-    return [parts[0]] + [shifted(parts[s], kind, s) for s in (1, 2, 3)]
+    far = shifted(parts[2], kind, 2)
+    return [parts[0], shifted(parts[1], kind, 1), far, shifted(parts[3], kind, 3)]
 
 
 def spread(v, kind):
-    return [v] + [shifted(v, kind, s) for s in (3, 2, 1)]
+    far = shifted(v, kind, 2)
+    return [v, shifted(v, kind, 3), far, shifted(v, kind, 1)]
 
 
 def reduce_y(at, near, far, width):

time: 155 us -> 155 us (level)
  no operation moved by 1% of the time
where the time goes in v6:
time: 155 us
  waiting for transfers between devices  49.9 us (32%)
  starting transfers between devices  43.9 us (28%)
  blocking collectives  34.2 us (22%)
  Pallas kernels  21.4 us (14%)
  local copies, waits for them, and re-layouts  4.1 us (3%)
    all_to_all x2, blocking collectives, over(): return lax.all_to_all(v, axes, 0, 0, tiled=True)  34.2 us
    ppermute x17, waiting for transfers between devices, shifted(): return lax.ppermute(v, axis, pairs)  29.9 us
    ppermute x17, starting transfers between devices, shifted(): return lax.ppermute(v, axis, pairs)  24.2 us
    pallas_call x18, Pallas kernels, call(): pl.pallas_call(body, out_shape=shapes, in_specs=[pl.BlockSpec(memory_spac...  21.4 us
    all_to_all x2, waiting for transfers between devices, over(): return lax.all_to_all(v, axes, 0, 0, tiled=True)  20 us
    all_to_all x2, starting transfers between devices, over(): return lax.all_to_all(v, axes, 0, 0, tiled=True)  19.7 us
    unnamed x44, local copies, waits for them, and re-layouts  4.1 us
  transfers between devices with their start and end apart: 19, of which 12 were waited for; matrix products, arithmetic and copies ran while one was open for 0% of the time, Pallas kernels for 8%

profile of v6, /device:TPU:1, one launch (start us, length us, event | category | flops | bytes accessed | tf_op | source)
XLA Modules:
  0.0 154.6 jit_solution(9545295023617176589)
XLA Ops:
  0.6 3.2 %shard_map.173 = (bf16[128,2048]{1,0:T(8,128)(2,1)}, f32[128,256]{1,0:T(8,128)S(1)}, f32[128,256]{1,0:T(8,128)S(1)}, f32[128,256]{1,0:T(8,128)S(1)}, f32[32,1024]{1,0:T(8,128)S(1)}, /*index=5*/f32[16,2048]{1,0:T(8,128)S(1)}) custom-call(s32[1]{0:T(128)} %bitcast.at, bf16[128,2048]{1,0:T(8,128)(2,1)} %bitcast.11, bf16[128,2048]{1,0:T(8,128)(2,1)} %bitcast.12, ...), custom_call_target="tpu_custom_call" | custom-call | tf_op jit(solution)/shard_map/pallas_call | solution.py:116
  3.9 2.2 %collective-permute-start = (f32[128,256]{1,0:T(8,128)S(1)}, f32[128,256]{1,0:T(8,128)S(1)}, u32[]{:S(2)}, u32[]{:S(2)}) collective-permute-start(f32[128,256]{1,0:T(8,128)S(1)} %get-tuple-element.57), channel_id=1, source_target_pairs={{0,1},{1,2},{2,3},{3,0},{4,5},{5,6},{6,7},{7,4},{8,9},{9,10},{10,1... | collective-permute-start | bytes 393224 | tf_op jit(solution)/shard_map/ppermute | solution.py:502
  6.1 2.6 %collective-permute-start.1 = (f32[128,256]{1,0:T(8,128)S(1)}, f32[128,256]{1,0:T(8,128)S(1)}, u32[]{:S(2)}, u32[]{:S(2)}) collective-permute-start(f32[128,256]{1,0:T(8,128)S(1)} %get-tuple-element.58), channel_id=1, source_target_pairs={{0,2},{1,3},{2,0},{3,1},{4,6},{5,7},{6,4},{7,5},{8,10},{9,11},{10,... | collective-permute-start | bytes 393224 | tf_op jit(solution)/shard_map/ppermute | solution.py:502
  8.7 1.1 collective-permute-start.2
  9.7 1.0 copy-done.3
  10.8 0.6 shard_map.174
  11.4 3.0 %collective-permute-done.1.c = f32[128,256]{1,0:T(8,128)S(1)} collective-permute-done((f32[128,256]{1,0:T(8,128)S(1)}, f32[128,256]{1,0:T(8,128)S(1)}, u32[]{:S(2)}, u32[]{:S(2)}) %collective-permute-start.1) | collective-permute-done | bytes 131104 | tf_op jit(solution)/shard_map/ppermute | solution.py:502
  14.4 1.1 shard_map.175
  15.5 13.1 %all-to-all-start = ((f32[64,4,256]{2,1,0:T(4,128)}), f32[64,4,256]{2,1,0:T(4,128)S(1)}, u32[]{:S(2)}, u32[]{:S(2)}) async-start(f32[64,4,256]{2,1,0:T(4,128)} %shard_map.175), calls=%async_computation | async-start | bytes 524288 | tf_op jit(solution)/shard_map/all_to_all | solution.py:523
  28.7 2.4 %shard_map.176 = (f32[128,2048]{1,0:T(8,128)}, f32[128,2048]{1,0:T(8,128)}, f32[64,64]{1,0:T(8,128)S(1)}, f32[128,512]{1,0:T(8,128)S(1)}, f32[128,512]{1,0:T(8,1...) custom-call(s32[1]{0:T(128)} %bitcast.at, bf16[128,2048]{1,0:T(8,128)(2,1)S(1)} %bitcast.10, ...), custom_call_target="tpu_custom_call" | custom-call | tf_op jit(solution)/shard_map/pallas_call | solution.py:116
  31.1 0.7 copy-done.8
  31.8 0.7 copy-done.16
  32.5 0.7 copy-done.18
  33.2 0.7 copy-done.20
  33.9 6.7 %all-to-all-done.got = f32[64,4,256]{2,1,0:T(4,128)S(1)} async-done(((f32[64,4,256]{2,1,0:T(4,128)}), f32[64,4,256]{2,1,0:T(4,128)S(1)}, u32[]{:S(2)}, u32[]{:S(2)}) %all-to-all-start) | async-done | bytes 262176 | tf_op jit(solution)/shard_map/all_to_all | solution.py:523
  40.6 0.4 shard_map.177
  41.1 17.9 %all_to_all.20.got = f32[64,4,256]{2,1,0:T(4,128)S(1)} all-to-all(f32[64,4,256]{2,1,0:T(4,128)S(1)} %get-tuple-element.72), channel_id=1, replica_groups=mesh['gz'=16,'gy'=4,'gx'=4] {'gz','gy'}, dimensions={0} | all-to-all | bytes 524288 | tf_op jit(solution)/shard_map/all_to_all | solution.py:523
  59.3 1.9 %collective-permute-start.3 = (f32[128,256]{1,0:T(8,128)S(1)}, f32[128,256]{1,0:T(8,128)S(1)}, u32[]{:S(2)}, u32[]{:S(2)}) collective-permute-start(f32[128,256]{1,0:T(8,128)S(1)} %shard_map.178.a), channel_id=1, source_target_pairs={{0,3},{1,0},{2,1},{3,2},{4,7},{5,4},{6,5},{7,6},{8,11},{9,8},{10,9... | collective-permute-start | bytes 393224 | tf_op jit(solution)/shard_map/ppermute | solution.py:502
  61.3 0.9 collective-permute-start.10
  62.1 1.1 collective-permute-start.11
  63.3 1.1 collective-permute-start.4
  64.3 0.8 collective-permute-start.5
  65.1 0.8 collective-permute-start.9
  65.9 6.8 %collective-permute-done.4.c = f32[128,256]{1,0:T(8,128)S(1)} collective-permute-done((f32[128,256]{1,0:T(8,128)S(1)}, f32[128,256]{1,0:T(8,128)S(1)}, u32[]{:S(2)}, u32[]{:S(2)}) %collective-permute-start.4) | collective-permute-done | bytes 131104 | tf_op jit(solution)/shard_map/ppermute | solution.py:502
  72.8 3.9 %collective-permute-done.5.d = f32[128,256]{1,0:T(8,128)S(1)} collective-permute-done((f32[128,256]{1,0:T(8,128)S(1)}, f32[128,256]{1,0:T(8,128)S(1)}, u32[]{:S(2)}, u32[]{:S(2)}) %collective-permute-start.5) | collective-permute-done | bytes 131104 | tf_op jit(solution)/shard_map/ppermute | solution.py:502
  76.6 4.5 %shard_map.179 = (bf16[128,2048]{1,0:T(8,128)(2,1)}, f32[128,256]{1,0:T(8,128)S(1)}, f32[128,256]{1,0:T(8,128)S(1)}, f32[128,256]{1,0:T(8,128)S(1)}) custom-call(s32[1]{0:T(128)} %bitcast.at, f32[128,2048]{1,0:T(8,128)} %get-tuple-element.63.local_from, f32[128,2048]{1,0:T(8,128)} %get-tuple-element.64.slope_from, f32[128,256]{1,0:T(8,128)S(1)} %shard_map.178.a, ...), custom_call_target="tpu_custom_call" | custom-call | tf_op jit(solution)/shard_map/pallas_call | solution.py:116
  81.2 3.2 %collective-permute-start.6 = (f32[128,256]{1,0:T(8,128)S(1)}, f32[128,256]{1,0:T(8,128)S(1)}, u32[]{:S(2)}, u32[]{:S(2)}) collective-permute-start(f32[128,256]{1,0:T(8,128)S(1)} %get-tuple-element.77), channel_id=1, source_target_pairs={{0,1},{1,2},{2,3},{3,0},{4,5},{5,6},{6,7},{7,4},{8,9},{9,10},{10,1... | collective-permute-start | bytes 393224 | tf_op jit(solution)/shard_map/ppermute | solution.py:502
  84.4 1.9 %collective-permute-start.7 = (f32[128,256]{1,0:T(8,128)S(1)}, f32[128,256]{1,0:T(8,128)S(1)}, u32[]{:S(2)}, u32[]{:S(2)}) collective-permute-start(f32[128,256]{1,0:T(8,128)S(1)} %get-tuple-element.78), channel_id=1, source_target_pairs={{0,2},{1,3},{2,0},{3,1},{4,6},{5,7},{6,4},{7,5},{8,10},{9,11},{10,... | collective-permute-start | bytes 393224 | tf_op jit(solution)/shard_map/ppermute | solution.py:502
  86.3 0.5 collective-permute-start.8
  87.4 0.7 shard_map.180
  88.1 2.9 %collective-permute-done.7.c = f32[128,256]{1,0:T(8,128)S(1)} collective-permute-done((f32[128,256]{1,0:T(8,128)S(1)}, f32[128,256]{1,0:T(8,128)S(1)}, u32[]{:S(2)}, u32[]{:S(2)}) %collective-permute-start.7) | collective-permute-done | bytes 131104 | tf_op jit(solution)/shard_map/ppermute | solution.py:502
  91.1 0.8 collective-permute-done.8.d
  92.1 1.8 %collective-permute-start.12 = (f32[64,1024]{1,0:T(8,128)S(1)}, f32[64,1024]{1,0:T(8,128)S(1)}, u32[]{:S(2)}, u32[]{:S(2)}) collective-permute-start(f32[64,1024]{1,0:T(8,128)S(1)} %get-tuple-element.88), channel_id=1, source_target_pairs={{0,4},{4,0},{8,12},{12,8},{1,5},{5,1},{9,13},{13,9},{2,6},{6,2},{1... | collective-permute-start | bytes 786440 | tf_op jit(solution)/shard_map/ppermute | solution.py:502
  93.9 1.2 collective-permute-done.12.got
  95.1 1.3 collective-permute-start.13
  96.4 3.4 %collective-permute-done.13.b = f32[32,1024]{1,0:T(8,128)S(1)} collective-permute-done((f32[32,1024]{1,0:T(8,128)S(1)}, f32[32,1024]{1,0:T(8,128)S(1)}, u32[]{:S(2)}, u32[]{:S(2)}) %collective-permute-start.13) | collective-permute-done | bytes 131104 | tf_op jit(solution)/shard_map/ppermute | solution.py:502
  100.1 16.2 %all_to_all.21.got = f32[16,4,896]{2,1,0:T(4,128)S(1)} all-to-all(f32[16,4,896]{2,1,0:T(4,128)S(1)} %shard_map.184), channel_id=1, replica_groups=mesh['gz'=16,'gy'=4,'gx'=4] {'gz'}, dimensions={0} | all-to-all | bytes 458752 | tf_op jit(solution)/shard_map/all_to_all | solution.py:523
  116.4 1.2 shard_map.185
  117.5 6.6 %all-to-all-start.3 = ((f32[64,4,384]{2,1,0:T(4,128)}), f32[64,4,384]{2,1,0:T(4,128)S(1)}, u32[]{:S(2)}, u32[]{:S(2)}) async-start(f32[64,4,384]{2,1,0:T(4,128)} %get-tuple-element.92), calls=%async_computation.3 | async-start | bytes 786432 | tf_op jit(solution)/shard_map/all_to_all | solution.py:523
  124.2 1.4 shard_map.186.local
  125.5 13.3 %all-to-all-done.3.got = f32[64,4,384]{2,1,0:T(4,128)S(1)} async-done(((f32[64,4,384]{2,1,0:T(4,128)}), f32[64,4,384]{2,1,0:T(4,128)S(1)}, u32[]{:S(2)}, u32[]{:S(2)}) %all-to-all-start.3) | async-done | bytes 393248 | tf_op jit(solution)/shard_map/all_to_all | solution.py:523
  139.2 2.0 %collective-permute-start.14 = (f32[160,256]{1,0:T(8,128)S(1)}, f32[160,256]{1,0:T(8,128)S(1)}, u32[]{:S(2)}, u32[]{:S(2)}) collective-permute-start(f32[160,256]{1,0:T(8,128)S(1)} %shard_map.187.a), channel_id=1, source_target_pairs={{0,3},{1,0},{2,1},{3,2},{4,7},{5,4},{6,5},{7,6},{8,11},{9,8},{10,9... | collective-permute-start | bytes 491528 | tf_op jit(solution)/shard_map/ppermute | solution.py:502
  141.1 0.9 collective-permute-start.15
  142.0 1.2 shard_map.190
  143.2 1.2 shard_map.189
  144.6 3.1 %collective-permute-done.15.c = f32[160,256]{1,0:T(8,128)S(1)} collective-permute-done((f32[160,256]{1,0:T(8,128)S(1)}, f32[160,256]{1,0:T(8,128)S(1)}, u32[]{:S(2)}, u32[]{:S(2)}) %collective-permute-start.15) | collective-permute-done | bytes 163872 | tf_op jit(solution)/shard_map/ppermute | solution.py:502
  147.7 4.5 %collective-permute-done.16.d = f32[160,256]{1,0:T(8,128)S(1)} collective-permute-done((f32[160,256]{1,0:T(8,128)S(1)}, f32[160,256]{1,0:T(8,128)S(1)}, u32[]{:S(2)}, u32[]{:S(2)}) %collective-permute-start.16) | collective-permute-done | bytes 163872 | tf_op jit(solution)/shard_map/ppermute | solution.py:502
  152.3 2.2 %shard_map.188 = (bf16[128,2048]{1,0:T(8,128)(2,1)}, f32[64,64]{1,0:T(8,128)}, f32[64,64]{1,0:T(8,128)}) custom-call(s32[1]{0:T(128)} %bitcast.at, f32[160,256]{1,0:T(8,128)S(1)} %shard_map.187.a, f32[160,256]{1,0:T(8,128)S(1)} %collective-permute-done.14.b, f32[160,256]{1,0:T(8,128)S(1)} %collective-permute-done.15.c, ...), custom_call_target="tpu_custom_call" | custom-call | tf_op jit(solution)/shard_map/pallas_call | solution.py:116
  (54 shorter events, 1.9 us)
Async XLA Ops:
  3.8 5.9 %copy-start.15 = (f32[16,128]{1,0:T(8,128)S(1)}, f32[16,128]{1,0:T(8,128)}, u32[]{:S(2)}) copy-start(f32[16,128]{1,0:T(8,128)} %constant.33.clone.few) | copy-start | bytes 24580
  3.9 7.6 %collective-permute-start = (f32[128,256]{1,0:T(8,128)S(1)}, f32[128,256]{1,0:T(8,128)S(1)}, u32[]{:S(2)}, u32[]{:S(2)}) collective-permute-start(f32[128,256]{1,0:T(8,128)S(1)} %get-tuple-element.57), channel_id=1, source_target_pairs={{0,1},{1,2},{2,3},{3,0},{4,5},{5,6},{6,7},{7,4},{8,9},{9,10},{10,1... | collective-permute-start | bytes 393224 | tf_op jit(solution)/shard_map/ppermute | solution.py:502
  6.1 8.3 %collective-permute-start.1 = (f32[128,256]{1,0:T(8,128)S(1)}, f32[128,256]{1,0:T(8,128)S(1)}, u32[]{:S(2)}, u32[]{:S(2)}) collective-permute-start(f32[128,256]{1,0:T(8,128)S(1)} %get-tuple-element.58), channel_id=1, source_target_pairs={{0,2},{1,3},{2,0},{3,1},{4,6},{5,7},{6,4},{7,5},{8,10},{9,11},{10,... | collective-permute-start | bytes 393224 | tf_op jit(solution)/shard_map/ppermute | solution.py:502
  8.7 5.7 %collective-permute-start.2 = (f32[128,256]{1,0:T(8,128)S(1)}, f32[128,256]{1,0:T(8,128)S(1)}, u32[]{:S(2)}, u32[]{:S(2)}) collective-permute-start(f32[128,256]{1,0:T(8,128)S(1)} %get-tuple-element.59), channel_id=1, source_target_pairs={{0,3},{1,0},{2,1},{3,2},{4,7},{5,4},{6,5},{7,6},{8,11},{9,8},{10,9... | collective-permute-start | bytes 393224 | tf_op jit(solution)/shard_map/ppermute | solution.py:502
  9.7 1.0 copy-start.3
  10.8 3.6 %copy-start.5 = (bf16[4,128,128]{2,1,0:T(8,128)(2,1)S(1)}, bf16[4,128,128]{2,1,0:T(8,128)(2,1)}, u32[]{:S(2)}) copy-start(bf16[4,128,128]{2,1,0:T(8,128)(2,1)} %constant.31.clone.flat) | copy-start | bytes 393220
  10.8 17.8 %copy-start.7 = (bf16[8,16,2048]{2,1,0:T(8,128)(2,1)S(1)}, bf16[8,16,2048]{2,1,0:T(8,128)(2,1)}, u32[]{:S(2)}) copy-start(bf16[8,16,2048]{2,1,0:T(8,128)(2,1)} %param.15) | copy-start | bytes 1572868
  14.4 14.2 %copy-start.1 = (bf16[8,16,2048]{2,1,0:T(8,128)(2,1)S(1)}, bf16[8,16,2048]{2,1,0:T(8,128)(2,1)}, u32[]{:S(2)}) copy-start(bf16[8,16,2048]{2,1,0:T(8,128)(2,1)} %param.14) | copy-start | bytes 1572868
  14.4 14.2 %copy-start.4 = (bf16[128,2048]{1,0:T(8,128)(2,1)S(1)}, bf16[128,2048]{1,0:T(8,128)(2,1)}, u32[]{:S(2)}) copy-start(bf16[128,2048]{1,0:T(8,128)(2,1)} %get-tuple-element.62.dz) | copy-start | bytes 1572868
  15.5 13.2 %copy-start.13 = (bf16[64,64]{1,0:T(8,128)(2,1)S(1)}, bf16[64,64]{1,0:T(8,128)(2,1)}, u32[]{:S(2)}) copy-start(bf16[64,64]{1,0:T(8,128)(2,1)} %point.2) | copy-start | bytes 24580
  15.5 25.1 %all-to-all-start = ((f32[64,4,256]{2,1,0:T(4,128)}), f32[64,4,256]{2,1,0:T(4,128)S(1)}, u32[]{:S(2)}, u32[]{:S(2)}) async-start(f32[64,4,256]{2,1,0:T(4,128)} %shard_map.175), calls=%async_computation | async-start | bytes 524288 | tf_op jit(solution)/shard_map/all_to_all | solution.py:523
  28.7 11.9 %copy-start.12 = (bf16[1,4,4,4096]{3,2,1,0:T(4,128)(2,1)S(1)}, bf16[1,4,4,4096]{3,2,1,0:T(4,128)(2,1)}, u32[]{:S(2)}) copy-start(bf16[1,4,4,4096]{3,2,1,0:T(4,128)(2,1)} %spectral.2) | copy-start | bytes 393220
  31.1 0.7 copy-start.8
  31.8 0.7 copy-start.16
  32.5 0.7 copy-start.18
  33.2 0.7 copy-start.20
  41.0 20.2 %copy-start.21 = (f32[128,512]{1,0:T(8,128)S(1)}, f32[128,512]{1,0:T(8,128)}, u32[]{:S(2)}) copy-start(f32[128,512]{1,0:T(8,128)} %copy-done.20) | copy-start | bytes 786436
  59.0 3.2 %copy-start.19 = (f32[128,512]{1,0:T(8,128)S(1)}, f32[128,512]{1,0:T(8,128)}, u32[]{:S(2)}) copy-start(f32[128,512]{1,0:T(8,128)} %copy-done.18) | copy-start | bytes 786436
  59.0 6.1 %copy-start.17 = (f32[128,512]{1,0:T(8,128)S(1)}, f32[128,512]{1,0:T(8,128)}, u32[]{:S(2)}) copy-start(f32[128,512]{1,0:T(8,128)} %copy-done.16) | copy-start | bytes 786436
  59.3 5.8 %collective-permute-start.3 = (f32[128,256]{1,0:T(8,128)S(1)}, f32[128,256]{1,0:T(8,128)S(1)}, u32[]{:S(2)}, u32[]{:S(2)}) collective-permute-start(f32[128,256]{1,0:T(8,128)S(1)} %shard_map.178.a), channel_id=1, source_target_pairs={{0,3},{1,0},{2,1},{3,2},{4,7},{5,4},{6,5},{7,6},{8,11},{9,8},{10,9... | collective-permute-start | bytes 393224 | tf_op jit(solution)/shard_map/ppermute | solution.py:502
  61.3 25.1 %collective-permute-start.10 = (f32[128,512]{1,0:T(8,128)S(1)}, f32[128,512]{1,0:T(8,128)S(1)}, u32[]{:S(2)}, u32[]{:S(2)}) collective-permute-start(f32[128,512]{1,0:T(8,128)S(1)} %copy-done.21), channel_id=1, source_target_pairs={{0,2},{1,3},{2,0},{3,1},{4,6},{5,7},{6,4},{7,5},{8,10},{9,11},{10,... | collective-permute-start | bytes 786440 | tf_op jit(solution)/shard_map/ppermute | solution.py:502
  62.1 24.7 %collective-permute-start.11 = (f32[128,512]{1,0:T(8,128)S(1)}, f32[128,512]{1,0:T(8,128)S(1)}, u32[]{:S(2)}, u32[]{:S(2)}) collective-permute-start(f32[128,512]{1,0:T(8,128)S(1)} %copy-done.19), channel_id=1, source_target_pairs={{0,3},{1,0},{2,1},{3,2},{4,7},{5,4},{6,5},{7,6},{8,11},{9,8},{10,9... | collective-permute-start | bytes 786440 | tf_op jit(solution)/shard_map/ppermute | solution.py:502
  63.3 9.5 %collective-permute-start.4 = (f32[128,256]{1,0:T(8,128)S(1)}, f32[128,256]{1,0:T(8,128)S(1)}, u32[]{:S(2)}, u32[]{:S(2)}) collective-permute-start(f32[128,256]{1,0:T(8,128)S(1)} %shard_map.178.a), channel_id=1, source_target_pairs={{0,2},{1,3},{2,0},{3,1},{4,6},{5,7},{6,4},{7,5},{8,10},{9,11},{10,... | collective-permute-start | bytes 393224 | tf_op jit(solution)/shard_map/ppermute | solution.py:502
  64.3 12.3 %collective-permute-start.5 = (f32[128,256]{1,0:T(8,128)S(1)}, f32[128,256]{1,0:T(8,128)S(1)}, u32[]{:S(2)}, u32[]{:S(2)}) collective-permute-start(f32[128,256]{1,0:T(8,128)S(1)} %shard_map.178.a), channel_id=1, source_target_pairs={{0,1},{1,2},{2,3},{3,0},{4,5},{5,6},{6,7},{7,4},{8,9},{9,10},{10,1... | collective-permute-start | bytes 393224 | tf_op jit(solution)/shard_map/ppermute | solution.py:502
  65.1 21.8 %collective-permute-start.9 = (f32[128,512]{1,0:T(8,128)S(1)}, f32[128,512]{1,0:T(8,128)S(1)}, u32[]{:S(2)}, u32[]{:S(2)}) collective-permute-start(f32[128,512]{1,0:T(8,128)S(1)} %copy-done.17), channel_id=1, source_target_pairs={{0,1},{1,2},{2,3},{3,0},{4,5},{5,6},{6,7},{7,4},{8,9},{9,10},{10,1... | collective-permute-start | bytes 786440 | tf_op jit(solution)/shard_map/ppermute | solution.py:502
  76.6 10.3 %copy-start.6 = (bf16[4,128,128]{2,1,0:T(8,128)(2,1)S(1)}, bf16[4,128,128]{2,1,0:T(8,128)(2,1)}, u32[]{:S(2)}) copy-start(bf16[4,128,128]{2,1,0:T(8,128)(2,1)} %constant.30.clone.ty) | copy-start | bytes 393220
  76.6 10.3 %copy-start.9 = (f32[128,512]{1,0:T(8,128)S(1)}, f32[128,512]{1,0:T(8,128)}, u32[]{:S(2)}) copy-start(f32[128,512]{1,0:T(8,128)} %copy-done.8) | copy-start | bytes 786436
  81.2 7.0 %collective-permute-start.6 = (f32[128,256]{1,0:T(8,128)S(1)}, f32[128,256]{1,0:T(8,128)S(1)}, u32[]{:S(2)}, u32[]{:S(2)}) collective-permute-start(f32[128,256]{1,0:T(8,128)S(1)} %get-tuple-element.77), channel_id=1, source_target_pairs={{0,1},{1,2},{2,3},{3,0},{4,5},{5,6},{6,7},{7,4},{8,9},{9,10},{10,1... | collective-permute-start | bytes 393224 | tf_op jit(solution)/shard_map/ppermute | solution.py:502
  84.4 6.7 %collective-permute-start.7 = (f32[128,256]{1,0:T(8,128)S(1)}, f32[128,256]{1,0:T(8,128)S(1)}, u32[]{:S(2)}, u32[]{:S(2)}) collective-permute-start(f32[128,256]{1,0:T(8,128)S(1)} %get-tuple-element.78), channel_id=1, source_target_pairs={{0,2},{1,3},{2,0},{3,1},{4,6},{5,7},{6,4},{7,5},{8,10},{9,11},{10,... | collective-permute-start | bytes 393224 | tf_op jit(solution)/shard_map/ppermute | solution.py:502
  86.3 1.0 copy-start.2
  86.3 5.5 %collective-permute-start.8 = (f32[128,256]{1,0:T(8,128)S(1)}, f32[128,256]{1,0:T(8,128)S(1)}, u32[]{:S(2)}, u32[]{:S(2)}) collective-permute-start(f32[128,256]{1,0:T(8,128)S(1)} %get-tuple-element.79), channel_id=1, source_target_pairs={{0,3},{1,0},{2,1},{3,2},{4,7},{5,4},{6,5},{7,6},{8,11},{9,8},{10,9... | collective-permute-start | bytes 393224 | tf_op jit(solution)/shard_map/ppermute | solution.py:502
  92.1 3.0 %collective-permute-start.12 = (f32[64,1024]{1,0:T(8,128)S(1)}, f32[64,1024]{1,0:T(8,128)S(1)}, u32[]{:S(2)}, u32[]{:S(2)}) collective-permute-start(f32[64,1024]{1,0:T(8,128)S(1)} %get-tuple-element.88), channel_id=1, source_target_pairs={{0,4},{4,0},{8,12},{12,8},{1,5},{5,1},{9,13},{13,9},{2,6},{6,2},{1... | collective-permute-start | bytes 786440 | tf_op jit(solution)/shard_map/ppermute | solution.py:502
  95.0 4.8 %copy-start.11 = (bf16[16,32,64]{2,1,0:T(8,128)(2,1)S(1)}, bf16[16,32,64]{2,1,0:T(8,128)(2,1)}, u32[]{:S(2)}) copy-start(bf16[16,32,64]{2,1,0:T(8,128)(2,1)} %constant.32.clone.tx) | copy-start | bytes 196612
  95.1 4.8 %collective-permute-start.13 = (f32[32,1024]{1,0:T(8,128)S(1)}, f32[32,1024]{1,0:T(8,128)S(1)}, u32[]{:S(2)}, u32[]{:S(2)}) collective-permute-start(f32[32,1024]{1,0:T(8,128)S(1)} %get-tuple-element.90), channel_id=1, source_target_pairs={{0,8},{4,12},{8,0},{12,4},{1,9},{5,13},{9,1},{13,5},{2,10},{6,14},... | collective-permute-start | bytes 393224 | tf_op jit(solution)/shard_map/ppermute | solution.py:502
  100.1 16.3 %copy-start.10 = (bf16[1,4,4,4096]{3,2,1,0:T(4,128)(2,1)S(1)}, bf16[1,4,4,4096]{3,2,1,0:T(4,128)(2,1)}, u32[]{:S(2)}) copy-start(bf16[1,4,4,4096]{3,2,1,0:T(4,128)(2,1)} %spectral.3) | copy-start | bytes 393220
  117.5 6.6 %copy-start.14 = (bf16[64,64]{1,0:T(8,128)(2,1)S(1)}, bf16[64,64]{1,0:T(8,128)(2,1)}, u32[]{:S(2)}) copy-start(bf16[64,64]{1,0:T(8,128)(2,1)} %point.3) | copy-start | bytes 24580
  117.5 21.3 %all-to-all-start.3 = ((f32[64,4,384]{2,1,0:T(4,128)}), f32[64,4,384]{2,1,0:T(4,128)S(1)}, u32[]{:S(2)}, u32[]{:S(2)}) async-start(f32[64,4,384]{2,1,0:T(4,128)} %get-tuple-element.92), calls=%async_computation.3 | async-start | bytes 786432 | tf_op jit(solution)/shard_map/all_to_all | solution.py:523
  139.2 5.4 %collective-permute-start.14 = (f32[160,256]{1,0:T(8,128)S(1)}, f32[160,256]{1,0:T(8,128)S(1)}, u32[]{:S(2)}, u32[]{:S(2)}) collective-permute-start(f32[160,256]{1,0:T(8,128)S(1)} %shard_map.187.a), channel_id=1, source_target_pairs={{0,3},{1,0},{2,1},{3,2},{4,7},{5,4},{6,5},{7,6},{8,11},{9,8},{10,9... | collective-permute-start | bytes 491528 | tf_op jit(solution)/shard_map/ppermute | solution.py:502
  141.1 6.6 %collective-permute-start.15 = (f32[160,256]{1,0:T(8,128)S(1)}, f32[160,256]{1,0:T(8,128)S(1)}, u32[]{:S(2)}, u32[]{:S(2)}) collective-permute-start(f32[160,256]{1,0:T(8,128)S(1)} %shard_map.187.a), channel_id=1, source_target_pairs={{0,2},{1,3},{2,0},{3,1},{4,6},{5,7},{6,4},{7,5},{8,10},{9,11},{10,... | collective-permute-start | bytes 491528 | tf_op jit(solution)/shard_map/ppermute | solution.py:502
  142.0 10.3 %collective-permute-start.16 = (f32[160,256]{1,0:T(8,128)S(1)}, f32[160,256]{1,0:T(8,128)S(1)}, u32[]{:S(2)}, u32[]{:S(2)}) collective-permute-start(f32[160,256]{1,0:T(8,128)S(1)} %shard_map.187.a), channel_id=1, source_target_pairs={{0,1},{1,2},{2,3},{3,0},{4,5},{5,6},{6,7},{7,4},{8,9},{9,10},{10,1... | collective-permute-start | bytes 491528 | tf_op jit(solution)/shard_map/ppermute | solution.py:502
  142.0 10.3 %copy-start = (f32[128,2048]{1,0:T(8,128)S(1)}, f32[128,2048]{1,0:T(8,128)}, u32[]{:S(2)}) copy-start(f32[128,2048]{1,0:T(8,128)} %shard_map.186.local) | copy-start | bytes 3145732
